TPU v7x, 32 devices: a whole 2x2x4 slice. The times are simulated.
32 devices in a mesh: groups: 2 (over y), gx: 4 (over z), gy: 2 (over x), gz: 2 (over core).
Axes of the slice: x: 2, y: 2, z: 4, core: 2. Of those that a mesh axis runs over, the one named last changes fastest.
Arguments:
- earlier_warmth_field: float32 [16, 512, 512], P(('groups', 'gz'), 'gy', 'gx'), parts along dimension 0, may hold values from -6 to 6
- caloric_storage: float32 [16, 512, 512], P(('groups', 'gz'), 'gy', 'gx'), parts along dimension 0, may hold values from 0.5 to 4
- thermal_diffusivity_coefficient: float32 [16, 512, 512], P(('groups', 'gz'), 'gy', 'gx'), parts along dimension 0, may hold values from 0.3 to 3
- dissipation_catalog: float32 [16, 64, 128], P('groups'), parts along dimension 0, may hold values from 0.1 to 3
- dissipation_selector: int32 [16, 8, 4], P(('groups', 'gz'), 'gy', 'gx'), parts along dimension 0, may hold values from 0 to 7
- refine_depth: int32 [16, 8, 4], P(('groups', 'gz'), 'gy', 'gx'), parts along dimension 0, may hold values from 1 to 4, as said below
- border_band_width: int32 [16, 4], P(('groups', 'gy'), 'gx'), parts along dimension 0, may hold values from 1 to 16
- microflow_flag: int32 [16], P(('groups', 'gz')), parts along dimension 0, may hold values 0 or 1
Outputs:
- warmth_solution: float32 [16, 512, 512], P(('groups', 'gz'), 'gy', 'gx'), parts along dimension 0
- leftover_misfit: float32 [16, 512, 512], P(('groups', 'gz'), 'gy', 'gx'), parts along dimension 0
There are 2 independent parts, one for each index of `groups`. A program takes and returns all parts, laid end to end along the dimension named above; each array names one. Nothing has to cross between parts.
Inputs may be any that keep to these rules, and one draw needn't show every extreme that they name: `refine_depth`: each tile's level is 1, 2 or 4.
All inputs are finite; a program needn't handle non-finite values. No bound on the sum of `microflow_flag` on one device may be relied on, other than what follows from the above.
Results may differ from a plain program's by a relative error of at most 0.00022.
Values sent between devices are 32-bit elements; how exact they have to be, the bound alone decides.
No kernel may reach another device: no remote copies, remote signals or barrier semaphores. Data moves between devices by JAX's collectives and lax.ppermute only.
A program may use at most 64 MiB of HBM per device.

v0:
```python
import jax
import jax.numpy as jnp
from jax import lax
from jax.sharding import PartitionSpec as P

TY = 64
ITERS = 2


interval_increment = 0.5
vertical_ratio = 2.0
coolant_film = 1.5
band_sink = 1.0
damping = 0.8


def with_halo(shard, sides, width):
    for axis, dim in sides:
        count, length = (lax.axis_size(axis), shard.shape[dim])
        up = [(i, (i + 1) % count) for i in range(count - 1)]
        down = [(j, i) for i, j in up]
        last = lax.slice_in_dim(shard, length - width, length, axis=dim)
        first = lax.slice_in_dim(shard, 0, width, axis=dim)
        before = lax.ppermute(last, axis, up)
        after = lax.ppermute(first, axis, down)
        shard = jnp.concatenate([before, shard, after], axis=dim)
    return shard


def harmonic(first, second):
    return 2.0 * first * second / (first + second)


def neighbours(padded):
    return (
        padded[:-2, 1:-1, 1:-1],
        padded[2:, 1:-1, 1:-1],
        padded[1:-1, :-2, 1:-1],
        padded[1:-1, 2:, 1:-1],
        padded[1:-1, 1:-1, :-2],
        padded[1:-1, 1:-1, 2:],
    )


def body(
    earlier_warmth_field,
    caloric_storage,
    thermal_diffusivity_coefficient,
    dissipation_catalog,
    dissipation_selector,
    refine_depth,
    border_band_width,
    microflow_flag,
):
    stacked_layers, vertical_count, horizontal_count = earlier_warmth_field.shape
    kappa_rim = with_halo(thermal_diffusivity_coefficient, (("gx", 2), ("gy", 1), ("gz", 0)), 1)
    faces = [harmonic(thermal_diffusivity_coefficient, other) for other in neighbours(kappa_rim)]
    faces[0] = vertical_ratio * faces[0]
    faces[1] = vertical_ratio * faces[1]
    edge_cells = jnp.repeat(border_band_width, TY, axis=0)
    row_tile = (jnp.arange(vertical_count, dtype=jnp.int32) % TY)[:, None]
    band = ((row_tile < edge_cells) | (row_tile >= TY - edge_cells)).astype(jnp.float32)
    sink = coolant_film * microflow_flag.astype(jnp.float32)[:, None, None] + band_sink * band[None]
    diagonal = caloric_storage / interval_increment + sink
    for face in faces:
        diagonal = diagonal + face
    column_patch = jnp.arange(horizontal_count, dtype=jnp.int32)
    tile_faces = (
        faces[2] * (row_tile != 0).astype(jnp.float32),
        faces[3] * (row_tile != TY - 1).astype(jnp.float32),
        faces[4] * (column_patch != 0).astype(jnp.float32),
        faces[5] * (column_patch != horizontal_count - 1).astype(jnp.float32),
    )
    level_cells = jnp.repeat(refine_depth, TY, axis=1)
    map_count = dissipation_catalog.shape[0]
    onehot = (dissipation_selector[:, :, 0, None] == jnp.arange(map_count, dtype=jnp.int32)).astype(
        jnp.float32
    )
    dissipation_density = jnp.einsum(
        "zjp,pyx->zjyx", onehot, dissipation_catalog, precision=lax.Precision.HIGHEST
    ).reshape(stacked_layers, vertical_count, horizontal_count)
    linear_source_term = (
        caloric_storage / interval_increment * earlier_warmth_field + dissipation_density
    )

    def linear_map_action(field):
        padded = with_halo(field, (("gx", 2), ("gy", 1), ("gz", 0)), 1)
        total = diagonal * field
        for face, other in zip(faces, neighbours(padded)):
            total = total - face * other
        return total

    def smooth(vector):
        state = damping * vector / diagonal
        for sweep in range(1, 4):
            padded = jnp.pad(state, ((0, 0), (1, 1), (1, 1)))
            inner = tile_faces[0] * padded[:, :-2, 1:-1] + tile_faces[1] * padded[:, 2:, 1:-1]
            inner = (
                inner + tile_faces[2] * padded[:, 1:-1, :-2] + tile_faces[3] * padded[:, 1:-1, 2:]
            )
            fresh = (1.0 - damping) * state + damping * (vector + inner) / diagonal
            state = jnp.where(level_cells > sweep, fresh, state)
        return state

    warmth_solution = earlier_warmth_field
    leftover_misfit = linear_source_term - linear_map_action(warmth_solution)
    smoothed = smooth(leftover_misfit)
    applied = linear_map_action(smoothed)
    for turn in range(ITERS):
        gamma_now, delta_now = lax.psum(
            (jnp.sum(leftover_misfit * smoothed), jnp.sum(applied * smoothed)), ("gx", "gy", "gz")
        )
        pre = smooth(applied)
        twice = linear_map_action(pre)
        if turn == 0:
            present_stride_amount = gamma_now / delta_now
            image_dir, smooth_dir, operator_times_direction, conjugate_update_heading = (
                twice,
                pre,
                applied,
                smoothed,
            )
        else:
            current_mixing_factor = gamma_now / gamma_prev
            present_stride_amount = gamma_now / (
                delta_now - current_mixing_factor * gamma_now / alpha_prev
            )
            image_dir = twice + current_mixing_factor * image_dir
            smooth_dir = pre + current_mixing_factor * smooth_dir
            operator_times_direction = applied + current_mixing_factor * operator_times_direction
            conjugate_update_heading = smoothed + current_mixing_factor * conjugate_update_heading
        warmth_solution = warmth_solution + present_stride_amount * conjugate_update_heading
        leftover_misfit = leftover_misfit - present_stride_amount * operator_times_direction
        if turn + 1 < ITERS:
            smoothed = smoothed - present_stride_amount * smooth_dir
            applied = linear_map_action(smoothed)
        gamma_prev, alpha_prev = (gamma_now, present_stride_amount)
    return (warmth_solution, leftover_misfit)


def solution(mesh):
    return jax.shard_map(
        body,
        mesh=mesh,
        in_specs=(
            P(("groups", "gz"), "gy", "gx"),
            P(("groups", "gz"), "gy", "gx"),
            P(("groups", "gz"), "gy", "gx"),
            P("groups", None, None),
            P(("groups", "gz"), "gy", "gx"),
            P(("groups", "gz"), "gy", "gx"),
            P(("groups", "gy"), "gx"),
            P(("groups", "gz")),
        ),
        out_specs=(P(("groups", "gz"), "gy", "gx"), P(("groups", "gz"), "gy", "gx")),
        check_vma=False,
    )
```

profile of v0, /device:TPU:0, one launch (start us, length us, event | category | flops | bytes accessed | tf_op | source)
XLA Modules:
  0.0 202.6 jit_solution(9930890958993695138)
XLA Ops:
  0.6 2.4 %fusion.120 = (f32[4,256,1]{2,1,0:T(8,128)}, f32[4,256,1]{2,1,0:T(8,128)}) fusion(f32[4,256,128]{2,1,0:T(8,128)} %param.10), kind=kLoop, calls=%fused_computation.277 | loop fusion | bytes 16384 | tf_op jit(solution)/shard_map/slice | solution.py:22
  3.0 5.0 %collective-permute-start = (f32[4,256,1]{2,1,0:T(8,128)}, f32[4,256,1]{2,1,0:T(8,128)S(1)}, u32[]{:S(2)}, u32[]{:S(2)}) collective-permute-start(f32[4,256,1]{2,1,0:T(8,128)} %get-tuple-element.41), channel_id=1, source_target_pairs={{0,4},{4,8},{8,12},{1,5},{5,9},{9,13},{2,6},{6,10},{10,14},{3,7},{... | collective-permute-start | bytes 12296 | tf_op jit(solution)/shard_map/ppermute | solution.py:24
  8.1 1.4 collective-permute-start.1
  9.5 1.1 fusion.121
  10.6 4.7 %collective-permute-start.6 = (f32[4,256,1]{2,1,0:T(8,128)}, f32[4,256,1]{2,1,0:T(8,128)S(1)}, u32[]{:S(2)}, u32[]{:S(2)}) collective-permute-start(f32[4,256,1]{2,1,0:T(8,128)} %get-tuple-element.43), channel_id=1, source_target_pairs={{0,4},{4,8},{8,12},{1,5},{5,9},{9,13},{2,6},{6,10},{10,14},{3,7},{... | collective-permute-start | bytes 12296 | tf_op jit(solution)/shard_map/ppermute | solution.py:24
  15.3 1.3 collective-permute-start.7
  17.5 3.1 %collective-permute-done = f32[4,256,1]{2,1,0:T(8,128)S(1)} collective-permute-done((f32[4,256,1]{2,1,0:T(8,128)}, f32[4,256,1]{2,1,0:T(8,128)S(1)}, u32[]{:S(2)}, u32[]{:S(2)}) %collective-permute-start) | collective-permute-done | bytes 4128 | tf_op jit(solution)/shard_map/ppermute | solution.py:24
  20.6 4.5 %collective-permute-done.1 = f32[4,256,1]{2,1,0:T(8,128)S(1)} collective-permute-done((f32[4,256,1]{2,1,0:T(8,128)}, f32[4,256,1]{2,1,0:T(8,128)S(1)}, u32[]{:S(2)}, u32[]{:S(2)}) %collective-permute-start.1) | collective-permute-done | bytes 4128 | tf_op jit(solution)/shard_map/ppermute | solution.py:25
  25.2 3.4 %collective-permute-start.2 = (f32[4,1,130]{2,1,0:T(1,128)S(1)}, f32[4,1,130]{2,1,0:T(1,128)S(1)}, u32[]{:S(2)}, u32[]{:S(2)}) collective-permute-start(f32[4,1,130]{2,1,0:T(1,128)S(1)} %get-tuple-element.33), channel_id=1, source_target_pairs={{0,2},{1,3},{4,6},{5,7},{8,10},{9,11},{12,14},{13,15},{16,18},{17,... | collective-permute-start | bytes 6248 | tf_op jit(solution)/shard_map/ppermute | solution.py:24
  28.6 1.3 collective-permute-start.3
  30.7 4.2 %collective-permute-done.7 = f32[4,256,1]{2,1,0:T(8,128)S(1)} collective-permute-done((f32[4,256,1]{2,1,0:T(8,128)}, f32[4,256,1]{2,1,0:T(8,128)S(1)}, u32[]{:S(2)}, u32[]{:S(2)}) %collective-permute-start.7) | collective-permute-done | bytes 4128 | tf_op jit(solution)/shard_map/ppermute | solution.py:25
  35.0 3.4 %collective-permute-start.8 = (f32[4,1,130]{2,1,0:T(1,128)S(1)}, f32[4,1,130]{2,1,0:T(1,128)S(1)}, u32[]{:S(2)}, u32[]{:S(2)}) collective-permute-start(f32[4,1,130]{2,1,0:T(1,128)S(1)} %get-tuple-element.35), channel_id=1, source_target_pairs={{0,2},{1,3},{4,6},{5,7},{8,10},{9,11},{12,14},{13,15},{16,18},{17,... | collective-permute-start | bytes 6248 | tf_op jit(solution)/shard_map/ppermute | solution.py:24
  38.4 1.3 collective-permute-start.9
  39.8 1.1 pad_maximum_fusion.87
  40.9 1.3 collective-permute-start.4
  42.2 1.3 collective-permute-start.5
  44.2 2.6 %collective-permute-start.10 = (f32[1,258,130]{2,1,0:T(8,128)S(1)}, f32[1,258,130]{2,1,0:T(8,128)S(1)}, u32[]{:S(2)}, u32[]{:S(2)}) collective-permute-start(f32[1,258,130]{2,1,0:T(8,128)S(1)} %get-tuple-element.27), channel_id=1, source_target_pairs={{0,1},{2,3},{4,5},{6,7},{8,9},{10,11},{12,13},{14,15},{16,17},{18,... | collective-permute-start | bytes 402488 | tf_op jit(solution)/shard_map/ppermute | solution.py:24
  46.9 1.3 collective-permute-start.11
  48.2 0.9 copy.12
  51.0 7.1 %multiply_divide_fusion.1 = (f32[4,256,128]{2,1,0:T(8,128)S(1)}, f32[4,256,128]{2,1,0:T(8,128)S(1)}, f32[4,256,128]{2,1,0:T(8,128)S(1)}, f32[4,256,128]{2,1,0:T(...) fusion(f32[4,256,1]{2,1,0:T(8,128)} %copy-done.16, ...), kind=kLoop, calls=%fused_computation.215 | loop fusion | flops 10878976 | bytes 7381184 | tf_op jit(solution)/shard_map/div | solution.py:94
  60.0 3.5 %collective-permute-start.12 = (f32[4,256,1]{2,1,0:T(8,128)S(1)}, f32[4,256,1]{2,1,0:T(8,128)S(1)}, u32[]{:S(2)}, u32[]{:S(2)}) collective-permute-start(f32[4,256,1]{2,1,0:T(8,128)S(1)} %get-tuple-element.39), channel_id=1, source_target_pairs={{0,4},{4,8},{8,12},{1,5},{5,9},{9,13},{2,6},{6,10},{10,14},{3,7},{... | collective-permute-start | bytes 12296 | tf_op jit(solution)/shard_map/ppermute | solution.py:24
  63.5 1.3 collective-permute-start.13
  64.8 10.1 %collective-permute-done.12 = f32[4,256,1]{2,1,0:T(8,128)S(1)} collective-permute-done((f32[4,256,1]{2,1,0:T(8,128)S(1)}, f32[4,256,1]{2,1,0:T(8,128)S(1)}, u32[]{:S(2)}, u32[]{:S(2)}) %collective-permute-start.12) | collective-permute-done | bytes 4128 | tf_op jit(solution)/shard_map/ppermute | solution.py:24
  74.9 4.7 %collective-permute-done.13 = f32[4,256,1]{2,1,0:T(8,128)S(1)} collective-permute-done((f32[4,256,1]{2,1,0:T(8,128)S(1)}, f32[4,256,1]{2,1,0:T(8,128)S(1)}, u32[]{:S(2)}, u32[]{:S(2)}) %collective-permute-start.13) | collective-permute-done | bytes 4128 | tf_op jit(solution)/shard_map/ppermute | solution.py:25
  79.7 4.5 %collective-permute-start.14 = (f32[4,1,130]{2,1,0:T(1,128)S(1)}, f32[4,1,130]{2,1,0:T(1,128)S(1)}, u32[]{:S(2)}, u32[]{:S(2)}) collective-permute-start(f32[4,1,130]{2,1,0:T(1,128)S(1)} %get-tuple-element.31), channel_id=1, source_target_pairs={{0,2},{1,3},{4,6},{5,7},{8,10},{9,11},{12,14},{13,15},{16,18},{17,... | collective-permute-start | bytes 6248 | tf_op jit(solution)/shard_map/ppermute | solution.py:24
  84.3 1.3 collective-permute-start.15
  85.6 4.2 %collective-permute-done.15 = f32[4,1,130]{2,1,0:T(1,128)S(1)} collective-permute-done((f32[4,1,130]{2,1,0:T(1,128)S(1)}, f32[4,1,130]{2,1,0:T(1,128)S(1)}, u32[]{:S(2)}, u32[]{:S(2)}) %collective-permute-start.15) | collective-permute-done | bytes 2112 | tf_op jit(solution)/shard_map/ppermute | solution.py:25
  90.1 1.3 collective-permute-start.16
  91.4 1.3 collective-permute-start.17
  92.7 2.1 %collective-permute-done.17 = f32[1,258,130]{2,1,0:T(8,128)S(1)} collective-permute-done((f32[1,258,130]{2,1,0:T(8,128)S(1)}, f32[1,258,130]{2,1,0:T(8,128)S(1)}, u32[]{:S(2)}, u32[]{:S(2)}) %collective-permute-start.17) | collective-permute-done | bytes 134192 | tf_op jit(solution)/shard_map/ppermute | solution.py:25
  94.8 1.7 multiply_reduce_fusion.2
  97.4 1.4 fusion.56
  98.7 30.3 %all-reduce.7 = (f32[]{:T(128)}, f32[]{:T(128)}) all-reduce(f32[]{:T(128)} %get-tuple-element.5, f32[]{:T(128)} %get-tuple-element.4), channel_id=1, replica_groups=mesh['groups'=2,'gx'=4,'gy'=2,'gz'=2] {'gx','gy','gz'}, use_global_device_ids=true, to_apply=%region_1.2 | all-reduce | flops 2 | bytes 16 | tf_op jit(solution)/shard_map/psum | solution.py:110
  130.3 2.9 %multiply_subtract_fusion.1 = f32[4,256,128]{2,1,0:T(8,128)S(1)} fusion(f32[4,256,128]{2,1,0:T(8,128)S(1)} %fusion.32, f32[4,256,128]{2,1,0:T(8,128)} %fusion.56, f32[4,256,128]{2,1,0:T(8,128)S(1)} %get-tuple-element.14, f32[4,256,128]{2,1,0:T(8,128)} %copy-done.3, f32[4,256,128]{2,1,0:T(8,128)S(1)} %get-tuple-element.20, ...), kind=kLoop, calls=%fused_computation.210 | loop fusion | flops 2490368 | bytes 4722692 | tf_op jit(solution)/shard_map/sub | solution.py:135
  133.4 1.3 collective-permute-start.18
  134.7 1.3 collective-permute-start.19
  136.0 10.0 %collective-permute-done.18 = f32[4,256,1]{2,1,0:T(8,128)S(1)} collective-permute-done((f32[4,256,1]{2,1,0:T(8,128)S(1)}, f32[4,256,1]{2,1,0:T(8,128)S(1)}, u32[]{:S(2)}, u32[]{:S(2)}) %collective-permute-start.18) | collective-permute-done | bytes 4128 | tf_op jit(solution)/shard_map/ppermute | solution.py:24
  146.0 4.1 %collective-permute-done.19 = f32[4,256,1]{2,1,0:T(8,128)S(1)} collective-permute-done((f32[4,256,1]{2,1,0:T(8,128)S(1)}, f32[4,256,1]{2,1,0:T(8,128)S(1)}, u32[]{:S(2)}, u32[]{:S(2)}) %collective-permute-start.19) | collective-permute-done | bytes 4128 | tf_op jit(solution)/shard_map/ppermute | solution.py:25
  150.3 1.3 collective-permute-start.20
  151.6 1.4 collective-permute-start.21
  153.0 4.2 %collective-permute-done.21 = f32[4,1,130]{2,1,0:T(1,128)S(1)} collective-permute-done((f32[4,1,130]{2,1,0:T(1,128)S(1)}, f32[4,1,130]{2,1,0:T(1,128)S(1)}, u32[]{:S(2)}, u32[]{:S(2)}) %collective-permute-start.21) | collective-permute-done | bytes 2112 | tf_op jit(solution)/shard_map/ppermute | solution.py:25
  157.5 1.3 collective-permute-start.22
  158.8 1.3 collective-permute-start.23
  160.1 2.1 %collective-permute-done.23 = f32[1,258,130]{2,1,0:T(8,128)S(1)} collective-permute-done((f32[1,258,130]{2,1,0:T(8,128)S(1)}, f32[1,258,130]{2,1,0:T(8,128)S(1)}, u32[]{:S(2)}, u32[]{:S(2)}) %collective-permute-start.23) | collective-permute-done | bytes 134192 | tf_op jit(solution)/shard_map/ppermute | solution.py:25
  162.3 2.5 %multiply_reduce_fusion = (f32[]{:T(128)}, f32[]{:T(128)}, f32[4,256,128]{2,1,0:T(8,128)}) fusion(f32[4,256,128]{2,1,0:T(8,128)S(1)} %multiply_subtract_fusion.1, f32[4,256,128]{2,1,0:T(8,128)S(1)} %copy-done.1, f32[4,256,128]{2,1,0:T(8,128)S(1)} %copy-done.4, f32[]{:T(128)S(6)} %div.69, f32[4,256,128]{2,1,0:T(8,128)S(1)} %get-tuple-element.20, ...), kind=kLoop, calls=%fused_computation.208 | loop fusion | flops 4849662 | bytes 6047852 | tf_op jit(solution)/shard_map/reduce_sum | solution.py:111
  164.8 30.2 %all-reduce.6 = (f32[]{:T(128)}, f32[]{:T(128)}) all-reduce(f32[]{:T(128)} %get-tuple-element.3, f32[]{:T(128)} %get-tuple-element.2), channel_id=1, replica_groups=mesh['groups'=2,'gx'=4,'gy'=2,'gz'=2] {'gx','gy','gz'}, use_global_device_ids=true, to_apply=%region_5.6 | all-reduce | flops 2 | bytes 16 | tf_op jit(solution)/shard_map/psum | solution.py:110
  199.4 2.2 %multiply_add_fusion = f32[4,256,128]{2,1,0:T(8,128)} fusion(f32[4,256,128]{2,1,0:T(8,128)} %copy-done.6, f32[4,256,128]{2,1,0:T(8,128)S(1)} %fusion.32, f32[4,256,128]{2,1,0:T(8,128)} %param.8, f32[]{:T(128)S(6)} %div.74, f32[]{:T(128)S(6)} %div.76, f32[]{:T(128)S(6)} %div.69), kind=kLoop, calls=%fused_computation.207 | loop fusion | flops 786432 | bytes 2097164 | tf_op jit(solution)/shard_map/add | solution.py:132
  201.7 0.9 multiply_subtract_fusion
  (94 shorter events, 8.2 us)
Async XLA Ops:
  0.6 8.9 %copy-start.7 = (f32[4,256,128]{2,1,0:T(8,128)S(1)}, f32[4,256,128]{2,1,0:T(8,128)}, u32[]{:S(2)}) copy-start(f32[4,256,128]{2,1,0:T(8,128)} %param.8) | copy-start | bytes 1572868
  3.0 17.6 %collective-permute-start = (f32[4,256,1]{2,1,0:T(8,128)}, f32[4,256,1]{2,1,0:T(8,128)S(1)}, u32[]{:S(2)}, u32[]{:S(2)}) collective-permute-start(f32[4,256,1]{2,1,0:T(8,128)} %get-tuple-element.41), channel_id=1, source_target_pairs={{0,4},{4,8},{8,12},{1,5},{5,9},{9,13},{2,6},{6,10},{10,14},{3,7},{... | collective-permute-start | bytes 12296 | tf_op jit(solution)/shard_map/ppermute | solution.py:24
  8.0 8.6 %copy-start.23 = (s32[4,1]{0,1:T(1,128)S(1)}, s32[4,1]{0,1:T(1,128)}, u32[]{:S(2)}) copy-start(s32[4,1]{0,1:T(1,128)} %param.14) | copy-start | bytes 52
  8.0 8.8 %copy-start.24 = (s32[4]{0:T(128)S(1)}, s32[4]{0:T(128)}, u32[]{:S(2)}) copy-start(s32[4]{0:T(128)} %param.15) | copy-start | bytes 52
  8.0 8.8 %copy-start.22 = (s32[4,4,1]{1,2,0:T(1,128)S(1)}, s32[4,4,1]{1,2,0:T(1,128)}, u32[]{:S(2)}) copy-start(s32[4,4,1]{1,2,0:T(1,128)} %param.13) | copy-start | bytes 196
  8.1 8.8 %copy-start.20 = (f32[8,64,128]{2,1,0:T(8,128)S(1)}, f32[8,64,128]{2,1,0:T(8,128)}, u32[]{:S(2)}) copy-start(f32[8,64,128]{2,1,0:T(8,128)} %param.11) | copy-start | bytes 786436
  8.1 8.8 %copy-start.21 = (s32[4,4,1]{1,2,0:T(1,128)S(1)}, s32[4,4,1]{1,2,0:T(1,128)}, u32[]{:S(2)}) copy-start(s32[4,4,1]{1,2,0:T(1,128)} %param.12) | copy-start | bytes 196
  8.1 17.0 %collective-permute-start.1 = (f32[4,256,1]{2,1,0:T(8,128)}, f32[4,256,1]{2,1,0:T(8,128)S(1)}, u32[]{:S(2)}, u32[]{:S(2)}) collective-permute-start(f32[4,256,1]{2,1,0:T(8,128)} %get-tuple-element.42), channel_id=1, source_target_pairs={{4,0},{8,4},{12,8},{5,1},{9,5},{13,9},{6,2},{10,6},{14,10},{7,3},{... | collective-permute-start | bytes 12296 | tf_op jit(solution)/shard_map/ppermute | solution.py:25
  10.6 14.5 %copy-start.8 = (f32[4,256,128]{2,1,0:T(8,128)S(1)}, f32[4,256,128]{2,1,0:T(8,128)}, u32[]{:S(2)}) copy-start(f32[4,256,128]{2,1,0:T(8,128)} %param.10) | copy-start | bytes 1572868
  10.6 20.1 %collective-permute-start.6 = (f32[4,256,1]{2,1,0:T(8,128)}, f32[4,256,1]{2,1,0:T(8,128)S(1)}, u32[]{:S(2)}, u32[]{:S(2)}) collective-permute-start(f32[4,256,1]{2,1,0:T(8,128)} %get-tuple-element.43), channel_id=1, source_target_pairs={{0,4},{4,8},{8,12},{1,5},{5,9},{9,13},{2,6},{6,10},{10,14},{3,7},{... | collective-permute-start | bytes 12296 | tf_op jit(solution)/shard_map/ppermute | solution.py:24
  15.3 19.6 %collective-permute-start.7 = (f32[4,256,1]{2,1,0:T(8,128)}, f32[4,256,1]{2,1,0:T(8,128)S(1)}, u32[]{:S(2)}, u32[]{:S(2)}) collective-permute-start(f32[4,256,1]{2,1,0:T(8,128)} %get-tuple-element.44), channel_id=1, source_target_pairs={{4,0},{8,4},{12,8},{5,1},{9,5},{13,9},{6,2},{10,6},{14,10},{7,3},{... | collective-permute-start | bytes 12296 | tf_op jit(solution)/shard_map/ppermute | solution.py:25
  20.6 19.2 %copy-start.13 = (f32[4,256,1]{2,1,0:T(8,128)}, f32[4,256,1]{2,1,0:T(8,128)S(1)}, u32[]{:S(2)}) copy-start(f32[4,256,1]{2,1,0:T(8,128)S(1)} %collective-permute-done) | copy-start | bytes 12292
  25.1 14.7 %copy-start.14 = (f32[4,256,1]{2,1,0:T(8,128)}, f32[4,256,1]{2,1,0:T(8,128)S(1)}, u32[]{:S(2)}) copy-start(f32[4,256,1]{2,1,0:T(8,128)S(1)} %collective-permute-done.1) | copy-start | bytes 12292
  25.2 14.5 %collective-permute-start.2 = (f32[4,1,130]{2,1,0:T(1,128)S(1)}, f32[4,1,130]{2,1,0:T(1,128)S(1)}, u32[]{:S(2)}, u32[]{:S(2)}) collective-permute-start(f32[4,1,130]{2,1,0:T(1,128)S(1)} %get-tuple-element.33), channel_id=1, source_target_pairs={{0,2},{1,3},{4,6},{5,7},{8,10},{9,11},{12,14},{13,15},{16,18},{17,... | collective-permute-start | bytes 6248 | tf_op jit(solution)/shard_map/ppermute | solution.py:24
  28.6 11.1 %collective-permute-start.3 = (f32[4,1,130]{2,1,0:T(1,128)S(1)}, f32[4,1,130]{2,1,0:T(1,128)S(1)}, u32[]{:S(2)}, u32[]{:S(2)}) collective-permute-start(f32[4,1,130]{2,1,0:T(1,128)S(1)} %get-tuple-element.34), channel_id=1, source_target_pairs={{2,0},{3,1},{6,4},{7,5},{10,8},{11,9},{14,12},{15,13},{18,16},{19,... | collective-permute-start | bytes 6248 | tf_op jit(solution)/shard_map/ppermute | solution.py:25
  30.7 13.2 %copy-start.15 = (f32[4,256,1]{2,1,0:T(8,128)}, f32[4,256,1]{2,1,0:T(8,128)S(1)}, u32[]{:S(2)}) copy-start(f32[4,256,1]{2,1,0:T(8,128)S(1)} %collective-permute-done.6) | copy-start | bytes 12292
  34.9 9.0 %copy-start.16 = (f32[4,256,1]{2,1,0:T(8,128)}, f32[4,256,1]{2,1,0:T(8,128)S(1)}, u32[]{:S(2)}) copy-start(f32[4,256,1]{2,1,0:T(8,128)S(1)} %collective-permute-done.7) | copy-start | bytes 12292
  35.0 8.4 %collective-permute-start.8 = (f32[4,1,130]{2,1,0:T(1,128)S(1)}, f32[4,1,130]{2,1,0:T(1,128)S(1)}, u32[]{:S(2)}, u32[]{:S(2)}) collective-permute-start(f32[4,1,130]{2,1,0:T(1,128)S(1)} %get-tuple-element.35), channel_id=1, source_target_pairs={{0,2},{1,3},{4,6},{5,7},{8,10},{9,11},{12,14},{13,15},{16,18},{17,... | collective-permute-start | bytes 6248 | tf_op jit(solution)/shard_map/ppermute | solution.py:24
  38.4 5.5 %collective-permute-start.9 = (f32[4,1,130]{2,1,0:T(1,128)S(1)}, f32[4,1,130]{2,1,0:T(1,128)S(1)}, u32[]{:S(2)}, u32[]{:S(2)}) collective-permute-start(f32[4,1,130]{2,1,0:T(1,128)S(1)} %get-tuple-element.36), channel_id=1, source_target_pairs={{2,0},{3,1},{6,4},{7,5},{10,8},{11,9},{14,12},{15,13},{18,16},{19,... | collective-permute-start | bytes 6248 | tf_op jit(solution)/shard_map/ppermute | solution.py:25
  40.9 8.7 %collective-permute-start.4 = (f32[1,258,130]{2,1,0:T(8,128)}, f32[1,258,130]{2,1,0:T(8,128)S(1)}, u32[]{:S(2)}, u32[]{:S(2)}) collective-permute-start(f32[1,258,130]{2,1,0:T(8,128)} %get-tuple-element.26), channel_id=1, source_target_pairs={{0,1},{2,3},{4,5},{6,7},{8,9},{10,11},{12,13},{14,15},{16,17},{18,... | collective-permute-start | bytes 402488 | tf_op jit(solution)/shard_map/ppermute | solution.py:24
  42.2 7.4 %collective-permute-start.5 = (f32[1,258,130]{2,1,0:T(8,128)}, f32[1,258,130]{2,1,0:T(8,128)S(1)}, u32[]{:S(2)}, u32[]{:S(2)}) collective-permute-start(f32[1,258,130]{2,1,0:T(8,128)} %get-tuple-element.25), channel_id=1, source_target_pairs={{1,0},{3,2},{5,4},{7,6},{9,8},{11,10},{13,12},{15,14},{17,16},{19,... | collective-permute-start | bytes 402488 | tf_op jit(solution)/shard_map/ppermute | solution.py:25
  44.2 5.3 %collective-permute-start.10 = (f32[1,258,130]{2,1,0:T(8,128)S(1)}, f32[1,258,130]{2,1,0:T(8,128)S(1)}, u32[]{:S(2)}, u32[]{:S(2)}) collective-permute-start(f32[1,258,130]{2,1,0:T(8,128)S(1)} %get-tuple-element.27), channel_id=1, source_target_pairs={{0,1},{2,3},{4,5},{6,7},{8,9},{10,11},{12,13},{14,15},{16,17},{18,... | collective-permute-start | bytes 402488 | tf_op jit(solution)/shard_map/ppermute | solution.py:24
  46.9 4.1 %collective-permute-start.11 = (f32[1,258,130]{2,1,0:T(8,128)S(1)}, f32[1,258,130]{2,1,0:T(8,128)}, u32[]{:S(2)}, u32[]{:S(2)}) collective-permute-start(f32[1,258,130]{2,1,0:T(8,128)S(1)} %get-tuple-element.28), channel_id=1, source_target_pairs={{1,0},{3,2},{5,4},{7,6},{9,8},{11,10},{13,12},{15,14},{17,16},{19,... | collective-permute-start | bytes 402488 | tf_op jit(solution)/shard_map/ppermute | solution.py:25
  49.5 0.7 copy-start.18
  58.0 36.8 %copy-start = (f32[4,256,128]{2,1,0:T(8,128)}, f32[4,256,128]{2,1,0:T(8,128)S(1)}, u32[]{:S(2)}) copy-start(f32[4,256,128]{2,1,0:T(8,128)S(1)} %get-tuple-element.13) | copy-start | bytes 1572868
  58.1 36.8 %copy-start.9 = (f32[4,256,128]{2,1,0:T(8,128)}, f32[4,256,128]{2,1,0:T(8,128)S(1)}, u32[]{:S(2)}) copy-start(f32[4,256,128]{2,1,0:T(8,128)S(1)} %get-tuple-element.15) | copy-start | bytes 1572868
  58.1 36.8 %copy-start.11 = (f32[4,256,128]{2,1,0:T(8,128)}, f32[4,256,128]{2,1,0:T(8,128)S(1)}, u32[]{:S(2)}) copy-start(f32[4,256,128]{2,1,0:T(8,128)S(1)} %get-tuple-element.16) | copy-start | bytes 1572868
  60.0 14.9 %collective-permute-start.12 = (f32[4,256,1]{2,1,0:T(8,128)S(1)}, f32[4,256,1]{2,1,0:T(8,128)S(1)}, u32[]{:S(2)}, u32[]{:S(2)}) collective-permute-start(f32[4,256,1]{2,1,0:T(8,128)S(1)} %get-tuple-element.39), channel_id=1, source_target_pairs={{0,4},{4,8},{8,12},{1,5},{5,9},{9,13},{2,6},{6,10},{10,14},{3,7},{... | collective-permute-start | bytes 12296 | tf_op jit(solution)/shard_map/ppermute | solution.py:24
  63.5 16.1 %collective-permute-start.13 = (f32[4,256,1]{2,1,0:T(8,128)S(1)}, f32[4,256,1]{2,1,0:T(8,128)S(1)}, u32[]{:S(2)}, u32[]{:S(2)}) collective-permute-start(f32[4,256,1]{2,1,0:T(8,128)S(1)} %get-tuple-element.40), channel_id=1, source_target_pairs={{4,0},{8,4},{12,8},{5,1},{9,5},{13,9},{6,2},{10,6},{14,10},{7,3},{... | collective-permute-start | bytes 12296 | tf_op jit(solution)/shard_map/ppermute | solution.py:25
  79.7 5.9 %collective-permute-start.14 = (f32[4,1,130]{2,1,0:T(1,128)S(1)}, f32[4,1,130]{2,1,0:T(1,128)S(1)}, u32[]{:S(2)}, u32[]{:S(2)}) collective-permute-start(f32[4,1,130]{2,1,0:T(1,128)S(1)} %get-tuple-element.31), channel_id=1, source_target_pairs={{0,2},{1,3},{4,6},{5,7},{8,10},{9,11},{12,14},{13,15},{16,18},{17,... | collective-permute-start | bytes 6248 | tf_op jit(solution)/shard_map/ppermute | solution.py:24
  84.3 5.5 %collective-permute-start.15 = (f32[4,1,130]{2,1,0:T(1,128)S(1)}, f32[4,1,130]{2,1,0:T(1,128)S(1)}, u32[]{:S(2)}, u32[]{:S(2)}) collective-permute-start(f32[4,1,130]{2,1,0:T(1,128)S(1)} %get-tuple-element.32), channel_id=1, source_target_pairs={{2,0},{3,1},{6,4},{7,5},{10,8},{11,9},{14,12},{15,13},{18,16},{19,... | collective-permute-start | bytes 6248 | tf_op jit(solution)/shard_map/ppermute | solution.py:25
  90.1 2.6 %collective-permute-start.16 = (f32[1,258,130]{2,1,0:T(8,128)S(1)}, f32[1,258,130]{2,1,0:T(8,128)S(1)}, u32[]{:S(2)}, u32[]{:S(2)}) collective-permute-start(f32[1,258,130]{2,1,0:T(8,128)S(1)} %get-tuple-element.23), channel_id=1, source_target_pairs={{0,1},{2,3},{4,5},{6,7},{8,9},{10,11},{12,13},{14,15},{16,17},{18,... | collective-permute-start | bytes 402488 | tf_op jit(solution)/shard_map/ppermute | solution.py:24
  91.4 3.4 %collective-permute-start.17 = (f32[1,258,130]{2,1,0:T(8,128)S(1)}, f32[1,258,130]{2,1,0:T(8,128)S(1)}, u32[]{:S(2)}, u32[]{:S(2)}) collective-permute-start(f32[1,258,130]{2,1,0:T(8,128)S(1)} %get-tuple-element.24), channel_id=1, source_target_pairs={{1,0},{3,2},{5,4},{7,6},{9,8},{11,10},{13,12},{15,14},{17,16},{19,... | collective-permute-start | bytes 402488 | tf_op jit(solution)/shard_map/ppermute | solution.py:25
  96.6 0.8 copy-start.3
  133.2 29.1 %copy-start.6 = (f32[4,256,128]{2,1,0:T(8,128)}, f32[4,256,128]{2,1,0:T(8,128)S(1)}, u32[]{:S(2)}) copy-start(f32[4,256,128]{2,1,0:T(8,128)S(1)} %multiply_subtract_fusion.1) | copy-start | bytes 1572868
  133.4 12.6 %collective-permute-start.18 = (f32[4,256,1]{2,1,0:T(8,128)S(1)}, f32[4,256,1]{2,1,0:T(8,128)S(1)}, u32[]{:S(2)}, u32[]{:S(2)}) collective-permute-start(f32[4,256,1]{2,1,0:T(8,128)S(1)} %get-tuple-element.37), channel_id=1, source_target_pairs={{0,4},{4,8},{8,12},{1,5},{5,9},{9,13},{2,6},{6,10},{10,14},{3,7},{... | collective-permute-start | bytes 12296 | tf_op jit(solution)/shard_map/ppermute | solution.py:24
  134.7 15.5 %collective-permute-start.19 = (f32[4,256,1]{2,1,0:T(8,128)S(1)}, f32[4,256,1]{2,1,0:T(8,128)S(1)}, u32[]{:S(2)}, u32[]{:S(2)}) collective-permute-start(f32[4,256,1]{2,1,0:T(8,128)S(1)} %get-tuple-element.38), channel_id=1, source_target_pairs={{4,0},{8,4},{12,8},{5,1},{9,5},{13,9},{6,2},{10,6},{14,10},{7,3},{... | collective-permute-start | bytes 12296 | tf_op jit(solution)/shard_map/ppermute | solution.py:25
  150.3 2.8 %collective-permute-start.20 = (f32[4,1,130]{2,1,0:T(1,128)S(1)}, f32[4,1,130]{2,1,0:T(1,128)S(1)}, u32[]{:S(2)}, u32[]{:S(2)}) collective-permute-start(f32[4,1,130]{2,1,0:T(1,128)S(1)} %get-tuple-element.29), channel_id=1, source_target_pairs={{0,2},{1,3},{4,6},{5,7},{8,10},{9,11},{12,14},{13,15},{16,18},{17,... | collective-permute-start | bytes 6248 | tf_op jit(solution)/shard_map/ppermute | solution.py:24
  151.6 10.7 %copy-start.1 = (f32[4,256,128]{2,1,0:T(8,128)S(1)}, f32[4,256,128]{2,1,0:T(8,128)}, u32[]{:S(2)}) copy-start(f32[4,256,128]{2,1,0:T(8,128)} %copy-done) | copy-start | bytes 1572868
  151.6 10.7 %copy-start.4 = (f32[4,256,128]{2,1,0:T(8,128)S(1)}, f32[4,256,128]{2,1,0:T(8,128)}, u32[]{:S(2)}) copy-start(f32[4,256,128]{2,1,0:T(8,128)} %copy-done.3) | copy-start | bytes 1572868
  151.6 10.7 %copy-start.10 = (f32[4,256,128]{2,1,0:T(8,128)S(1)}, f32[4,256,128]{2,1,0:T(8,128)}, u32[]{:S(2)}) copy-start(f32[4,256,128]{2,1,0:T(8,128)} %copy-done.9) | copy-start | bytes 1572868
  151.6 10.7 %copy-start.12 = (f32[4,256,128]{2,1,0:T(8,128)S(1)}, f32[4,256,128]{2,1,0:T(8,128)}, u32[]{:S(2)}) copy-start(f32[4,256,128]{2,1,0:T(8,128)} %copy-done.11) | copy-start | bytes 1572868
  151.6 5.6 %collective-permute-start.21 = (f32[4,1,130]{2,1,0:T(1,128)S(1)}, f32[4,1,130]{2,1,0:T(1,128)S(1)}, u32[]{:S(2)}, u32[]{:S(2)}) collective-permute-start(f32[4,1,130]{2,1,0:T(1,128)S(1)} %get-tuple-element.30), channel_id=1, source_target_pairs={{2,0},{3,1},{6,4},{7,5},{10,8},{11,9},{14,12},{15,13},{18,16},{19,... | collective-permute-start | bytes 6248 | tf_op jit(solution)/shard_map/ppermute | solution.py:25
  157.5 2.6 %collective-permute-start.22 = (f32[1,258,130]{2,1,0:T(8,128)S(1)}, f32[1,258,130]{2,1,0:T(8,128)S(1)}, u32[]{:S(2)}, u32[]{:S(2)}) collective-permute-start(f32[1,258,130]{2,1,0:T(8,128)S(1)} %get-tuple-element.21), channel_id=1, source_target_pairs={{0,1},{2,3},{4,5},{6,7},{8,9},{10,11},{12,13},{14,15},{16,17},{18,... | collective-permute-start | bytes 402488 | tf_op jit(solution)/shard_map/ppermute | solution.py:24
  158.8 3.4 %collective-permute-start.23 = (f32[1,258,130]{2,1,0:T(8,128)S(1)}, f32[1,258,130]{2,1,0:T(8,128)S(1)}, u32[]{:S(2)}, u32[]{:S(2)}) collective-permute-start(f32[1,258,130]{2,1,0:T(8,128)S(1)} %get-tuple-element.22), channel_id=1, source_target_pairs={{1,0},{3,2},{5,4},{7,6},{9,8},{11,10},{13,12},{15,14},{17,16},{19,... | collective-permute-start | bytes 402488 | tf_op jit(solution)/shard_map/ppermute | solution.py:25
  199.4 2.2 %copy-start.2 = (f32[4,256,128]{2,1,0:T(8,128)S(1)}, f32[4,256,128]{2,1,0:T(8,128)}, u32[]{:S(2)}) copy-start(f32[4,256,128]{2,1,0:T(8,128)} %copy-done) | copy-start | bytes 1572868
  199.4 2.2 %copy-start.5 = (f32[4,256,128]{2,1,0:T(8,128)S(1)}, f32[4,256,128]{2,1,0:T(8,128)}, u32[]{:S(2)}) copy-start(f32[4,256,128]{2,1,0:T(8,128)} %copy-done.3) | copy-start | bytes 1572868
  199.4 2.2 %copy-start.17 = (f32[4,256,128]{2,1,0:T(8,128)S(1)}, f32[4,256,128]{2,1,0:T(8,128)}, u32[]{:S(2)}) copy-start(f32[4,256,128]{2,1,0:T(8,128)} %get-tuple-element.10) | copy-start | bytes 1572868
  (1 other events, 0.7 us)
where the time goes:
time: 203 us
  blocking collectives  60.5 us (30%)
  waiting for transfers between devices  54.7 us (27%)
  starting transfers between devices  49.4 us (24%)
  other arithmetic  23.4 us (12%)
  local copies, waits for them, and re-layouts  7.08 us (3%)
  between operations  6.83 us (3%)
    psum x2, blocking collectives, body(): lax.psum((jnp.sum(leftover_misfit * smoothed), jnp.sum(applied * smoothed...  60.5 us
    ppermute x12, starting transfers between devices, with_halo(): before = lax.ppermute(last, axis, up)  33.6 us
    ppermute x12, waiting for transfers between devices, with_halo(): after = lax.ppermute(first, axis, down)  30.7 us
    ppermute x12, waiting for transfers between devices, with_halo(): before = lax.ppermute(last, axis, up)  24.1 us
    ppermute x12, starting transfers between devices, with_halo(): after = lax.ppermute(first, axis, down)  15.8 us
    div x2, other arithmetic, smooth(): state = damping * vector / diagonal  7.15 us
    reduce_sum x2, other arithmetic, body(): jnp.sum(applied * smoothed)  4.26 us
  transfers between devices with their start and end apart: 24, of which 13 were waited for; matrix products, arithmetic and copies ran while one was open for 2% of the time, Pallas kernels for 0%

commit v1 on v0

v1 whole, which is shorter than its diff:
```python
import functools
import math

import jax
import jax.numpy as jnp
from jax import lax
from jax.experimental import pallas as pl
from jax.experimental.pallas import tpu as pltpu
from jax.sharding import PartitionSpec as P

interval_increment = 0.5
vertical_ratio = 2.0
coolant_film = 1.5
band_sink = 1.0
damping = 0.8
GRID_AXES = ("gx", "gy", "gz")
VMEM = pl.BlockSpec(memory_space=pltpu.VMEM)
SMEM = pl.BlockSpec(memory_space=pltpu.SMEM)
F32 = jnp.float32


def harmonic(first, second):
    return 2.0 * first * second / (first + second)


def lanes(shape=(8, 128)):
    return lax.broadcasted_iota(jnp.int32, shape, len(shape) - 1)


def rows(shape):
    return lax.broadcasted_iota(jnp.int32, shape, 0)


def odd(axis):
    return lax.rem(lax.axis_index(axis), 2) == 1


def pack_columns(load, count):
    lane = lanes()
    firsts, lasts = [], []
    for start in range(0, count, 128):
        parts = [jnp.zeros((8, 128), F32), jnp.zeros((8, 128), F32)]
        for i in range(min(128, count - start)):
            turned = load(start + i)
            if i:
                turned = pltpu.roll(turned, i, 1)
            here = (lane == i) | (lane == (i + 127) % 128)
            parts[i % 2] = jnp.where(here, turned, parts[i % 2])
        even = lane % 2 == 0
        firsts.append(jnp.where(even, parts[0], parts[1]))
        lasts.append(pltpu.roll(jnp.where(even, parts[1], parts[0]), 1, 1))
    return jnp.concatenate(firsts, 0), jnp.concatenate(lasts, 0)


def stage_columns(pair_ref, slot, first, last):
    for g in range(first.shape[0] // 8):
        f = first[8 * g : 8 * g + 8]
        l = pltpu.roll(last[8 * g : 8 * g + 8], 127, 1)
        even = lanes() % 2 == 0
        pair_ref[slot, 0, g] = jnp.where(even, f, l)
        pair_ref[slot, 1, g] = jnp.where(even, l, f)


def spread_columns(pair_ref, slot, base, count):
    lane = lanes()
    edge = (lane == 0) | (lane == 127)
    out = []
    for j in range(count):
        i = base + j
        group = lax.div(i, 128)
        turned = pltpu.roll(pair_ref[slot, j % 2, group], lax.rem(128 * (group + 1) - i, 128), 1)
        out.append(jnp.where(edge, turned, 0.0))
    return jnp.concatenate(out, 0)


def both_sides(axis, halo_refs, index=()):
    if len(halo_refs) == 1:
        got = halo_refs[0][index] if index else halo_refs[0][...]
        return got, got
    a, b = (ref[index] if index else ref[...] for ref in halo_refs)
    flag = odd(axis)
    return jnp.where(flag, a, b), jnp.where(flag, b, a)


def present(axis):
    here = lax.axis_index(axis)
    low = jnp.where(here > 0, 1.0, 0.0).astype(F32)
    high = jnp.where(here < lax.axis_size(axis) - 1, 1.0, 0.0).astype(F32)
    return low, high


def fill_sends(field_ref, send_refs, slot, columns):
    z, y, _ = field_ref.shape
    sx, sy, sz = send_refs
    put = (slot,) if slot is not None else ()
    for axis, refs in zip(GRID_AXES, (sx, sy, sz)):
        flag = odd(axis)
        for n, ref in enumerate(refs):
            high_first = flag if n else ~flag
            if axis == "gx":
                ref[put + (slice(None), slice(None))] = jnp.where(high_first, columns[1], columns[0])
            elif axis == "gy":
                low = field_ref[:, 0, :]
                high = field_ref[:, y - 1, :]
                ref[put + (slice(None), slice(None))] = jnp.where(high_first, high, low)
            else:
                ref[put + (slice(None), slice(None))] = field_ref[jnp.where(high_first, z - 1, 0)]


def regroup(refs, counts):
    out, at = [], 0
    for c in counts:
        out.append(refs[at : at + c])
        at += c
    return out, refs[at:]


def vreg(ref, i):
    per = ref.shape[1] // 8
    return ref[i // per, 8 * (i % per) : 8 * (i % per) + 8, :]


def first_kernel(rounds, x_ref, k_ref, *refs):
    sends, (own_ref,) = regroup(refs, rounds)
    count = x_ref.shape[0] * x_ref.shape[1] // 8
    for slot, ref in enumerate((x_ref, k_ref)):
        columns = pack_columns(functools.partial(vreg, ref), count)
        own_ref[slot, 0] = columns[0]
        own_ref[slot, 1] = columns[1]
        fill_sends(ref, sends, slot, columns)


def sweep_tile(value, weight, north, south, east, level):
    tall = value.shape[0]
    row = rows(value.shape)
    north = jnp.where(row == 0, 0.0, north)
    south = jnp.where(row == tall - 1, 0.0, south)
    start = weight * value

    def once(_, state):
        inner = north * pltpu.roll(state, 1, 0) + south * pltpu.roll(state, tall - 1, 0)
        inner = inner + east * pltpu.roll(state, 127, 1) + pltpu.roll(east * state, 1, 1)
        return (1.0 - damping) * state + (start + weight * inner)

    return lax.fori_loop(1, jnp.minimum(level, 4), once, start)


def tile_loop(z_count, t_count, body, carry):
    def step(i, carry):
        return body(lax.div(i, t_count), lax.rem(i, t_count), carry)

    return lax.fori_loop(0, z_count * t_count, step, carry)


def second_kernel(rounds, tall, *refs):
    (x_ref, c_ref, k_ref, cat_ref, own_ref, sel_ref, lev_ref, band_ref, flow_ref), refs = refs[:9], refs[9:]
    (hx, hy, hz), refs = regroup(refs, rounds)
    (r_ref, u_ref, cz_ref, cn_ref, ce_ref, diag_ref, wt_ref, cx_ref), refs = refs[:8], refs[8:]
    sends, (kp, xp, pairs) = regroup(refs, rounds)
    z, y, _ = x_ref.shape
    tiles = y // tall
    per = tall // 8

    row8 = rows((8, 128))
    for slot, (src, dst) in enumerate(((x_ref, xp), (k_ref, kp))):
        dst[1 : z + 1, 8 : 8 + y, :] = src[...]
        ylo, yhi = both_sides("gy", hy, (slot,))
        zlo, zhi = both_sides("gz", hz, (slot,))
        if slot:
            has = present("gy")
            ylo, yhi = ylo * has[0], yhi * has[1]
            has = present("gz")
            zlo, zhi = zlo * has[0], zhi * has[1]
        dst[0, 8 : 8 + y, :] = zlo
        dst[z + 1, 8 : 8 + y, :] = zhi
        for i in range(z):
            dst[i + 1, 0:8, :] = jnp.broadcast_to(ylo[i : i + 1], (8, 128))
            dst[i + 1, 8 + y : 16 + y, :] = jnp.broadcast_to(yhi[i : i + 1], (8, 128))
    xlo, xhi = both_sides("gx", hx, (0,))
    klo, khi = both_sides("gx", hx, (1,))
    has = present("gx")
    west = harmonic(own_ref[1, 0], klo * has[0])
    east = harmonic(own_ref[1, 1], khi * has[1])
    cx_ref[0] = west
    cx_ref[1] = east
    stage_columns(pairs, 0, west, east)
    stage_columns(pairs, 1, west * (xlo - own_ref[0, 0]), east * (xhi - own_ref[0, 1]))

    lane = lanes((tall, 128))
    row = rows((tall, 128))

    def faces(i, t, carry):
        at = pl.multiple_of(t * tall, 8)
        here = kp[i + 1, pl.ds(at + 8, tall), :]
        cn_ref[i, pl.ds(at, tall), :] = harmonic(here, kp[i + 1, pl.ds(at + 7, tall), :])
        ce_ref[i, pl.ds(at, tall), :] = jnp.where(lane == 127, 0.0, harmonic(here, pltpu.roll(here, 127, 1)))
        cz_ref[i, pl.ds(at, tall), :] = vertical_ratio * harmonic(here, kp[i, pl.ds(at + 8, tall), :])

        @pl.when(i == z - 1)
        def _():
            cz_ref[z, pl.ds(at, tall), :] = vertical_ratio * harmonic(here, kp[z + 1, pl.ds(at + 8, tall), :])

        return carry

    tile_loop(z, tiles, faces, 0)
    for i in range(z):
        last = kp[i + 1, y + 7 : y + 8, :]
        face = harmonic(last, kp[i + 1, y + 8 : y + 9, :])
        cn_ref[i, y : y + 8, :] = jnp.where(row8 == 0, face, 0.0)

    def body(i, t, carry):
        at = pl.multiple_of(t * tall, 8)
        near = pl.ds(at, tall)
        x = xp[i + 1, pl.ds(at + 8, tall), :]
        width = band_ref[t, 0]
        band = jnp.where((row < width) | (row >= tall - width), band_sink, 0.0)
        sink = coolant_film * flow_ref[i].astype(F32) + band
        cn = cn_ref[i, near, :]
        cs = cn_ref[i, pl.ds(at + 1, tall), :]
        ce = ce_ref[i, near, :]
        cw = pltpu.roll(ce, 1, 1)
        cd = cz_ref[i, near, :]
        cu = cz_ref[i + 1, near, :]
        base = i * (y // 8) + t * per
        diag = c_ref[i, near, :] / interval_increment + sink
        diag = diag + cd + cu + cn + cs + ce + cw + spread_columns(pairs, 0, base, per)
        power = cat_ref[sel_ref[i, t, 0]]
        r = power - sink * x + spread_columns(pairs, 1, base, per)
        r = r + cn * (xp[i + 1, pl.ds(at + 7, tall), :] - x) + cs * (xp[i + 1, pl.ds(at + 9, tall), :] - x)
        r = r + ce * (pltpu.roll(x, 127, 1) - x) + cw * (pltpu.roll(x, 1, 1) - x)
        r = r + cd * (xp[i, pl.ds(at + 8, tall), :] - x) + cu * (xp[i + 2, pl.ds(at + 8, tall), :] - x)
        weight = damping / diag
        diag_ref[i, near, :] = diag
        wt_ref[i, near, :] = weight
        r_ref[i, near, :] = r
        u_ref[i, near, :] = sweep_tile(r, weight, cn, cs, ce, lev_ref[i, t, 0])
        return carry

    tile_loop(z, tiles, body, 0)
    fill_sends(u_ref, sends, None, pack_columns(functools.partial(vreg, u_ref), z * y // 8))


def pad_field(src, dst, pairs, cx_ref, halos):
    z, y, _ = src.shape
    hx, hy, hz = halos
    dst[1 : z + 1, 8 : 8 + y, :] = src[...]
    ylo, yhi = both_sides("gy", hy)
    zlo, zhi = both_sides("gz", hz)
    dst[0, 8 : 8 + y, :] = zlo
    dst[z + 1, 8 : 8 + y, :] = zhi
    for i in range(z):
        dst[i + 1, 0:8, :] = jnp.broadcast_to(ylo[i : i + 1], (8, 128))
        dst[i + 1, 8 + y : 16 + y, :] = jnp.broadcast_to(yhi[i : i + 1], (8, 128))
    xlo, xhi = both_sides("gx", hx)
    stage_columns(pairs, 0, cx_ref[0] * xlo, cx_ref[1] * xhi)


def apply_tile(i, t, tall, y, vp, pairs, cz_ref, cn_ref, ce_ref, diag_ref):
    at = pl.multiple_of(t * tall, 8)
    near = pl.ds(at, tall)
    v = vp[i + 1, pl.ds(at + 8, tall), :]
    cn = cn_ref[i, near, :]
    cs = cn_ref[i, pl.ds(at + 1, tall), :]
    ce = ce_ref[i, near, :]
    total = cn * vp[i + 1, pl.ds(at + 7, tall), :] + cs * vp[i + 1, pl.ds(at + 9, tall), :]
    total = total + ce * pltpu.roll(v, 127, 1) + pltpu.roll(ce * v, 1, 1)
    total = total + cz_ref[i, near, :] * vp[i, pl.ds(at + 8, tall), :]
    total = total + cz_ref[i + 1, near, :] * vp[i + 2, pl.ds(at + 8, tall), :]
    total = total + spread_columns(pairs, 0, i * (y // 8) + t * (tall // 8), tall // 8)
    return near, v, diag_ref[i, near, :] * v - total, cn, cs, ce


def fold(product):
    return jnp.sum(product.reshape(-1, 8, 128), axis=0)


def third_kernel(rounds, tall, *refs):
    (u_ref, r_ref, cz_ref, cn_ref, ce_ref, diag_ref, wt_ref, cx_ref, lev_ref), refs = refs[:9], refs[9:]
    halos, refs = regroup(refs, rounds)
    (w_ref, m_ref, sum_ref), refs = refs[:3], refs[3:]
    sends, (up, pairs) = regroup(refs, rounds)
    z, y, _ = u_ref.shape
    pad_field(u_ref, up, pairs, cx_ref, halos)

    def body(i, t, carry):
        near, u, w, cn, cs, ce = apply_tile(i, t, tall, y, up, pairs, cz_ref, cn_ref, ce_ref, diag_ref)
        m = sweep_tile(w, wt_ref[i, near, :], cn, cs, ce, lev_ref[i, t, 0])
        w_ref[i, near, :] = w
        m_ref[i, near, :] = m
        gamma, delta, cross = carry
        return gamma + fold(r_ref[i, near, :] * u), delta + fold(w * u), cross + fold(w * m)

    zero = jnp.zeros((8, 128), F32)
    sums = tile_loop(z, y // tall, body, (zero, zero, zero))
    for n, value in enumerate(sums):
        sum_ref[n] = value
    fill_sends(m_ref, sends, None, pack_columns(functools.partial(vreg, m_ref), z * y // 8))


def fourth_kernel(rounds, tall, *refs):
    (m_ref, sum_ref, cz_ref, cn_ref, ce_ref, diag_ref, cx_ref), refs = refs[:7], refs[7:]
    halos, refs = regroup(refs, rounds)
    n_ref, out_ref, mp, pairs = refs
    z, y, _ = m_ref.shape
    pad_field(m_ref, mp, pairs, cx_ref, halos)

    def body(i, t, carry):
        near, m, n, _, _, _ = apply_tile(i, t, tall, y, mp, pairs, cz_ref, cn_ref, ce_ref, diag_ref)
        n_ref[i, near, :] = n
        return carry + fold(n * m)

    last = tile_loop(z, y // tall, body, jnp.zeros((8, 128), F32))
    parts = [sum_ref[0], sum_ref[1], sum_ref[2], last]
    parts = jnp.concatenate([jnp.sum(p, axis=0, keepdims=True) for p in parts], 0)
    for d in range(out_ref.shape[0]):
        out_ref[d] = parts


def last_kernel(all_ref, x_ref, r_ref, u_ref, w_ref, m_ref, n_ref, xo_ref, ro_ref):
    sums = jnp.sum(all_ref[...], axis=0)
    gamma, delta, cross, last = (sums[i : i + 1] for i in range(4))

    def total(v):
        return jnp.sum(v, axis=1, keepdims=True)

    gamma0 = total(gamma)
    alpha0 = gamma0 / total(delta)
    gamma1 = total(gamma - 2.0 * alpha0 * delta + alpha0 * alpha0 * cross)
    delta1 = total(delta - 2.0 * alpha0 * cross + alpha0 * alpha0 * last)
    beta = gamma1 / gamma0
    alpha1 = gamma1 / (delta1 - beta * gamma1 / alpha0)
    near = alpha0 + alpha1 * (1.0 + beta)
    far = alpha1 * alpha0
    for i in range(x_ref.shape[0]):
        xo_ref[i] = x_ref[i] + near * u_ref[i] - far * m_ref[i]
        ro_ref[i] = r_ref[i] - near * w_ref[i] + far * n_ref[i]


def swap_pairs(axis, start):
    count = lax.axis_size(axis)
    pairs = []
    for i in range(start, count - 1, 2):
        pairs += [(i, i + 1), (i + 1, i)]
    return pairs


def body(
    earlier_warmth_field,
    caloric_storage,
    thermal_diffusivity_coefficient,
    dissipation_catalog,
    dissipation_selector,
    refine_depth,
    border_band_width,
    microflow_flag,
):
    z, y, x = earlier_warmth_field.shape
    tall = dissipation_catalog.shape[1]
    groups = -(-(z * y // 8) // 128)
    rounds = tuple(2 if lax.axis_size(axis) > 2 else 1 for axis in GRID_AXES)
    shape = lambda *s: jax.ShapeDtypeStruct(s, F32)
    full = shape(z, y, x)

    def call(kernel, outs, ins, name, scratch=()):
        specs = [SMEM if v.dtype == jnp.int32 else VMEM for v in ins]
        return pl.pallas_call(
            kernel, out_shape=outs, in_specs=specs, out_specs=[VMEM] * len(outs), scratch_shapes=list(scratch), name=name
        )(*ins)

    def face_shapes(front):
        out = []
        for axis, n in zip(((8 * groups, x), (z, x), (y, x)), rounds):
            out += [shape(*front, *axis)] * n
        return out

    def swap(faces):
        faces, got = list(faces), []
        for axis, n in zip(GRID_AXES, rounds):
            for start in range(n):
                got.append(lax.ppermute(faces.pop(0), axis, swap_pairs(axis, start)))
        return got

    sends = sum(rounds)
    pairs = pltpu.VMEM((2, 2, groups, 8, 128), F32)
    padded = pltpu.VMEM((z + 2, y + 16, x), F32)
    levels = refine_depth

    outs = call(
        functools.partial(first_kernel, rounds),
        face_shapes((2,)) + [shape(2, 2, 8 * groups, x)],
        [earlier_warmth_field, thermal_diffusivity_coefficient],
        "faces",
    )
    own, halos = outs[sends], swap(outs[:sends])
    outs = call(
        functools.partial(second_kernel, rounds, tall),
        [full, full, shape(z + 1, y, x), shape(z, y + 8, x), full, full, full, shape(2, 8 * groups, x)] + face_shapes(()),
        [
            earlier_warmth_field,
            caloric_storage,
            thermal_diffusivity_coefficient,
            dissipation_catalog,
            own,
            dissipation_selector,
            levels,
            border_band_width,
            microflow_flag,
        ]
        + halos,
        "residual",
        [padded, padded, pairs],
    )
    r, u, cz, cn, ce, diag, weight, cx = outs[:8]
    halos = swap(outs[8:])
    outs = call(
        functools.partial(third_kernel, rounds, tall),
        [full, full, shape(3, 8, 128)] + face_shapes(()),
        [u, r, cz, cn, ce, diag, weight, cx, levels] + halos,
        "applied",
        [padded, pairs],
    )
    w, m, sums = outs[:3]
    halos = swap(outs[3:])
    members = math.prod(lax.axis_size(axis) for axis in GRID_AXES)
    n, parts = call(
        functools.partial(fourth_kernel, rounds, tall),
        [full, shape(members, 4, 128)],
        [m, sums, cz, cn, ce, diag, cx] + halos,
        "twice",
        [padded, pairs],
    )
    every = lax.all_to_all(parts, GRID_AXES, 0, 0, tiled=True)
    return tuple(
        call(last_kernel, [full, full], [every, earlier_warmth_field, r, u, w, m, n], "update")
    )


def solution(mesh):
    cells = P(("groups", "gz"), "gy", "gx")
    return jax.shard_map(
        body,
        mesh=mesh,
        in_specs=(
            cells,
            cells,
            cells,
            P("groups", None, None),
            cells,
            cells,
            P(("groups", "gy"), "gx"),
            P(("groups", "gz")),
        ),
        out_specs=(cells, cells),
        check_vma=False,
    )
```

time: 203 us -> 64.7 us (0.32)
  waiting for transfers between devices: 54.7 us -> 3.73 us
  blocking collectives: 60.5 us -> 13.1 us
  starting transfers between devices: 49.4 us -> 17 us
  Pallas kernels: 0 us -> 25.2 us
  other arithmetic: 23.4 us -> 0 us
  between operations: 6.83 us -> 0.83 us
  local copies, waits for them, and re-layouts: 7.08 us -> 4.09 us
    psum x2 -> x0, blocking collectives: 60.5 us -> none  [body(): lax.psum((jnp.sum(leftover_misfit * smoothed), jnp.sum(applied * smoothed...]
    ppermute x24 -> x12, waiting for transfers between devices: 54.7 us -> 3.73 us  [swap(): got.append(lax.ppermute(faces.pop(0), axis, swap_pairs(axis, start)))]
    ppermute x24 -> x12, starting transfers between devices: 49.4 us -> 17 us  [swap(): got.append(lax.ppermute(faces.pop(0), axis, swap_pairs(axis, start)))]
    pallas_call x0 -> x5, Pallas kernels: none -> 25.2 us  [call(): pl.pallas_call(kernel, out_shape=outs, in_specs=specs, out_specs=[VMEM] *...]
    all_to_all x0 -> x1, blocking collectives: none -> 13.1 us  [body(): every = lax.all_to_all(parts, GRID_AXES, 0, 0, tiled=True)]
    div x2 -> x0, other arithmetic: 7.15 us -> none  [smooth(): state = damping * vector / diagonal]
    reduce_sum x2 -> x0, other arithmetic: 4.26 us -> none  [body(): jnp.sum(applied * smoothed)]
    slice x4 -> x0, local copies, waits for them, and re-layouts: 3.9 us -> none  [with_halo(): last = lax.slice_in_dim(shard, length - width, length, axis=dim)]
  transfers between devices with their start and end apart: 24 -> 12, of which waited for: 13 -> 3; matrix products, arithmetic and copies ran while one was open for 2% -> 3% of each run, Pallas kernels for 0% -> 0%
where the time goes in v1:
time: 64.7 us; the launch traced here: 63.8 us
  Pallas kernels  25.2 us (39%)
  starting transfers between devices  17 us (26%)
  blocking collectives  13.1 us (20%)
  local copies, waits for them, and re-layouts  4.09 us (6%)
  waiting for transfers between devices  3.73 us (6%)
  between operations  0.83 us (1%)
    pallas_call x5, Pallas kernels, call(): pl.pallas_call(kernel, out_shape=outs, in_specs=specs, out_specs=[VMEM] *...  25.2 us
    ppermute x12, starting transfers between devices, swap(): got.append(lax.ppermute(faces.pop(0), axis, swap_pairs(axis, start)))  17 us
    all_to_all x1, blocking collectives, body(): every = lax.all_to_all(parts, GRID_AXES, 0, 0, tiled=True)  13.1 us
    unnamed x43, local copies, waits for them, and re-layouts  4.09 us
    ppermute x12, waiting for transfers between devices, swap(): got.append(lax.ppermute(faces.pop(0), axis, swap_pairs(axis, start)))  3.73 us
  transfers between devices with their start and end apart: 12, of which 3 were waited for; matrix products, arithmetic and copies ran while one was open for 3% of the time, Pallas kernels for 0%

profile of v1, /device:TPU:0, one launch (start us, length us, event | category | flops | bytes accessed | tf_op | source)
XLA Modules:
  0.0 63.8 jit_solution(10502486154563505277)
XLA Ops:
  0.6 2.4 %faces.1 = (f32[2,8,128]{2,1,0:T(8,128)}, f32[2,8,128]{2,1,0:T(8,128)}, f32[2,4,128]{2,1,0:T(4,128)}, f32[2,256,128]{2,1,0:T(8,128)}, f32[2,2,8,128]{3,2,1,0:T(8,128)}) custom-call(f32[4,256,128]{2,1,0:T(8,128)} %x_ref.3, f32[4,256,128]{2,1,0:T(8,128)} %refs_2_.1), custom_call_target="tpu_custom_call" | custom-call | tf_op jit(solution)/shard_map/faces/pallas_call | solution.py:366
  3.0 0.5 collective-permute-start.3
  3.5 2.6 %collective-permute-start = (f32[2,8,128]{2,1,0:T(8,128)}, f32[2,8,128]{2,1,0:T(8,128)S(1)}, u32[]{:S(2)}, u32[]{:S(2)}) collective-permute-start(f32[2,8,128]{2,1,0:T(8,128)} %get-tuple-element.29), channel_id=1, source_target_pairs={{0,4},{4,0},{8,12},{12,8},{1,5},{5,1},{9,13},{13,9},{2,6},{6,2},{1... | collective-permute-start | bytes 24584 | tf_op jit(solution)/shard_map/ppermute | solution.py:380
  6.1 0.8 %collective-permute-start.1 = (f32[2,8,128]{2,1,0:T(8,128)}, f32[2,8,128]{2,1,0:T(8,128)S(1)}, u32[]{:S(2)}, u32[]{:S(2)}) collective-permute-start(f32[2,8,128]{2,1,0:T(8,128)} %get-tuple-element.30), channel_id=1, source_target_pairs={{4,8},{8,4},{5,9},{9,5},{6,10},{10,6},{7,11},{11,7},{20,24},{24,20... | collective-permute-start | bytes 24584 | tf_op jit(solution)/shard_map/ppermute | solution.py:380
  6.9 0.0 copy-done.17
  6.9 1.6 %collective-permute-start.2 = (f32[2,4,128]{2,1,0:T(4,128)S(1)}, f32[2,4,128]{2,1,0:T(4,128)S(1)}, u32[]{:S(2)}, u32[]{:S(2)}) collective-permute-start(f32[2,4,128]{2,1,0:T(4,128)S(1)} %copy-done.17), channel_id=1, source_target_pairs={{0,2},{2,0},{1,3},{3,1},{4,6},{6,4},{5,7},{7,5},{8,10},{10,8},{9,1... | collective-permute-start | bytes 12296 | tf_op jit(solution)/shard_map/ppermute | solution.py:380
  8.5 0.0 copy-done.14
  8.5 0.7 %copy.12.refs_7_ = s32[4,1]{1,0:T(4,128)} copy(s32[4,1]{0,1:T(1,128)S(1)} %copy-done.14) | data formatting | bytes 32 | tf_op args[6]
  9.2 0.7 %copy.11.refs_6_.refs_8_ = s32[4,4,1]{2,1,0:T(4,128)} copy(s32[4,4,1]{1,2,0:T(1,128)S(1)} %copy-done.12) | data formatting | bytes 128 | tf_op args[5]
  9.9 0.7 %copy.10.refs_5_ = s32[4,4,1]{2,1,0:T(4,128)} copy(s32[4,4,1]{1,2,0:T(1,128)S(1)} %copy-done.13) | data formatting | bytes 128 | tf_op args[4]
  10.6 0.1 collective-permute-done.2.refs_11_
  10.6 0.0 collective-permute-done.refs_9_
  10.6 0.0 collective-permute-done.1.refs_10_
  10.6 0.0 collective-permute-done.3.refs_12_
  10.6 0.5 copy-done.5
  11.2 0.0 copy-done.3
  11.2 0.1 copy-done
  11.3 8.5 %residual.1 = (f32[4,256,128]{2,1,0:T(8,128)}, f32[4,256,128]{2,1,0:T(8,128)}, f32[5,256,128]{2,1,0:T(8,128)}, f32[4,264,128]{2,1,0:T(8,128)}, f32[4,256,128]{2,...) custom-call(f32[4,256,128]{2,1,0:T(8,128)} %x_ref.3, ...), custom_call_target="tpu_custom_call" | custom-call | tf_op jit(solution)/shard_map/residual/pallas_call | solution.py:366
  19.8 0.1 collective-permute-start.7
  19.9 4.4 %collective-permute-start.4 = (f32[8,128]{1,0:T(8,128)}, f32[8,128]{1,0:T(8,128)S(1)}, u32[]{:S(2)}, u32[]{:S(2)}) collective-permute-start(f32[8,128]{1,0:T(8,128)} %get-tuple-element.41), channel_id=1, source_target_pairs={{0,4},{4,0},{8,12},{12,8},{1,5},{5,1},{9,13},{13,9},{2,6},{6,2},{1... | collective-permute-start | bytes 12296 | tf_op jit(solution)/shard_map/ppermute | solution.py:380
  24.3 0.7 %collective-permute-start.5 = (f32[8,128]{1,0:T(8,128)S(1)}, f32[8,128]{1,0:T(8,128)S(1)}, u32[]{:S(2)}, u32[]{:S(2)}) collective-permute-start(f32[8,128]{1,0:T(8,128)S(1)} %copy-done.15), channel_id=1, source_target_pairs={{4,8},{8,4},{5,9},{9,5},{6,10},{10,6},{7,11},{11,7},{20,24},{24,20... | collective-permute-start | bytes 12296 | tf_op jit(solution)/shard_map/ppermute | solution.py:380
  25.0 1.7 %collective-permute-start.6 = (f32[4,128]{1,0:T(4,128)S(1)}, f32[4,128]{1,0:T(4,128)S(1)}, u32[]{:S(2)}, u32[]{:S(2)}) collective-permute-start(f32[4,128]{1,0:T(4,128)S(1)} %copy-done.18), channel_id=1, source_target_pairs={{0,2},{2,0},{1,3},{3,1},{4,6},{6,4},{5,7},{7,5},{8,10},{10,8},{9,1... | collective-permute-start | bytes 6152 | tf_op jit(solution)/shard_map/ppermute | solution.py:380
  26.7 1.9 %collective-permute-done.6.refs_11_ = f32[4,128]{1,0:T(4,128)S(1)} collective-permute-done((f32[4,128]{1,0:T(4,128)S(1)}, f32[4,128]{1,0:T(4,128)S(1)}, u32[]{:S(2)}, u32[]{:S(2)}) %collective-permute-start.6) | collective-permute-done | bytes 2080 | tf_op jit(solution)/shard_map/ppermute | solution.py:380
  28.6 0.0 collective-permute-done.4.refs_9_
  28.6 0.0 collective-permute-done.5.refs_10_
  28.7 0.0 collective-permute-done.7.refs_12_
  28.7 0.0 copy-start.1
  28.7 0.5 copy-done.6
  29.2 0.0 copy-done.8
  29.2 0.1 copy-done.1
  29.3 6.4 %applied.1 = (f32[4,256,128]{2,1,0:T(8,128)}, f32[4,256,128]{2,1,0:T(8,128)}, f32[3,8,128]{2,1,0:T(8,128)}, f32[8,128]{1,0:T(8,128)}, f32[8,128]{1,0:T(8,128)}, /*index=5*/f32[4,128]{1,0:T(4,128)}, f32[256,128]{1,0:T(8,128)}) custom-call(f32[4,256,128]{2,1,0:T(8,128)} %get-tuple-element.33.refs_0_.u_ref, f32[4,256,128]{2,1,0:T(8,128)} %get-tuple-element.34.refs_1_.r_ref, ...), custom_call_target="tpu_custom_call" | custom-call | tf_op jit(solution)/shard_map/applied/pallas_call | solution.py:366
  35.7 0.1 collective-permute-start.11
  35.8 2.0 %collective-permute-start.8 = (f32[8,128]{1,0:T(8,128)}, f32[8,128]{1,0:T(8,128)S(1)}, u32[]{:S(2)}, u32[]{:S(2)}) collective-permute-start(f32[8,128]{1,0:T(8,128)} %get-tuple-element.47), channel_id=1, source_target_pairs={{0,4},{4,0},{8,12},{12,8},{1,5},{5,1},{9,13},{13,9},{2,6},{6,2},{1... | collective-permute-start | bytes 12296 | tf_op jit(solution)/shard_map/ppermute | solution.py:380
  37.8 0.7 %collective-permute-start.9 = (f32[8,128]{1,0:T(8,128)S(1)}, f32[8,128]{1,0:T(8,128)S(1)}, u32[]{:S(2)}, u32[]{:S(2)}) collective-permute-start(f32[8,128]{1,0:T(8,128)S(1)} %copy-done.16), channel_id=1, source_target_pairs={{4,8},{8,4},{5,9},{9,5},{6,10},{10,6},{7,11},{11,7},{20,24},{24,20... | collective-permute-start | bytes 12296 | tf_op jit(solution)/shard_map/ppermute | solution.py:380
  38.5 0.0 copy-done.19
  38.5 1.9 %collective-permute-start.10 = (f32[4,128]{1,0:T(4,128)S(1)}, f32[4,128]{1,0:T(4,128)S(1)}, u32[]{:S(2)}, u32[]{:S(2)}) collective-permute-start(f32[4,128]{1,0:T(4,128)S(1)} %copy-done.19), channel_id=1, source_target_pairs={{0,2},{2,0},{1,3},{3,1},{4,6},{6,4},{5,7},{7,5},{8,10},{10,8},{9,1... | collective-permute-start | bytes 6152 | tf_op jit(solution)/shard_map/ppermute | solution.py:380
  40.4 1.7 %collective-permute-done.10.refs_9_ = f32[4,128]{1,0:T(4,128)S(1)} collective-permute-done((f32[4,128]{1,0:T(4,128)S(1)}, f32[4,128]{1,0:T(4,128)S(1)}, u32[]{:S(2)}, u32[]{:S(2)}) %collective-permute-start.10) | collective-permute-done | bytes 2080 | tf_op jit(solution)/shard_map/ppermute | solution.py:380
  42.2 0.0 collective-permute-done.8.refs_7_
  42.2 0.0 collective-permute-done.9.refs_8_
  42.2 0.0 copy-start.9
  42.2 0.0 collective-permute-done.11.refs_10_
  42.2 0.5 copy-done.11
  42.8 0.0 copy-done.7
  42.8 0.0 copy-done.9
  42.8 0.1 copy-done.2
  42.9 4.6 %twice.1 = (f32[4,256,128]{2,1,0:T(8,128)}, f32[16,4,128]{2,1,0:T(4,128)}) custom-call(f32[4,256,128]{2,1,0:T(8,128)} %get-tuple-element.45.refs_0_.m_ref, f32[3,8,128]{2,1,0:T(8,128)} %get-tuple-element.46.refs_1_, f32[5,256,128]{2,1,0:T(8,128)} %get-tuple-element.35.refs_2_, f32[4,264,128]{2,1,0:T(8,128)} %get-tuple-element.36.refs_3_, ...), custom_call_target="tpu_custom_call" | custom-call | tf_op jit(solution)/shard_map/twice/pallas_call | solution.py:366
  47.4 13.1 %all_to_all.5.all_ref = f32[16,4,128]{2,1,0:T(4,128)} all-to-all(f32[16,4,128]{2,1,0:T(4,128)} %get-tuple-element.51), channel_id=1, replica_groups=mesh['groups'=2,'gx'=4,'gy'=2,'gz'=2] {'gx','gy','gz'}, dimensions={0} | all-to-all | bytes 65536 | tf_op jit(solution)/shard_map/all_to_all | solution.py:432
  60.5 3.3 %update.1 = (f32[4,256,128]{2,1,0:T(8,128)}, f32[4,256,128]{2,1,0:T(8,128)}) custom-call(f32[16,4,128]{2,1,0:T(4,128)} %all_to_all.5.all_ref, f32[4,256,128]{2,1,0:T(8,128)} %x_ref.3, f32[4,256,128]{2,1,0:T(8,128)} %get-tuple-element.34.refs_1_.r_ref, f32[4,256,128]{2,1,0:T(8,128)} %get-tuple-element.33.refs_0_.u_ref, ...), custom_call_target="tpu_custom_call" | custom-call | tf_op jit(solution)/shard_map/update/pallas_call | solution.py:366
  (25 shorter events, 0.0 us)
Async XLA Ops:
  3.0 3.9 %copy-start.17 = (f32[2,4,128]{2,1,0:T(4,128)S(1)}, f32[2,4,128]{2,1,0:T(4,128)}, u32[]{:S(2)}) copy-start(f32[2,4,128]{2,1,0:T(4,128)} %get-tuple-element.31) | copy-start | bytes 12292
  3.0 7.6 %collective-permute-start.3 = (f32[2,256,128]{2,1,0:T(8,128)}, f32[2,256,128]{2,1,0:T(8,128)S(1)}, u32[]{:S(2)}, u32[]{:S(2)}) collective-permute-start(f32[2,256,128]{2,1,0:T(8,128)} %get-tuple-element.32), channel_id=1, source_target_pairs={{0,1},{1,0},{2,3},{3,2},{4,5},{5,4},{6,7},{7,6},{8,9},{9,8},{10,11... | collective-permute-start | bytes 786440 | tf_op jit(solution)/shard_map/ppermute | solution.py:380
  3.5 7.1 %collective-permute-start = (f32[2,8,128]{2,1,0:T(8,128)}, f32[2,8,128]{2,1,0:T(8,128)S(1)}, u32[]{:S(2)}, u32[]{:S(2)}) collective-permute-start(f32[2,8,128]{2,1,0:T(8,128)} %get-tuple-element.29), channel_id=1, source_target_pairs={{0,4},{4,0},{8,12},{12,8},{1,5},{5,1},{9,13},{13,9},{2,6},{6,2},{1... | collective-permute-start | bytes 24584 | tf_op jit(solution)/shard_map/ppermute | solution.py:380
  6.1 2.4 %copy-start.14 = (s32[4,1]{0,1:T(1,128)S(1)}, s32[4,1]{0,1:T(1,128)}, u32[]{:S(2)}) copy-start(s32[4,1]{0,1:T(1,128)} %param.14) | copy-start | bytes 52
  6.1 3.0 %copy-start.12 = (s32[4,4,1]{1,2,0:T(1,128)S(1)}, s32[4,4,1]{1,2,0:T(1,128)}, u32[]{:S(2)}) copy-start(s32[4,4,1]{1,2,0:T(1,128)} %param.13) | copy-start | bytes 196
  6.1 4.5 %collective-permute-start.1 = (f32[2,8,128]{2,1,0:T(8,128)}, f32[2,8,128]{2,1,0:T(8,128)S(1)}, u32[]{:S(2)}, u32[]{:S(2)}) collective-permute-start(f32[2,8,128]{2,1,0:T(8,128)} %get-tuple-element.30), channel_id=1, source_target_pairs={{4,8},{8,4},{5,9},{9,5},{6,10},{10,6},{7,11},{11,7},{20,24},{24,20... | collective-permute-start | bytes 24584 | tf_op jit(solution)/shard_map/ppermute | solution.py:380
  6.9 3.7 %collective-permute-start.2 = (f32[2,4,128]{2,1,0:T(4,128)S(1)}, f32[2,4,128]{2,1,0:T(4,128)S(1)}, u32[]{:S(2)}, u32[]{:S(2)}) collective-permute-start(f32[2,4,128]{2,1,0:T(4,128)S(1)} %copy-done.17), channel_id=1, source_target_pairs={{0,2},{2,0},{1,3},{3,1},{4,6},{6,4},{5,7},{7,5},{8,10},{10,8},{9,1... | collective-permute-start | bytes 12296 | tf_op jit(solution)/shard_map/ppermute | solution.py:380
  9.2 0.7 %copy-start.13 = (s32[4,4,1]{1,2,0:T(1,128)S(1)}, s32[4,4,1]{1,2,0:T(1,128)}, u32[]{:S(2)}) copy-start(s32[4,4,1]{1,2,0:T(1,128)} %param.12) | copy-start | bytes 196
  10.6 0.6 copy-start.5
  10.6 0.6 copy-start.3
  10.6 0.6 copy-start.4
  10.6 0.7 %copy-start = (f32[2,256,128]{2,1,0:T(8,128)}, f32[2,256,128]{2,1,0:T(8,128)S(1)}, u32[]{:S(2)}) copy-start(f32[2,256,128]{2,1,0:T(8,128)S(1)} %collective-permute-done.3.refs_12_) | copy-start | bytes 786436
  19.8 4.5 %copy-start.15 = (f32[8,128]{1,0:T(8,128)S(1)}, f32[8,128]{1,0:T(8,128)}, u32[]{:S(2)}) copy-start(f32[8,128]{1,0:T(8,128)} %get-tuple-element.42) | copy-start | bytes 12292
  19.8 8.8 %collective-permute-start.7 = (f32[256,128]{1,0:T(8,128)}, f32[256,128]{1,0:T(8,128)S(1)}, u32[]{:S(2)}, u32[]{:S(2)}) collective-permute-start(f32[256,128]{1,0:T(8,128)} %get-tuple-element.44), channel_id=1, source_target_pairs={{0,1},{1,0},{2,3},{3,2},{4,5},{5,4},{6,7},{7,6},{8,9},{9,8},{10,11... | collective-permute-start | bytes 393224 | tf_op jit(solution)/shard_map/ppermute | solution.py:380
  19.9 5.1 %copy-start.18 = (f32[4,128]{1,0:T(4,128)S(1)}, f32[4,128]{1,0:T(4,128)}, u32[]{:S(2)}) copy-start(f32[4,128]{1,0:T(4,128)} %get-tuple-element.43) | copy-start | bytes 6148
  19.9 8.7 %collective-permute-start.4 = (f32[8,128]{1,0:T(8,128)}, f32[8,128]{1,0:T(8,128)S(1)}, u32[]{:S(2)}, u32[]{:S(2)}) collective-permute-start(f32[8,128]{1,0:T(8,128)} %get-tuple-element.41), channel_id=1, source_target_pairs={{0,4},{4,0},{8,12},{12,8},{1,5},{5,1},{9,13},{13,9},{2,6},{6,2},{1... | collective-permute-start | bytes 12296 | tf_op jit(solution)/shard_map/ppermute | solution.py:380
  24.3 4.3 %collective-permute-start.5 = (f32[8,128]{1,0:T(8,128)S(1)}, f32[8,128]{1,0:T(8,128)S(1)}, u32[]{:S(2)}, u32[]{:S(2)}) collective-permute-start(f32[8,128]{1,0:T(8,128)S(1)} %copy-done.15), channel_id=1, source_target_pairs={{4,8},{8,4},{5,9},{9,5},{6,10},{10,6},{7,11},{11,7},{20,24},{24,20... | collective-permute-start | bytes 12296 | tf_op jit(solution)/shard_map/ppermute | solution.py:380
  25.0 3.7 %collective-permute-start.6 = (f32[4,128]{1,0:T(4,128)S(1)}, f32[4,128]{1,0:T(4,128)S(1)}, u32[]{:S(2)}, u32[]{:S(2)}) collective-permute-start(f32[4,128]{1,0:T(4,128)S(1)} %copy-done.18), channel_id=1, source_target_pairs={{0,2},{2,0},{1,3},{3,1},{4,6},{6,4},{5,7},{7,5},{8,10},{10,8},{9,1... | collective-permute-start | bytes 6152 | tf_op jit(solution)/shard_map/ppermute | solution.py:380
  28.6 0.6 copy-start.10
  28.6 0.6 copy-start.6
  28.6 0.6 copy-start.8
  28.7 0.7 %copy-start.1 = (f32[256,128]{1,0:T(8,128)}, f32[256,128]{1,0:T(8,128)S(1)}, u32[]{:S(2)}) copy-start(f32[256,128]{1,0:T(8,128)S(1)} %collective-permute-done.7.refs_12_) | copy-start | bytes 393220
  35.7 2.1 %copy-start.16 = (f32[8,128]{1,0:T(8,128)S(1)}, f32[8,128]{1,0:T(8,128)}, u32[]{:S(2)}) copy-start(f32[8,128]{1,0:T(8,128)} %get-tuple-element.48) | copy-start | bytes 12292
  35.7 6.5 %collective-permute-start.11 = (f32[256,128]{1,0:T(8,128)}, f32[256,128]{1,0:T(8,128)S(1)}, u32[]{:S(2)}, u32[]{:S(2)}) collective-permute-start(f32[256,128]{1,0:T(8,128)} %get-tuple-element.50), channel_id=1, source_target_pairs={{0,1},{1,0},{2,3},{3,2},{4,5},{5,4},{6,7},{7,6},{8,9},{9,8},{10,11... | collective-permute-start | bytes 393224 | tf_op jit(solution)/shard_map/ppermute | solution.py:380
  35.8 2.7 %copy-start.19 = (f32[4,128]{1,0:T(4,128)S(1)}, f32[4,128]{1,0:T(4,128)}, u32[]{:S(2)}) copy-start(f32[4,128]{1,0:T(4,128)} %get-tuple-element.49) | copy-start | bytes 6148
  35.8 6.4 %collective-permute-start.8 = (f32[8,128]{1,0:T(8,128)}, f32[8,128]{1,0:T(8,128)S(1)}, u32[]{:S(2)}, u32[]{:S(2)}) collective-permute-start(f32[8,128]{1,0:T(8,128)} %get-tuple-element.47), channel_id=1, source_target_pairs={{0,4},{4,0},{8,12},{12,8},{1,5},{5,1},{9,13},{13,9},{2,6},{6,2},{1... | collective-permute-start | bytes 12296 | tf_op jit(solution)/shard_map/ppermute | solution.py:380
  37.8 4.3 %collective-permute-start.9 = (f32[8,128]{1,0:T(8,128)S(1)}, f32[8,128]{1,0:T(8,128)S(1)}, u32[]{:S(2)}, u32[]{:S(2)}) collective-permute-start(f32[8,128]{1,0:T(8,128)S(1)} %copy-done.16), channel_id=1, source_target_pairs={{4,8},{8,4},{5,9},{9,5},{6,10},{10,6},{7,11},{11,7},{20,24},{24,20... | collective-permute-start | bytes 12296 | tf_op jit(solution)/shard_map/ppermute | solution.py:380
  38.5 3.7 %collective-permute-start.10 = (f32[4,128]{1,0:T(4,128)S(1)}, f32[4,128]{1,0:T(4,128)S(1)}, u32[]{:S(2)}, u32[]{:S(2)}) collective-permute-start(f32[4,128]{1,0:T(4,128)S(1)} %copy-done.19), channel_id=1, source_target_pairs={{0,2},{2,0},{1,3},{3,1},{4,6},{6,4},{5,7},{7,5},{8,10},{10,8},{9,1... | collective-permute-start | bytes 6152 | tf_op jit(solution)/shard_map/ppermute | solution.py:380
  42.2 0.6 copy-start.11
  42.2 0.6 copy-start.7
  42.2 0.6 copy-start.9
  42.2 0.7 %copy-start.2 = (f32[256,128]{1,0:T(8,128)}, f32[256,128]{1,0:T(8,128)S(1)}, u32[]{:S(2)}) copy-start(f32[256,128]{1,0:T(8,128)S(1)} %collective-permute-done.11.refs_10_) | copy-start | bytes 393220

commit v2 on v1

--- a/solution.py
+++ b/solution.py
@@ -120,14 +120,21 @@
     return ref[i // per, 8 * (i % per) : 8 * (i % per) + 8, :]
 
 
-def first_kernel(rounds, x_ref, k_ref, *refs):
-    sends, (own_ref,) = regroup(refs, rounds)
-    count = x_ref.shape[0] * x_ref.shape[1] // 8
-    for slot, ref in enumerate((x_ref, k_ref)):
-        columns = pack_columns(functools.partial(vreg, ref), count)
+def first_kernel(rounds, *refs):
+    sources, fields, refs = refs[:4], refs[4:8], refs[8:]
+    sends, (own_ref, sems) = regroup(refs, rounds)
+    copies = [pltpu.make_async_copy(a, b, sems.at[n]) for n, (a, b) in enumerate(zip(sources, fields))]
+    for copy in copies:
+        copy.start()
+    z, y, _ = fields[0].shape
+    for slot, ref in enumerate(fields[:2]):
+        copies[slot].wait()
+        columns = pack_columns(functools.partial(vreg, ref), z * y // 8)
         own_ref[slot, 0] = columns[0]
         own_ref[slot, 1] = columns[1]
         fill_sends(ref, sends, slot, columns)
+    for copy in copies[2:]:
+        copy.wait()
 
 
 def sweep_tile(value, weight, north, south, east, level):
@@ -212,7 +219,7 @@
         at = pl.multiple_of(t * tall, 8)
         near = pl.ds(at, tall)
         x = xp[i + 1, pl.ds(at + 8, tall), :]
-        width = band_ref[t, 0]
+        width = band_ref[0, t]
         band = jnp.where((row < width) | (row >= tall - width), band_sink, 0.0)
         sink = coolant_film * flow_ref[i].astype(F32) + band
         cn = cn_ref[i, near, :]
@@ -224,7 +231,7 @@
         base = i * (y // 8) + t * per
         diag = c_ref[i, near, :] / interval_increment + sink
         diag = diag + cd + cu + cn + cs + ce + cw + spread_columns(pairs, 0, base, per)
-        power = cat_ref[sel_ref[i, t, 0]]
+        power = cat_ref[sel_ref[i, 0, t]]
         r = power - sink * x + spread_columns(pairs, 1, base, per)
         r = r + cn * (xp[i + 1, pl.ds(at + 7, tall), :] - x) + cs * (xp[i + 1, pl.ds(at + 9, tall), :] - x)
         r = r + ce * (pltpu.roll(x, 127, 1) - x) + cw * (pltpu.roll(x, 1, 1) - x)
@@ -233,7 +240,7 @@
         diag_ref[i, near, :] = diag
         wt_ref[i, near, :] = weight
         r_ref[i, near, :] = r
-        u_ref[i, near, :] = sweep_tile(r, weight, cn, cs, ce, lev_ref[i, t, 0])
+        u_ref[i, near, :] = sweep_tile(r, weight, cn, cs, ce, lev_ref[i, 0, t])
         return carry
 
     tile_loop(z, tiles, body, 0)
@@ -284,7 +291,7 @@
 
     def body(i, t, carry):
         near, u, w, cn, cs, ce = apply_tile(i, t, tall, y, up, pairs, cz_ref, cn_ref, ce_ref, diag_ref)
-        m = sweep_tile(w, wt_ref[i, near, :], cn, cs, ce, lev_ref[i, t, 0])
+        m = sweep_tile(w, wt_ref[i, near, :], cn, cs, ce, lev_ref[i, 0, t])
         w_ref[i, near, :] = w
         m_ref[i, near, :] = m
         gamma, delta, cross = carry
@@ -358,13 +365,14 @@
     tall = dissipation_catalog.shape[1]
     groups = -(-(z * y // 8) // 128)
     rounds = tuple(2 if lax.axis_size(axis) > 2 else 1 for axis in GRID_AXES)
-    shape = lambda *s: jax.ShapeDtypeStruct(s, F32)
+    shape = lambda *s: pltpu.VMEM(s, F32)
     full = shape(z, y, x)
 
-    def call(kernel, outs, ins, name, scratch=()):
-        specs = [SMEM if v.dtype == jnp.int32 else VMEM for v in ins]
+    def call(kernel, outs, ins, name, scratch=(), specs=None):
+        specs = specs or [SMEM if v.dtype == jnp.int32 else VMEM for v in ins]
         return pl.pallas_call(
-            kernel, out_shape=outs, in_specs=specs, out_specs=[VMEM] * len(outs), scratch_shapes=list(scratch), name=name
+            kernel, out_shape=outs, in_specs=specs, out_specs=[VMEM] * len(outs), scratch_shapes=list(scratch), name=name,
+            compiler_params=pltpu.CompilerParams(vmem_limit_bytes=16 * 2**20),
         )(*ins)
 
     def face_shapes(front):
@@ -383,30 +391,24 @@
     sends = sum(rounds)
     pairs = pltpu.VMEM((2, 2, groups, 8, 128), F32)
     padded = pltpu.VMEM((z + 2, y + 16, x), F32)
-    levels = refine_depth
 
     outs = call(
         functools.partial(first_kernel, rounds),
-        face_shapes((2,)) + [shape(2, 2, 8 * groups, x)],
-        [earlier_warmth_field, thermal_diffusivity_coefficient],
+        [full, full, full, shape(*dissipation_catalog.shape)] + face_shapes((2,)) + [shape(2, 2, 8 * groups, x)],
+        [earlier_warmth_field, thermal_diffusivity_coefficient, caloric_storage, dissipation_catalog],
         "faces",
-    )
+        [pltpu.SemaphoreType.DMA((4,))],
+        [pl.BlockSpec(memory_space=pltpu.HBM)] * 4,
+    )
+    (field, kappa, storage, catalog), outs = outs[:4], outs[4:]
     own, halos = outs[sends], swap(outs[:sends])
+    selector = jnp.swapaxes(dissipation_selector, 1, 2)
+    levels = jnp.swapaxes(refine_depth, 1, 2)
+    width = jnp.swapaxes(border_band_width, 0, 1)
     outs = call(
         functools.partial(second_kernel, rounds, tall),
         [full, full, shape(z + 1, y, x), shape(z, y + 8, x), full, full, full, shape(2, 8 * groups, x)] + face_shapes(()),
-        [
-            earlier_warmth_field,
-            caloric_storage,
-            thermal_diffusivity_coefficient,
-            dissipation_catalog,
-            own,
-            dissipation_selector,
-            levels,
-            border_band_width,
-            microflow_flag,
-        ]
-        + halos,
+        [field, storage, kappa, catalog, own, selector, levels, width, microflow_flag] + halos,
         "residual",
         [padded, padded, pairs],
     )
@@ -431,7 +433,7 @@
     )
     every = lax.all_to_all(parts, GRID_AXES, 0, 0, tiled=True)
     return tuple(
-        call(last_kernel, [full, full], [every, earlier_warmth_field, r, u, w, m, n], "update")
+        call(last_kernel, [jax.ShapeDtypeStruct((z, y, x), F32)] * 2, [every, field, r, u, w, m, n], "update")
     )
 
 

time: 64.7 us -> 54.6 us (0.84)
  Pallas kernels: 25.2 us -> 13.8 us
  waiting for transfers between devices: 3.73 us -> 6.33 us
  starting transfers between devices: 17 us -> 16.1 us
  local copies, waits for them, and re-layouts: 4.09 us -> 4.74 us
    pallas_call x5, Pallas kernels: 25.2 us -> 13.8 us  [call(): pl.pallas_call(kernel, out_shape=outs, in_specs=specs, out_specs=[VMEM] *...]
    ppermute x12, waiting for transfers between devices: 3.73 us -> 6.33 us  [swap(): got.append(lax.ppermute(faces.pop(0), axis, swap_pairs(axis, start)))]
    ppermute x12, starting transfers between devices: 17 us -> 16.1 us  [swap(): got.append(lax.ppermute(faces.pop(0), axis, swap_pairs(axis, start)))]
    unnamed x43 -> x16, local copies, waits for them, and re-layouts: 4.09 us -> 4.74 us
  transfers between devices with their start and end apart: 12 -> 12, of which waited for: 3 -> 3; matrix products, arithmetic and copies ran while one was open for 3% -> 0% of each run, Pallas kernels for 0% -> 0%
where the time goes in v2:
time: 54.6 us; the launch traced here: 54.3 us
  starting transfers between devices  16.1 us (29%)
  Pallas kernels  13.8 us (25%)
  blocking collectives  12.5 us (23%)
  waiting for transfers between devices  6.33 us (12%)
  local copies, waits for them, and re-layouts  4.74 us (9%)
  between operations  0.74 us (1%)
    ppermute x12, starting transfers between devices, swap(): got.append(lax.ppermute(faces.pop(0), axis, swap_pairs(axis, start)))  16.1 us
    pallas_call x5, Pallas kernels, call(): pl.pallas_call(kernel, out_shape=outs, in_specs=specs, out_specs=[VMEM] *...  13.8 us
    all_to_all x1, blocking collectives, body(): every = lax.all_to_all(parts, GRID_AXES, 0, 0, tiled=True)  12.5 us
    ppermute x12, waiting for transfers between devices, swap(): got.append(lax.ppermute(faces.pop(0), axis, swap_pairs(axis, start)))  6.33 us
    unnamed x16, local copies, waits for them, and re-layouts  4.74 us
  transfers between devices with their start and end apart: 12, of which 3 were waited for; matrix products, arithmetic and copies ran while one was open for 0% of the time, Pallas kernels for 0%

profile of v2, /device:TPU:0, one launch (start us, length us, event | category | flops | bytes accessed | tf_op | source)
XLA Modules:
  0.0 54.3 jit_solution(9717779435276699867)
XLA Ops:
  0.6 0.0 copy-start
  0.6 1.0 %copy-done = f32[4,256,128]{2,1,0:T(8,128)S(1)} copy-done((f32[4,256,128]{2,1,0:T(8,128)S(1)}, f32[4,256,128]{2,1,0:T(8,128)}, u32[]{:S(2)}) %copy-start) | copy-done | bytes 524312
  1.7 0.0 copy-start.1
  1.7 1.0 %copy-done.1 = f32[4,256,128]{2,1,0:T(8,128)S(1)} copy-done((f32[4,256,128]{2,1,0:T(8,128)S(1)}, f32[4,256,128]{2,1,0:T(8,128)}, u32[]{:S(2)}) %copy-start.1) | copy-done | bytes 524312
  2.7 0.0 copy-start.2
  2.7 1.0 %copy-done.2 = f32[4,256,128]{2,1,0:T(8,128)S(1)} copy-done((f32[4,256,128]{2,1,0:T(8,128)S(1)}, f32[4,256,128]{2,1,0:T(8,128)}, u32[]{:S(2)}) %copy-start.2) | copy-done | bytes 524312
  3.8 0.0 copy-start.3
  3.8 0.9 %copy-done.3 = f32[8,64,128]{2,1,0:T(8,128)S(1)} copy-done((f32[8,64,128]{2,1,0:T(8,128)S(1)}, f32[8,64,128]{2,1,0:T(8,128)}, u32[]{:S(2)}) %copy-start.3) | copy-done | bytes 262168
  4.7 0.7 %faces.1 = (f32[4,256,128]{2,1,0:T(8,128)S(1)}, f32[4,256,128]{2,1,0:T(8,128)S(1)}, f32[4,256,128]{2,1,0:T(8,128)S(1)}, f32[8,64,128]{2,1,0:T(8,128)S(1)}, f32[2...) custom-call(f32[4,256,128]{2,1,0:T(8,128)S(1)} %copy-done, ...), custom_call_target="tpu_custom_call" | custom-call | tf_op jit(solution)/shard_map/faces/pallas_call | solution.py:373
  5.4 0.6 %collective-permute-start.3 = (f32[2,256,128]{2,1,0:T(8,128)S(1)}, f32[2,256,128]{2,1,0:T(8,128)S(1)}, u32[]{:S(2)}, u32[]{:S(2)}) collective-permute-start(f32[2,256,128]{2,1,0:T(8,128)S(1)} %get-tuple-element.40), channel_id=1, source_target_pairs={{0,1},{1,0},{2,3},{3,2},{4,5},{5,4},{6,7},{7,6},{8,9},{9,8},{10,11... | collective-permute-start | bytes 786440 | tf_op jit(solution)/shard_map/ppermute | solution.py:388
  6.0 2.6 %collective-permute-start = (f32[2,8,128]{2,1,0:T(8,128)S(1)}, f32[2,8,128]{2,1,0:T(8,128)S(1)}, u32[]{:S(2)}, u32[]{:S(2)}) collective-permute-start(f32[2,8,128]{2,1,0:T(8,128)S(1)} %get-tuple-element.37), channel_id=1, source_target_pairs={{0,4},{4,0},{8,12},{12,8},{1,5},{5,1},{9,13},{13,9},{2,6},{6,2},{1... | collective-permute-start | bytes 24584 | tf_op jit(solution)/shard_map/ppermute | solution.py:388
  8.6 0.6 %collective-permute-start.1 = (f32[2,8,128]{2,1,0:T(8,128)S(1)}, f32[2,8,128]{2,1,0:T(8,128)S(1)}, u32[]{:S(2)}, u32[]{:S(2)}) collective-permute-start(f32[2,8,128]{2,1,0:T(8,128)S(1)} %get-tuple-element.38), channel_id=1, source_target_pairs={{4,8},{8,4},{5,9},{9,5},{6,10},{10,6},{7,11},{11,7},{20,24},{24,20... | collective-permute-start | bytes 24584 | tf_op jit(solution)/shard_map/ppermute | solution.py:388
  9.3 1.6 %collective-permute-start.2 = (f32[2,4,128]{2,1,0:T(4,128)S(1)}, f32[2,4,128]{2,1,0:T(4,128)S(1)}, u32[]{:S(2)}, u32[]{:S(2)}) collective-permute-start(f32[2,4,128]{2,1,0:T(4,128)S(1)} %get-tuple-element.39), channel_id=1, source_target_pairs={{0,2},{2,0},{1,3},{3,1},{4,6},{6,4},{5,7},{7,5},{8,10},{10,8},{9,1... | collective-permute-start | bytes 12296 | tf_op jit(solution)/shard_map/ppermute | solution.py:388
  10.8 2.1 %collective-permute-done.2.refs_11_ = f32[2,4,128]{2,1,0:T(4,128)S(1)} collective-permute-done((f32[2,4,128]{2,1,0:T(4,128)S(1)}, f32[2,4,128]{2,1,0:T(4,128)S(1)}, u32[]{:S(2)}, u32[]{:S(2)}) %collective-permute-start.2) | collective-permute-done | bytes 4128 | tf_op jit(solution)/shard_map/ppermute | solution.py:388
  13.0 0.0 collective-permute-done.refs_9_
  13.0 0.0 collective-permute-done.1.refs_10_
  13.0 0.0 collective-permute-done.3.refs_12_
  13.0 0.0 copy-start.5
  13.0 0.0 copy-start.4
  13.0 0.0 copy-start.6
  13.0 0.0 copy-start.7
  13.0 0.6 %copy-done.5 = s32[4,4,1]{1,2,0:T(1,128)S(1)} copy-done((s32[4,4,1]{1,2,0:T(1,128)S(1)}, s32[4,4,1]{1,2,0:T(1,128)}, u32[]{:S(2)}) %copy-start.5) | copy-done | bytes 88
  13.7 0.0 copy-done.4
  13.7 0.0 copy-done.6
  13.7 0.0 copy-done.7
  13.7 5.7 %residual.1 = (f32[4,256,128]{2,1,0:T(8,128)S(1)}, f32[4,256,128]{2,1,0:T(8,128)S(1)}, f32[5,256,128]{2,1,0:T(8,128)S(1)}, f32[4,264,128]{2,1,0:T(8,128)S(1)}, f...) custom-call(f32[4,256,128]{2,1,0:T(8,128)S(1)} %get-tuple-element.32, ...), custom_call_target="tpu_custom_call" | custom-call | tf_op jit(solution)/shard_map/residual/pallas_call | solution.py:373
  19.4 0.0 collective-permute-start.7
  19.4 4.6 %collective-permute-start.4 = (f32[8,128]{1,0:T(8,128)S(1)}, f32[8,128]{1,0:T(8,128)S(1)}, u32[]{:S(2)}, u32[]{:S(2)}) collective-permute-start(f32[8,128]{1,0:T(8,128)S(1)} %get-tuple-element.49), channel_id=1, source_target_pairs={{0,4},{4,0},{8,12},{12,8},{1,5},{5,1},{9,13},{13,9},{2,6},{6,2},{1... | collective-permute-start | bytes 12296 | tf_op jit(solution)/shard_map/ppermute | solution.py:388
  23.9 0.6 %collective-permute-start.5 = (f32[8,128]{1,0:T(8,128)S(1)}, f32[8,128]{1,0:T(8,128)S(1)}, u32[]{:S(2)}, u32[]{:S(2)}) collective-permute-start(f32[8,128]{1,0:T(8,128)S(1)} %get-tuple-element.50), channel_id=1, source_target_pairs={{4,8},{8,4},{5,9},{9,5},{6,10},{10,6},{7,11},{11,7},{20,24},{24,20... | collective-permute-start | bytes 12296 | tf_op jit(solution)/shard_map/ppermute | solution.py:388
  24.6 1.6 %collective-permute-start.6 = (f32[4,128]{1,0:T(4,128)S(1)}, f32[4,128]{1,0:T(4,128)S(1)}, u32[]{:S(2)}, u32[]{:S(2)}) collective-permute-start(f32[4,128]{1,0:T(4,128)S(1)} %get-tuple-element.51), channel_id=1, source_target_pairs={{0,2},{2,0},{1,3},{3,1},{4,6},{6,4},{5,7},{7,5},{8,10},{10,8},{9,1... | collective-permute-start | bytes 6152 | tf_op jit(solution)/shard_map/ppermute | solution.py:388
  26.2 2.0 %collective-permute-done.6.refs_11_ = f32[4,128]{1,0:T(4,128)S(1)} collective-permute-done((f32[4,128]{1,0:T(4,128)S(1)}, f32[4,128]{1,0:T(4,128)S(1)}, u32[]{:S(2)}, u32[]{:S(2)}) %collective-permute-start.6) | collective-permute-done | bytes 2080 | tf_op jit(solution)/shard_map/ppermute | solution.py:388
  28.2 0.0 collective-permute-done.4.refs_9_
  28.3 0.0 collective-permute-done.5.refs_10_
  28.3 0.0 collective-permute-done.7.refs_12_
  28.3 3.9 %applied.1 = (f32[4,256,128]{2,1,0:T(8,128)S(1)}, f32[4,256,128]{2,1,0:T(8,128)S(1)}, f32[3,8,128]{2,1,0:T(8,128)S(1)}, f32[8,128]{1,0:T(8,128)S(1)}, f32[8,128]...) custom-call(f32[4,256,128]{2,1,0:T(8,128)S(1)} %get-tuple-element.41.refs_0_.u_ref, ...), custom_call_target="tpu_custom_call" | custom-call | tf_op jit(solution)/shard_map/applied/pallas_call | solution.py:373
  32.2 0.0 collective-permute-start.11
  32.2 1.7 %collective-permute-start.8 = (f32[8,128]{1,0:T(8,128)S(1)}, f32[8,128]{1,0:T(8,128)S(1)}, u32[]{:S(2)}, u32[]{:S(2)}) collective-permute-start(f32[8,128]{1,0:T(8,128)S(1)} %get-tuple-element.55), channel_id=1, source_target_pairs={{0,4},{4,0},{8,12},{12,8},{1,5},{5,1},{9,13},{13,9},{2,6},{6,2},{1... | collective-permute-start | bytes 12296 | tf_op jit(solution)/shard_map/ppermute | solution.py:388
  33.9 0.6 %collective-permute-start.9 = (f32[8,128]{1,0:T(8,128)S(1)}, f32[8,128]{1,0:T(8,128)S(1)}, u32[]{:S(2)}, u32[]{:S(2)}) collective-permute-start(f32[8,128]{1,0:T(8,128)S(1)} %get-tuple-element.56), channel_id=1, source_target_pairs={{4,8},{8,4},{5,9},{9,5},{6,10},{10,6},{7,11},{11,7},{20,24},{24,20... | collective-permute-start | bytes 12296 | tf_op jit(solution)/shard_map/ppermute | solution.py:388
  34.6 1.5 %collective-permute-start.10 = (f32[4,128]{1,0:T(4,128)S(1)}, f32[4,128]{1,0:T(4,128)S(1)}, u32[]{:S(2)}, u32[]{:S(2)}) collective-permute-start(f32[4,128]{1,0:T(4,128)S(1)} %get-tuple-element.57), channel_id=1, source_target_pairs={{0,2},{2,0},{1,3},{3,1},{4,6},{6,4},{5,7},{7,5},{8,10},{10,8},{9,1... | collective-permute-start | bytes 6152 | tf_op jit(solution)/shard_map/ppermute | solution.py:388
  36.0 2.2 %collective-permute-done.10.refs_9_ = f32[4,128]{1,0:T(4,128)S(1)} collective-permute-done((f32[4,128]{1,0:T(4,128)S(1)}, f32[4,128]{1,0:T(4,128)S(1)}, u32[]{:S(2)}, u32[]{:S(2)}) %collective-permute-start.10) | collective-permute-done | bytes 2080 | tf_op jit(solution)/shard_map/ppermute | solution.py:388
  38.2 0.0 collective-permute-done.8.refs_7_
  38.2 0.0 collective-permute-done.9.refs_8_
  38.2 0.0 collective-permute-done.11.refs_10_
  38.2 2.0 %twice.1 = (f32[4,256,128]{2,1,0:T(8,128)S(1)}, f32[16,4,128]{2,1,0:T(4,128)S(1)}) custom-call(f32[4,256,128]{2,1,0:T(8,128)S(1)} %get-tuple-element.53.refs_0_.m_ref, f32[3,8,128]{2,1,0:T(8,128)S(1)} %get-tuple-element.54.refs_1_, f32[5,256,128]{2,1,0:T(8,128)S(1)} %get-tuple-element.43.refs_2_, f32[4,264,128]{2,1,0:T(8,128)S(1)} %get-tuple-element.44.refs_3_, ...), custom_call_target="tpu_custom_call" | custom-call | tf_op jit(solution)/shard_map/twice/pallas_call | solution.py:373
  40.3 12.5 %all_to_all.5.all_ref = f32[16,4,128]{2,1,0:T(4,128)S(1)} all-to-all(f32[16,4,128]{2,1,0:T(4,128)S(1)} %get-tuple-element.59), channel_id=1, replica_groups=mesh['groups'=2,'gx'=4,'gy'=2,'gz'=2] {'gx','gy','gz'}, dimensions={0} | all-to-all | bytes 65536 | tf_op jit(solution)/shard_map/all_to_all | solution.py:434
  52.8 1.5 %update.1 = (f32[4,256,128]{2,1,0:T(8,128)}, f32[4,256,128]{2,1,0:T(8,128)}) custom-call(f32[16,4,128]{2,1,0:T(4,128)S(1)} %all_to_all.5.all_ref, f32[4,256,128]{2,1,0:T(8,128)S(1)} %get-tuple-element.32.refs_0_.x_ref, f32[4,256,128]{2,1,0:T(8,128)S(1)} %get-tuple-element.42.refs_1_.r_ref, f32[4,256,128]{2,1,0:T(8,128)S(1)} %get-tuple-element.41.refs_0_.u_ref, ...), custom_call_target="tpu_custom_call" | custom-call | tf_op jit(solution)/shard_map/update/pallas_call | solution.py:373
Async XLA Ops:
  0.6 1.0 %copy-start = (f32[4,256,128]{2,1,0:T(8,128)S(1)}, f32[4,256,128]{2,1,0:T(8,128)}, u32[]{:S(2)}) copy-start(f32[4,256,128]{2,1,0:T(8,128)} %refs_0_.1) | copy-start | bytes 1572868
  1.7 1.0 %copy-start.1 = (f32[4,256,128]{2,1,0:T(8,128)S(1)}, f32[4,256,128]{2,1,0:T(8,128)}, u32[]{:S(2)}) copy-start(f32[4,256,128]{2,1,0:T(8,128)} %refs_1_.1) | copy-start | bytes 1572868
  2.7 1.0 %copy-start.2 = (f32[4,256,128]{2,1,0:T(8,128)S(1)}, f32[4,256,128]{2,1,0:T(8,128)}, u32[]{:S(2)}) copy-start(f32[4,256,128]{2,1,0:T(8,128)} %refs_2_.1) | copy-start | bytes 1572868
  3.8 0.9 %copy-start.3 = (f32[8,64,128]{2,1,0:T(8,128)S(1)}, f32[8,64,128]{2,1,0:T(8,128)}, u32[]{:S(2)}) copy-start(f32[8,64,128]{2,1,0:T(8,128)} %refs_3_.1) | copy-start | bytes 786436
  5.4 7.5 %collective-permute-start.3 = (f32[2,256,128]{2,1,0:T(8,128)S(1)}, f32[2,256,128]{2,1,0:T(8,128)S(1)}, u32[]{:S(2)}, u32[]{:S(2)}) collective-permute-start(f32[2,256,128]{2,1,0:T(8,128)S(1)} %get-tuple-element.40), channel_id=1, source_target_pairs={{0,1},{1,0},{2,3},{3,2},{4,5},{5,4},{6,7},{7,6},{8,9},{9,8},{10,11... | collective-permute-start | bytes 786440 | tf_op jit(solution)/shard_map/ppermute | solution.py:388
  6.0 7.0 %collective-permute-start = (f32[2,8,128]{2,1,0:T(8,128)S(1)}, f32[2,8,128]{2,1,0:T(8,128)S(1)}, u32[]{:S(2)}, u32[]{:S(2)}) collective-permute-start(f32[2,8,128]{2,1,0:T(8,128)S(1)} %get-tuple-element.37), channel_id=1, source_target_pairs={{0,4},{4,0},{8,12},{12,8},{1,5},{5,1},{9,13},{13,9},{2,6},{6,2},{1... | collective-permute-start | bytes 24584 | tf_op jit(solution)/shard_map/ppermute | solution.py:388
  8.6 4.3 %collective-permute-start.1 = (f32[2,8,128]{2,1,0:T(8,128)S(1)}, f32[2,8,128]{2,1,0:T(8,128)S(1)}, u32[]{:S(2)}, u32[]{:S(2)}) collective-permute-start(f32[2,8,128]{2,1,0:T(8,128)S(1)} %get-tuple-element.38), channel_id=1, source_target_pairs={{4,8},{8,4},{5,9},{9,5},{6,10},{10,6},{7,11},{11,7},{20,24},{24,20... | collective-permute-start | bytes 24584 | tf_op jit(solution)/shard_map/ppermute | solution.py:388
  9.3 3.7 %collective-permute-start.2 = (f32[2,4,128]{2,1,0:T(4,128)S(1)}, f32[2,4,128]{2,1,0:T(4,128)S(1)}, u32[]{:S(2)}, u32[]{:S(2)}) collective-permute-start(f32[2,4,128]{2,1,0:T(4,128)S(1)} %get-tuple-element.39), channel_id=1, source_target_pairs={{0,2},{2,0},{1,3},{3,1},{4,6},{6,4},{5,7},{7,5},{8,10},{10,8},{9,1... | collective-permute-start | bytes 12296 | tf_op jit(solution)/shard_map/ppermute | solution.py:388
  13.0 0.7 %copy-start.5 = (s32[4,4,1]{1,2,0:T(1,128)S(1)}, s32[4,4,1]{1,2,0:T(1,128)}, u32[]{:S(2)}) copy-start(s32[4,4,1]{1,2,0:T(1,128)} %param.12) | copy-start | bytes 196
  13.0 0.7 %copy-start.4 = (s32[4,4,1]{1,2,0:T(1,128)S(1)}, s32[4,4,1]{1,2,0:T(1,128)}, u32[]{:S(2)}) copy-start(s32[4,4,1]{1,2,0:T(1,128)} %param.13) | copy-start | bytes 196
  13.0 0.7 %copy-start.6 = (s32[4,1]{0,1:T(1,128)S(1)}, s32[4,1]{0,1:T(1,128)}, u32[]{:S(2)}) copy-start(s32[4,1]{0,1:T(1,128)} %param.14) | copy-start | bytes 52
  13.0 0.7 %copy-start.7 = (s32[4]{0:T(128)S(1)}, s32[4]{0:T(128)}, u32[]{:S(2)}) copy-start(s32[4]{0:T(128)} %refs_8_.1) | copy-start | bytes 52
  19.4 8.9 %collective-permute-start.7 = (f32[256,128]{1,0:T(8,128)S(1)}, f32[256,128]{1,0:T(8,128)S(1)}, u32[]{:S(2)}, u32[]{:S(2)}) collective-permute-start(f32[256,128]{1,0:T(8,128)S(1)} %get-tuple-element.52), channel_id=1, source_target_pairs={{0,1},{1,0},{2,3},{3,2},{4,5},{5,4},{6,7},{7,6},{8,9},{9,8},{10,11... | collective-permute-start | bytes 393224 | tf_op jit(solution)/shard_map/ppermute | solution.py:388
  19.4 8.9 %collective-permute-start.4 = (f32[8,128]{1,0:T(8,128)S(1)}, f32[8,128]{1,0:T(8,128)S(1)}, u32[]{:S(2)}, u32[]{:S(2)}) collective-permute-start(f32[8,128]{1,0:T(8,128)S(1)} %get-tuple-element.49), channel_id=1, source_target_pairs={{0,4},{4,0},{8,12},{12,8},{1,5},{5,1},{9,13},{13,9},{2,6},{6,2},{1... | collective-permute-start | bytes 12296 | tf_op jit(solution)/shard_map/ppermute | solution.py:388
  23.9 4.3 %collective-permute-start.5 = (f32[8,128]{1,0:T(8,128)S(1)}, f32[8,128]{1,0:T(8,128)S(1)}, u32[]{:S(2)}, u32[]{:S(2)}) collective-permute-start(f32[8,128]{1,0:T(8,128)S(1)} %get-tuple-element.50), channel_id=1, source_target_pairs={{4,8},{8,4},{5,9},{9,5},{6,10},{10,6},{7,11},{11,7},{20,24},{24,20... | collective-permute-start | bytes 12296 | tf_op jit(solution)/shard_map/ppermute | solution.py:388
  24.6 3.7 %collective-permute-start.6 = (f32[4,128]{1,0:T(4,128)S(1)}, f32[4,128]{1,0:T(4,128)S(1)}, u32[]{:S(2)}, u32[]{:S(2)}) collective-permute-start(f32[4,128]{1,0:T(4,128)S(1)} %get-tuple-element.51), channel_id=1, source_target_pairs={{0,2},{2,0},{1,3},{3,1},{4,6},{6,4},{5,7},{7,5},{8,10},{10,8},{9,1... | collective-permute-start | bytes 6152 | tf_op jit(solution)/shard_map/ppermute | solution.py:388
  32.2 6.0 %collective-permute-start.11 = (f32[256,128]{1,0:T(8,128)S(1)}, f32[256,128]{1,0:T(8,128)S(1)}, u32[]{:S(2)}, u32[]{:S(2)}) collective-permute-start(f32[256,128]{1,0:T(8,128)S(1)} %get-tuple-element.58), channel_id=1, source_target_pairs={{0,1},{1,0},{2,3},{3,2},{4,5},{5,4},{6,7},{7,6},{8,9},{9,8},{10,11... | collective-permute-start | bytes 393224 | tf_op jit(solution)/shard_map/ppermute | solution.py:388
  32.2 6.0 %collective-permute-start.8 = (f32[8,128]{1,0:T(8,128)S(1)}, f32[8,128]{1,0:T(8,128)S(1)}, u32[]{:S(2)}, u32[]{:S(2)}) collective-permute-start(f32[8,128]{1,0:T(8,128)S(1)} %get-tuple-element.55), channel_id=1, source_target_pairs={{0,4},{4,0},{8,12},{12,8},{1,5},{5,1},{9,13},{13,9},{2,6},{6,2},{1... | collective-permute-start | bytes 12296 | tf_op jit(solution)/shard_map/ppermute | solution.py:388
  33.9 4.3 %collective-permute-start.9 = (f32[8,128]{1,0:T(8,128)S(1)}, f32[8,128]{1,0:T(8,128)S(1)}, u32[]{:S(2)}, u32[]{:S(2)}) collective-permute-start(f32[8,128]{1,0:T(8,128)S(1)} %get-tuple-element.56), channel_id=1, source_target_pairs={{4,8},{8,4},{5,9},{9,5},{6,10},{10,6},{7,11},{11,7},{20,24},{24,20... | collective-permute-start | bytes 12296 | tf_op jit(solution)/shard_map/ppermute | solution.py:388
  34.6 3.7 %collective-permute-start.10 = (f32[4,128]{1,0:T(4,128)S(1)}, f32[4,128]{1,0:T(4,128)S(1)}, u32[]{:S(2)}, u32[]{:S(2)}) collective-permute-start(f32[4,128]{1,0:T(4,128)S(1)} %get-tuple-element.57), channel_id=1, source_target_pairs={{0,2},{2,0},{1,3},{3,1},{4,6},{6,4},{5,7},{7,5},{8,10},{10,8},{9,1... | collective-permute-start | bytes 6152 | tf_op jit(solution)/shard_map/ppermute | solution.py:388

commit v3 on v0

v3 whole, which is shorter than its diff:
```python
import functools
import math

import jax
import jax.numpy as jnp
from jax import lax
from jax.experimental import pallas as pl
from jax.experimental.pallas import tpu as pltpu
from jax.sharding import PartitionSpec as P

interval_increment = 0.5
vertical_ratio = 2.0
coolant_film = 1.5
band_sink = 1.0
damping = 0.8
GRID_AXES = ("gx", "gy", "gz")
VMEM = pl.BlockSpec(memory_space=pltpu.VMEM)
SMEM = pl.BlockSpec(memory_space=pltpu.SMEM)
F32 = jnp.float32


def harmonic(first, second):
    return 2.0 * first * second / (first + second)


def lanes(shape=(8, 128)):
    return lax.broadcasted_iota(jnp.int32, shape, len(shape) - 1)


def rows(shape):
    return lax.broadcasted_iota(jnp.int32, shape, 0)


def low_side(axis, turn):
    odd = lax.rem(lax.axis_index(axis), 2) == 1
    return ~odd if turn else odd


def regroup(refs, counts):
    out, at = [], 0
    for c in counts:
        out.append(refs[at : at + c])
        at += c
    return out, refs[at:]


def pack_columns(load, count):
    lane = lanes()
    firsts, lasts = [], []
    for start in range(0, count, 128):
        parts = [jnp.zeros((8, 128), F32), jnp.zeros((8, 128), F32)]
        for i in range(min(128, count - start)):
            turned = load(start + i)
            if i:
                turned = pltpu.roll(turned, i, 1)
            here = (lane == i) | (lane == (i + 127) % 128)
            parts[i % 2] = jnp.where(here, turned, parts[i % 2])
        even = lane % 2 == 0
        firsts.append(jnp.where(even, parts[0], parts[1]))
        lasts.append(pltpu.roll(jnp.where(even, parts[1], parts[0]), 1, 1))
    return jnp.concatenate(firsts, 0), jnp.concatenate(lasts, 0)


def stage_columns(first, last):
    even = lanes() % 2 == 0
    out = []
    for g in range(first.shape[0] // 8):
        f = first[8 * g : 8 * g + 8]
        l = pltpu.roll(last[8 * g : 8 * g + 8], 127, 1)
        out.append((jnp.where(even, f, l), jnp.where(even, l, f)))
    return out


def spread_columns(staged, edge, i):
    turned = staged[i // 128][i % 2]
    if i % 128:
        turned = pltpu.roll(turned, 128 - i % 128, 1)
    return jnp.where(edge, turned, 0.0)


def edge_lanes():
    lane = lanes()
    return (lane == 0) | (lane == 127)


def column_halos(refs, slot=()):
    low = low_side("gx", 0)
    got = [ref[slot] if slot else ref[...] for ref in refs]
    if len(got) == 1:
        got.append(jnp.zeros_like(got[0]))
    return jnp.where(low, got[0], got[1]), jnp.where(low, got[1], got[0])


def fill_sends(tier, row, send_refs, slot, columns, z, y):
    for axis, refs in zip(GRID_AXES, send_refs):
        for n, ref in enumerate(refs):
            low = low_side(axis, n)
            if axis == "gx":
                value = jnp.where(low, columns[0], columns[1])
            elif axis == "gy":
                value = jnp.where(low, row(0), row(y - 1))
            else:
                value = tier(jnp.where(low, 0, z - 1))
            if slot is None:
                ref[...] = value
            else:
                ref[slot] = value


def padded_access(ref):
    y = ref.shape[1] - 16

    def tier(i):
        return ref[i, pl.ds(8, y), :]

    def row(r):
        return ref[:, 8 + r, :]

    def vreg(i):
        return ref[i // (y // 8), 8 + 8 * (i % (y // 8)) : 16 + 8 * (i % (y // 8)), :]

    return tier, row, vreg


def clear_margins(ref):
    z, y, _ = ref.shape
    for i in range(z):
        ref[i, 0:8, :] = jnp.zeros((8, 128), F32)
        ref[i, y - 8 : y, :] = jnp.zeros((8, 128), F32)


def start_all(sources, targets, sems):
    copies = [pltpu.make_async_copy(a, b, sems.at[n]) for n, (a, b) in enumerate(zip(sources, targets))]
    for copy in copies:
        copy.start()
    return copies


def faces_kernel(rounds, x_in, k_in, sel_in, lev_in, band_in, flow_in, *refs):
    (x_ref, k_ref, sel_ref, lev_ref, band_ref, flow_ref), refs = refs[:6], refs[6:]
    sends, (own_ref, sems) = regroup(refs, rounds)
    z, y, _ = x_in.shape
    inner = pl.ds(8, y)
    copies = start_all(
        (x_in, k_in, sel_in, lev_in, band_in, flow_in),
        (x_ref.at[:, inner, :], k_ref.at[:, inner, :], sel_ref, lev_ref, band_ref, flow_ref),
        sems,
    )
    for slot, ref in enumerate((x_ref, k_ref)):
        clear_margins(ref)
        copies[slot].wait()
        tier, row, vreg = padded_access(ref)
        columns = pack_columns(vreg, z * y // 8)
        own_ref[slot, 0] = columns[0]
        own_ref[slot, 1] = columns[1]
        fill_sends(tier, row, sends, slot, columns, z, y)
    for copy in copies[2:]:
        copy.wait()


def inner_kernel(tall, x_ref, k_ref, c_in, cat_in, sel_ref, band_ref, flow_ref, *refs):
    r_ref, diag_ref, cz_ref, cs_ref, ce_ref, c_ref, cat_ref, sems = refs
    z, y, _ = c_ref.shape
    copies = start_all((c_in, cat_in), (c_ref, cat_ref), sems)
    lane = lanes((tall, 128))
    row = rows((tall, 128))
    for i in range(z):
        cs_ref[i, 0:8, :] = jnp.zeros((8, 128), F32)

    def faces(t, carry):
        at = pl.multiple_of(t * tall, 8)
        last = jnp.where(t == y // tall - 1, tall - 1, tall)
        for i in range(z):
            here = k_ref[i, pl.ds(at + 8, tall), :]
            south = harmonic(here, k_ref[i, pl.ds(at + 9, tall), :])
            cs_ref[i, pl.ds(at + 8, tall), :] = jnp.where(row == last, 0.0, south)
            ce_ref[i, pl.ds(at, tall), :] = jnp.where(lane == 127, 0.0, harmonic(here, pltpu.roll(here, 127, 1)))
            if i + 1 < z:
                above = k_ref[i + 1, pl.ds(at + 8, tall), :]
                cz_ref[i, pl.ds(at, tall), :] = vertical_ratio * harmonic(here, above)
        return carry

    lax.fori_loop(0, y // tall, faces, 0)
    for copy in copies:
        copy.wait()

    def rest(t, carry):
        at = pl.multiple_of(t * tall, 8)
        near = pl.ds(at, tall)
        mid = pl.ds(at + 8, tall)
        width = band_ref[0, t]
        band = jnp.where((row < width) | (row >= tall - width), band_sink, 0.0)
        for i in range(z):
            x = x_ref[i, mid, :]
            sink = coolant_film * flow_ref[i].astype(F32) + band
            cn = cs_ref[i, pl.ds(at + 7, tall), :]
            cs = cs_ref[i, mid, :]
            ce = ce_ref[i, near, :]
            cw = pltpu.roll(ce, 1, 1)
            r = cat_ref[sel_ref[i, 0, t]] - sink * x
            r = r + cn * (x_ref[i, pl.ds(at + 7, tall), :] - x) + cs * (x_ref[i, pl.ds(at + 9, tall), :] - x)
            r = r + ce * (pltpu.roll(x, 127, 1) - x) + cw * (pltpu.roll(x, 1, 1) - x)
            diag = c_ref[i, near, :] * (1.0 / interval_increment) + sink
            diag = diag + ((cn + cs) + (ce + cw))
            if i:
                cd = cz_ref[i - 1, near, :]
                diag = diag + cd
                r = r + cd * (x_ref[i - 1, mid, :] - x)
            if i + 1 < z:
                cu = cz_ref[i, near, :]
                diag = diag + cu
                r = r + cu * (x_ref[i + 1, mid, :] - x)
            diag_ref[i, near, :] = diag
            r_ref[i, near, :] = r
        return carry

    lax.fori_loop(0, y // tall, rest, 0)


def sweeps(field_ref, diag_ref, cs_ref, ce_ref, lev_ref, tall):
    z, y, _ = diag_ref.shape
    tiles = y // tall
    row = rows((tall, 128))

    def tile(i, t):
        level = lev_ref[i, 0, t]

        @pl.when(level > 1)
        def _():
            at = pl.multiple_of(t * tall, 8)
            mid = pl.ds(at + 8, tall)
            start = field_ref[i, mid, :]
            weight = damping / diag_ref[i, pl.ds(at, tall), :]
            north = jnp.where(row == 0, 0.0, cs_ref[i, pl.ds(at + 7, tall), :])
            south = jnp.where(row == tall - 1, 0.0, cs_ref[i, mid, :])
            east = ce_ref[i, pl.ds(at, tall), :]

            def once(_, state):
                inner = north * pltpu.roll(state, 1, 0) + south * pltpu.roll(state, tall - 1, 0)
                inner = inner + east * pltpu.roll(state, 127, 1) + pltpu.roll(east * state, 1, 1)
                return (1.0 - damping) * state + (start + weight * inner)

            field_ref[i, mid, :] = lax.fori_loop(1, jnp.minimum(level, 4), once, start)

    def tier(i, carry):
        def step(t, carry):
            tile(i, t)
            return carry

        return lax.fori_loop(0, tiles, step, carry)

    lax.fori_loop(0, z, tier, 0)


def border_kernel(rounds, tall, *refs):
    (x_ref, k_ref, own_ref, r_in, diag_in, cs_ref, ce_ref, lev_ref), refs = refs[:8], refs[8:]
    (hx, hy, hz), refs = regroup(refs, rounds)
    (r_ref, diag_ref, u_ref, cx_ref, cy_ref, czh_ref), refs = refs[:6], refs[6:]
    sends, _ = regroup(refs, rounds)
    z, y, _ = r_ref.shape
    for n, ref in enumerate(hz):
        p = jnp.where(low_side("gz", n), 0, z - 1)
        face = vertical_ratio * harmonic(k_ref[p, pl.ds(8, y), :], ref[1])
        czh_ref[n] = face
        diag_in[p] = diag_in[p] + face
        r_in[p] = r_in[p] + face * (ref[0] - x_ref[p, pl.ds(8, y), :])
    row8 = rows((8, 128))
    for n, ref in enumerate(hy):
        low = low_side("gy", n)
        at = pl.multiple_of(jnp.where(low, 0, y - 8), 8)
        mask = row8 == jnp.where(low, 0, 7)
        for i in range(z):
            there = pl.ds(at, 8)
            inside = pl.ds(at + 8, 8)
            face = harmonic(k_ref[i, inside, :], ref[1, i : i + 1, :])
            face = jnp.where(mask, face, 0.0)
            cy_ref[n, i] = face
            diag_in[i, there, :] = diag_in[i, there, :] + face
            r_in[i, there, :] = r_in[i, there, :] + face * (ref[0, i : i + 1, :] - x_ref[i, inside, :])
    xlo, xhi = column_halos(hx, (0,))
    klo, khi = column_halos(hx, (1,))
    west = harmonic(own_ref[1, 0], klo)
    east = harmonic(own_ref[1, 1], khi)
    cx_ref[0] = west
    cx_ref[1] = east
    faces = stage_columns(west, east)
    flux = stage_columns(west * (xlo - own_ref[0, 0]), east * (xhi - own_ref[0, 1]))
    edge = edge_lanes()
    clear_margins(u_ref)
    per = y // 8
    for i in range(z * per):
        at = (i // per, slice(8 * (i % per), 8 * (i % per) + 8))
        diag = diag_in[at] + spread_columns(faces, edge, i)
        r = r_in[at] + spread_columns(flux, edge, i)
        diag_ref[at] = diag
        r_ref[at] = r
        u_ref[i // per, 8 + 8 * (i % per) : 16 + 8 * (i % per)] = r * (damping / diag)
    sweeps(u_ref, diag_ref, cs_ref, ce_ref, lev_ref, tall)
    tier, row, vreg = padded_access(u_ref)
    fill_sends(tier, row, sends, None, pack_columns(vreg, z * per), z, y)


def apply_inner(field_ref, diag_ref, cz_ref, cs_ref, ce_ref, i, at, tall):
    z = diag_ref.shape[0]
    near = pl.ds(at, tall)
    mid = pl.ds(at + 8, tall)
    v = field_ref[i, mid, :]
    ce = ce_ref[i, near, :]
    total = cs_ref[i, pl.ds(at + 7, tall), :] * field_ref[i, pl.ds(at + 7, tall), :]
    total = total + cs_ref[i, mid, :] * field_ref[i, pl.ds(at + 9, tall), :]
    total = total + (ce * pltpu.roll(v, 127, 1) + pltpu.roll(ce * v, 1, 1))
    if i:
        total = total + cz_ref[i - 1, near, :] * field_ref[i - 1, mid, :]
    if i + 1 < z:
        total = total + cz_ref[i, near, :] * field_ref[i + 1, mid, :]
    return v, diag_ref[i, near, :] * v - total


def apply_kernel(tall, u_ref, diag_ref, cz_ref, cs_ref, ce_ref, w_ref):
    z, y, _ = diag_ref.shape

    def step(t, carry):
        at = pl.multiple_of(t * tall, 8)
        for i in range(z):
            w_ref[i, pl.ds(at, tall), :] = apply_inner(u_ref, diag_ref, cz_ref, cs_ref, ce_ref, i, at, tall)[1]
        return carry

    lax.fori_loop(0, y // tall, step, 0)


def subtract_halos(w_ref, halos, cy_ref, czh_ref):
    hx, hy, hz = halos
    z, y, _ = w_ref.shape
    for n, ref in enumerate(hz):
        p = jnp.where(low_side("gz", n), 0, z - 1)
        w_ref[p] = w_ref[p] - czh_ref[n] * ref[...]
    for n, ref in enumerate(hy):
        at = pl.ds(pl.multiple_of(jnp.where(low_side("gy", n), 0, y - 8), 8), 8)
        for i in range(z):
            w_ref[i, at, :] = w_ref[i, at, :] - cy_ref[n, i] * ref[i : i + 1, :]


def smooth_kernel(rounds, tall, *refs):
    (w_in, diag_ref, cs_ref, ce_ref, cx_ref, cy_ref, czh_ref, lev_ref), refs = refs[:8], refs[8:]
    halos, refs = regroup(refs, rounds)
    (w_ref, m_ref), refs = refs[:2], refs[2:]
    sends, _ = regroup(refs, rounds)
    z, y, _ = w_ref.shape
    subtract_halos(w_in, halos, cy_ref, czh_ref)
    xlo, xhi = column_halos(halos[0])
    flux = stage_columns(cx_ref[0] * xlo, cx_ref[1] * xhi)
    edge = edge_lanes()
    clear_margins(m_ref)
    per = y // 8
    for i in range(z * per):
        at = (i // per, slice(8 * (i % per), 8 * (i % per) + 8))
        w = w_in[at] - spread_columns(flux, edge, i)
        w_ref[at] = w
        m_ref[i // per, 8 + 8 * (i % per) : 16 + 8 * (i % per)] = w * (damping / diag_ref[at])
    sweeps(m_ref, diag_ref, cs_ref, ce_ref, lev_ref, tall)
    tier, row, vreg = padded_access(m_ref)
    fill_sends(tier, row, sends, None, pack_columns(vreg, z * per), z, y)


def fold(product):
    return jnp.sum(product.reshape(-1, 8, 128), axis=0)


def sums_kernel(tall, m_ref, u_ref, r_ref, w_ref, diag_ref, cz_ref, cs_ref, ce_ref, n_ref, sum_ref):
    z, y, _ = diag_ref.shape

    def step(t, carry):
        gamma, delta, cross = carry
        at = pl.multiple_of(t * tall, 8)
        near = pl.ds(at, tall)
        for i in range(z):
            m, n_ref[i, near, :] = apply_inner(m_ref, diag_ref, cz_ref, cs_ref, ce_ref, i, at, tall)
            u = u_ref[i, pl.ds(at + 8, tall), :]
            w = w_ref[i, near, :]
            gamma = gamma + fold(r_ref[i, near, :] * u)
            delta = delta + fold(w * u)
            cross = cross + fold(w * m)
        return gamma, delta, cross

    zero = jnp.zeros((8, 128), F32)
    for n, value in enumerate(lax.fori_loop(0, y // tall, step, (zero, zero, zero))):
        sum_ref[n] = value


def finish_kernel(rounds, *refs):
    (n_in, m_ref, sum_ref, cx_ref, cy_ref, czh_ref), refs = refs[:6], refs[6:]
    halos, (n_ref, out_ref) = regroup(refs, rounds)
    z, y, _ = n_ref.shape
    subtract_halos(n_in, halos, cy_ref, czh_ref)
    xlo, xhi = column_halos(halos[0])
    flux = stage_columns(cx_ref[0] * xlo, cx_ref[1] * xhi)
    edge = edge_lanes()
    per = y // 8
    parts = [jnp.zeros((8, 128), F32) for _ in range(8)]
    for i in range(z * per):
        at = (i // per, slice(8 * (i % per), 8 * (i % per) + 8))
        n = n_in[at] - spread_columns(flux, edge, i)
        n_ref[at] = n
        parts[i % 8] = parts[i % 8] + n * m_ref[i // per, 8 + 8 * (i % per) : 16 + 8 * (i % per)]
    while len(parts) > 1:
        parts = [a + b for a, b in zip(parts[::2], parts[1::2])]
    parts = [sum_ref[0], sum_ref[1], sum_ref[2], parts[0]]
    parts = jnp.concatenate([jnp.sum(p, axis=0, keepdims=True) for p in parts], 0)
    for d in range(out_ref.shape[0]):
        out_ref[d] = parts


def update_kernel(all_ref, x_ref, r_ref, u_ref, w_ref, m_ref, n_ref, x_out, r_out, xo_ref, ro_ref, sems):
    sums = jnp.sum(all_ref[...], axis=0)
    gamma, delta, cross, last = (sums[i : i + 1] for i in range(4))

    def total(v):
        return jnp.sum(v, axis=1, keepdims=True)

    gamma0 = total(gamma)
    alpha0 = gamma0 / total(delta)
    gamma1 = total(gamma - 2.0 * alpha0 * delta + alpha0 * alpha0 * cross)
    delta1 = total(delta - 2.0 * alpha0 * cross + alpha0 * alpha0 * last)
    beta = gamma1 / gamma0
    alpha1 = gamma1 / (delta1 - beta * gamma1 / alpha0)
    near = alpha0 + alpha1 * (1.0 + beta)
    far = alpha1 * alpha0
    z, y, _ = r_ref.shape
    copies = []
    for i in range(z):
        inner = (i, slice(8, 8 + y))
        xo_ref[i] = x_ref[inner] + near * u_ref[inner] - far * m_ref[inner]
        ro_ref[i] = r_ref[i] - near * w_ref[i] + far * n_ref[i]
        copies += start_all((xo_ref.at[i], ro_ref.at[i]), (x_out.at[i], r_out.at[i]), sems.at[i])
    for copy in copies:
        copy.wait()


def swap_pairs(axis, start):
    count = lax.axis_size(axis)
    pairs = []
    for i in range(start, count - 1, 2):
        pairs += [(i, i + 1), (i + 1, i)]
    return pairs


def body(
    earlier_warmth_field,
    caloric_storage,
    thermal_diffusivity_coefficient,
    dissipation_catalog,
    dissipation_selector,
    refine_depth,
    border_band_width,
    microflow_flag,
):
    z, y, x = earlier_warmth_field.shape
    tall = dissipation_catalog.shape[1]
    groups = -(-(z * y // 8) // 128)
    rounds = tuple(2 if lax.axis_size(axis) > 2 else 1 for axis in GRID_AXES)
    sends = sum(rounds)
    shape = lambda *s: pltpu.VMEM(s, F32)
    full = shape(z, y, x)
    tall_field = shape(z, y + 16, x)

    def outside(v):
        return pltpu.with_memory_space_constraint(v, pltpu.HBM)

    def call(kernel, outs, ins, name, scratch=(), specs=None, out_specs=None, alias=None):
        specs = specs or [SMEM if v.dtype == jnp.int32 else VMEM for v in ins]
        return pl.pallas_call(
            kernel,
            out_shape=outs,
            in_specs=specs,
            out_specs=out_specs or [VMEM] * len(outs),
            scratch_shapes=list(scratch),
            input_output_aliases=alias or {},
            name=name,
            compiler_params=pltpu.CompilerParams(vmem_limit_bytes=16 * 2**20),
        )(*ins)

    def face_shapes(front):
        out = []
        for axis, n in zip(((8 * groups, x), (z, x), (y, x)), rounds):
            out += [shape(*front, *axis)] * n
        return out

    def swap(faces):
        faces, got = list(faces), []
        for axis, n in zip(GRID_AXES, rounds):
            for start in range(n):
                got.append(lax.ppermute(faces.pop(0), axis, swap_pairs(axis, start)))
        return got

    tables = [
        jnp.swapaxes(dissipation_selector, 1, 2),
        jnp.swapaxes(refine_depth, 1, 2),
        jnp.swapaxes(border_band_width, 0, 1),
        microflow_flag,
    ]
    hbm = pl.BlockSpec(memory_space=pltpu.HBM)
    outs = call(
        functools.partial(faces_kernel, rounds),
        [tall_field, tall_field]
        + [pltpu.VMEM(t.shape, t.dtype) for t in tables]
        + face_shapes((2,))
        + [shape(2, 2, 8 * groups, x)],
        [outside(v) for v in (earlier_warmth_field, thermal_diffusivity_coefficient, *tables)],
        "faces",
        [pltpu.SemaphoreType.DMA((6,))],
        [hbm] * 6,
    )
    (field, kappa, selector, levels, width, flow), outs = outs[:6], outs[6:]
    own, halos = outs[sends], swap(outs[:sends])
    r, diag, cz, cs, ce = call(
        functools.partial(inner_kernel, tall),
        [full, full, shape(max(z - 1, 1), y, x), shape(z, y + 8, x), full],
        [field, kappa, outside(caloric_storage), outside(dissipation_catalog), selector, width, flow],
        "inner",
        [full, shape(*dissipation_catalog.shape), pltpu.SemaphoreType.DMA((2,))],
        [VMEM, VMEM, hbm, hbm, SMEM, SMEM, SMEM],
    )
    outs = call(
        functools.partial(border_kernel, rounds, tall),
        [full, full, tall_field, shape(2, 8 * groups, x), shape(rounds[1], z, 8, x), shape(rounds[2], y, x)]
        + face_shapes(()),
        [field, kappa, own, r, diag, cs, ce, levels] + halos,
        "border",
        alias={3: 0, 4: 1},
    )
    r, diag, u, cx, cy, czh = outs[:6]
    halos = swap(outs[6:])
    (w,) = call(functools.partial(apply_kernel, tall), [full], [u, diag, cz, cs, ce], "apply")
    outs = call(
        functools.partial(smooth_kernel, rounds, tall),
        [full, tall_field] + face_shapes(()),
        [w, diag, cs, ce, cx, cy, czh, levels] + halos,
        "smooth",
        alias={0: 0},
    )
    w, m = outs[:2]
    halos = swap(outs[2:])
    n, sums = call(
        functools.partial(sums_kernel, tall), [full, shape(3, 8, 128)], [m, u, r, w, diag, cz, cs, ce], "sums"
    )
    members = math.prod(lax.axis_size(axis) for axis in GRID_AXES)
    n, parts = call(
        functools.partial(finish_kernel, rounds),
        [full, shape(members, 4, 128)],
        [n, m, sums, cx, cy, czh] + halos,
        "finish",
        alias={0: 0},
    )
    every = lax.all_to_all(parts, GRID_AXES, 0, 0, tiled=True)
    return tuple(
        call(
            update_kernel,
            [jax.ShapeDtypeStruct((z, y, x), F32)] * 2,
            [every, field, r, u, w, m, n],
            "update",
            [full, full, pltpu.SemaphoreType.DMA((z, 2))],
            out_specs=[hbm, hbm],
        )
    )


def solution(mesh):
    cells = P(("groups", "gz"), "gy", "gx")
    return jax.shard_map(
        body,
        mesh=mesh,
        in_specs=(
            cells,
            cells,
            cells,
            P("groups", None, None),
            cells,
            cells,
            P(("groups", "gy"), "gx"),
            P(("groups", "gz")),
        ),
        out_specs=(cells, cells),
        check_vma=False,
    )
```

time: 203 us -> 43.9 us (0.22)
  waiting for transfers between devices: 54.7 us -> 2.87 us
  blocking collectives: 60.5 us -> 12.1 us
  starting transfers between devices: 49.4 us -> 14.4 us
  other arithmetic: 23.4 us -> 0 us
  Pallas kernels: 0 us -> 13 us
  local copies, waits for them, and re-layouts: 7.08 us -> 0 us
  between operations: 6.83 us -> 0.75 us
    psum x2 -> x0, blocking collectives: 60.5 us -> none  [body(): lax.psum((jnp.sum(leftover_misfit * smoothed), jnp.sum(applied * smoothed...]
    ppermute x24 -> x12, waiting for transfers between devices: 54.7 us -> 2.87 us  [swap(): got.append(lax.ppermute(faces.pop(0), axis, swap_pairs(axis, start)))]
    ppermute x24 -> x12, starting transfers between devices: 49.4 us -> 14.4 us  [swap(): got.append(lax.ppermute(faces.pop(0), axis, swap_pairs(axis, start)))]
    pallas_call x0 -> x8, Pallas kernels: none -> 13 us  [call(): pl.pallas_call(kernel, out_shape=outs, in_specs=specs, out_specs=out_spec...]
    all_to_all x0 -> x1, blocking collectives: none -> 12.1 us  [body(): every = lax.all_to_all(parts, GRID_AXES, 0, 0, tiled=True)]
    div x2 -> x0, other arithmetic: 7.15 us -> none  [smooth(): state = damping * vector / diagonal]
    reduce_sum x2 -> x0, other arithmetic: 4.26 us -> none  [body(): jnp.sum(applied * smoothed)]
    slice x4 -> x0, local copies, waits for them, and re-layouts: 3.9 us -> none  [with_halo(): last = lax.slice_in_dim(shard, length - width, length, axis=dim)]
  transfers between devices with their start and end apart: 24 -> 12, of which waited for: 13 -> 2; matrix products, arithmetic and copies ran while one was open for 2% -> 0% of each run, Pallas kernels for 0% -> 9%
where the time goes in v3:
time: 43.9 us; the launch traced here: 43.2 us
  starting transfers between devices  14.4 us (33%)
  Pallas kernels  13 us (30%)
  blocking collectives  12.1 us (28%)
  waiting for transfers between devices  2.87 us (7%)
  between operations  0.75 us (2%)
    ppermute x12, starting transfers between devices, swap(): got.append(lax.ppermute(faces.pop(0), axis, swap_pairs(axis, start)))  14.4 us
    pallas_call x8, Pallas kernels, call(): pl.pallas_call(kernel, out_shape=outs, in_specs=specs, out_specs=out_spec...  13 us
    all_to_all x1, blocking collectives, body(): every = lax.all_to_all(parts, GRID_AXES, 0, 0, tiled=True)  12.1 us
    ppermute x12, waiting for transfers between devices, swap(): got.append(lax.ppermute(faces.pop(0), axis, swap_pairs(axis, start)))  2.87 us
  transfers between devices with their start and end apart: 12, of which 2 were waited for; matrix products, arithmetic and copies ran while one was open for 0% of the time, Pallas kernels for 9%

profile of v3, /device:TPU:0, one launch (start us, length us, event | category | flops | bytes accessed | tf_op | source)
XLA Modules:
  0.0 43.2 jit_solution(2824187998934056302)
XLA Ops:
  0.6 1.7 %faces.1 = (f32[4,272,128]{2,1,0:T(8,128)S(1)}, f32[4,272,128]{2,1,0:T(8,128)S(1)}, s32[4,1,4]{2,1,0:T(1,128)S(1)}, s32[4,1,4]{2,1,0:T(1,128)S(1)}, s32[1,4]{1,0...) custom-call(f32[4,256,128]{2,1,0:T(8,128)} %x_in.1, ...), custom_call_target="tpu_custom_call" | custom-call | tf_op jit(solution)/shard_map/faces/pallas_call | solution.py:471
  2.3 0.6 %collective-permute-start.3 = (f32[2,256,128]{2,1,0:T(8,128)S(1)}, f32[2,256,128]{2,1,0:T(8,128)S(1)}, u32[]{:S(2)}, u32[]{:S(2)}) collective-permute-start(f32[2,256,128]{2,1,0:T(8,128)S(1)} %get-tuple-element.52), channel_id=1, source_target_pairs={{0,1},{1,0},{2,3},{3,2},{4,5},{5,4},{6,7},{7,6},{8,9},{9,8},{10,11... | collective-permute-start | bytes 786440 | tf_op jit(solution)/shard_map/ppermute | solution.py:492
  2.9 2.6 %collective-permute-start = (f32[2,8,128]{2,1,0:T(8,128)S(1)}, f32[2,8,128]{2,1,0:T(8,128)S(1)}, u32[]{:S(2)}, u32[]{:S(2)}) collective-permute-start(f32[2,8,128]{2,1,0:T(8,128)S(1)} %get-tuple-element.49), channel_id=1, source_target_pairs={{0,4},{4,0},{8,12},{12,8},{1,5},{5,1},{9,13},{13,9},{2,6},{6,2},{1... | collective-permute-start | bytes 24584 | tf_op jit(solution)/shard_map/ppermute | solution.py:492
  5.5 0.6 %collective-permute-start.1 = (f32[2,8,128]{2,1,0:T(8,128)S(1)}, f32[2,8,128]{2,1,0:T(8,128)S(1)}, u32[]{:S(2)}, u32[]{:S(2)}) collective-permute-start(f32[2,8,128]{2,1,0:T(8,128)S(1)} %get-tuple-element.50), channel_id=1, source_target_pairs={{4,8},{8,4},{5,9},{9,5},{6,10},{10,6},{7,11},{11,7},{20,24},{24,20... | collective-permute-start | bytes 24584 | tf_op jit(solution)/shard_map/ppermute | solution.py:492
  6.2 1.6 %collective-permute-start.2 = (f32[2,4,128]{2,1,0:T(4,128)S(1)}, f32[2,4,128]{2,1,0:T(4,128)S(1)}, u32[]{:S(2)}, u32[]{:S(2)}) collective-permute-start(f32[2,4,128]{2,1,0:T(4,128)S(1)} %get-tuple-element.51), channel_id=1, source_target_pairs={{0,2},{2,0},{1,3},{3,1},{4,6},{6,4},{5,7},{7,5},{8,10},{10,8},{9,1... | collective-permute-start | bytes 12296 | tf_op jit(solution)/shard_map/ppermute | solution.py:492
  7.7 2.6 %inner.1 = (f32[4,256,128]{2,1,0:T(8,128)S(1)}, f32[4,256,128]{2,1,0:T(8,128)S(1)}, f32[3,256,128]{2,1,0:T(8,128)S(1)}, f32[4,264,128]{2,1,0:T(8,128)S(1)}, f32[4,256,128]{2,1,0:T(8,128)S(1)}) custom-call(f32[4,272,128]{2,1,0:T(8,128)S(1)} %get-tuple-element.38.x_ref.refs_0_, f32[4,272,128]{2,1,0:T(8,128)S(1)} %get-tuple-element.39.k_ref.refs_1_, ...), custom_call_target="tpu_custom_call" | custom-call | tf_op jit(solution)/shard_map/inner/pallas_call | solution.py:471
  10.3 0.0 collective-permute-done.2.refs_10_
  10.3 0.0 collective-permute-done.refs_8_
  10.3 0.0 collective-permute-done.1.refs_9_
  10.3 0.0 collective-permute-done.3.refs_11_
  10.3 3.1 %border.1 = (f32[4,256,128]{2,1,0:T(8,128)S(1)}, f32[4,256,128]{2,1,0:T(8,128)S(1)}, f32[4,272,128]{2,1,0:T(8,128)S(1)}, f32[2,8,128]{2,1,0:T(8,128)S(1)}, f32[1...) custom-call(f32[4,272,128]{2,1,0:T(8,128)S(1)} %get-tuple-element.38, ...), custom_call_target="tpu_custom_call", output_to_operand_aliasing={{0}: (3, {}), {1}: (4, {})} | custom-call | tf_op jit(solution)/shard_map/border/pallas_call | solution.py:471
  13.4 0.0 collective-permute-start.7
  13.4 3.8 %collective-permute-start.4 = (f32[8,128]{1,0:T(8,128)S(1)}, f32[8,128]{1,0:T(8,128)S(1)}, u32[]{:S(2)}, u32[]{:S(2)}) collective-permute-start(f32[8,128]{1,0:T(8,128)S(1)} %get-tuple-element.59), channel_id=1, source_target_pairs={{0,4},{4,0},{8,12},{12,8},{1,5},{5,1},{9,13},{13,9},{2,6},{6,2},{1... | collective-permute-start | bytes 12296 | tf_op jit(solution)/shard_map/ppermute | solution.py:492
  17.2 0.6 %collective-permute-start.5 = (f32[8,128]{1,0:T(8,128)S(1)}, f32[8,128]{1,0:T(8,128)S(1)}, u32[]{:S(2)}, u32[]{:S(2)}) collective-permute-start(f32[8,128]{1,0:T(8,128)S(1)} %get-tuple-element.60), channel_id=1, source_target_pairs={{4,8},{8,4},{5,9},{9,5},{6,10},{10,6},{7,11},{11,7},{20,24},{24,20... | collective-permute-start | bytes 12296 | tf_op jit(solution)/shard_map/ppermute | solution.py:492
  17.8 1.5 %collective-permute-start.6 = (f32[4,128]{1,0:T(4,128)S(1)}, f32[4,128]{1,0:T(4,128)S(1)}, u32[]{:S(2)}, u32[]{:S(2)}) collective-permute-start(f32[4,128]{1,0:T(4,128)S(1)} %get-tuple-element.61), channel_id=1, source_target_pairs={{0,2},{2,0},{1,3},{3,1},{4,6},{6,4},{5,7},{7,5},{8,10},{10,8},{9,1... | collective-permute-start | bytes 6152 | tf_op jit(solution)/shard_map/ppermute | solution.py:492
  19.3 0.6 %apply.1.refs_0_ = f32[4,256,128]{2,1,0:T(8,128)S(1)} custom-call(f32[4,272,128]{2,1,0:T(8,128)S(1)} %get-tuple-element.53.u_ref, f32[4,256,128]{2,1,0:T(8,128)S(1)} %get-tuple-element.54.diag_ref.refs_1_, f32[3,256,128]{2,1,0:T(8,128)S(1)} %get-tuple-element.55.cz_ref, f32[4,264,128]{2,1,0:T(8,128)S(1)} %get-tuple-element.46.refs_5_.cs_ref.refs_2_, ...), custom_call_target="tpu_custom_call" | custom-call | tf_op jit(solution)/shard_map/apply/pallas_call | solution.py:471
  19.9 1.6 %collective-permute-done.6.refs_10_ = f32[4,128]{1,0:T(4,128)S(1)} collective-permute-done((f32[4,128]{1,0:T(4,128)S(1)}, f32[4,128]{1,0:T(4,128)S(1)}, u32[]{:S(2)}, u32[]{:S(2)}) %collective-permute-start.6) | collective-permute-done | bytes 2080 | tf_op jit(solution)/shard_map/ppermute | solution.py:492
  21.5 0.0 collective-permute-done.4.refs_8_
  21.5 0.0 collective-permute-done.5.refs_9_
  21.5 0.0 collective-permute-done.7.refs_11_
  21.5 2.8 %smooth.1 = (f32[4,256,128]{2,1,0:T(8,128)S(1)}, f32[4,272,128]{2,1,0:T(8,128)S(1)}, f32[8,128]{1,0:T(8,128)S(1)}, f32[8,128]{1,0:T(8,128)S(1)}, f32[4,128]{1,0:T(4,128)S(1)}, /*index=5*/f32[256,128]{1,0:T(8,128)S(1)}) custom-call(f32[4,256,128]{2,1,0:T(8,128)S(1)} %apply.1.refs_0_, ...), custom_call_target="tpu_custom_call", output_to_operand_aliasing={{0}: (0, {})} | custom-call | tf_op jit(solution)/shard_map/smooth/pallas_call | solution.py:471
  24.2 0.0 collective-permute-start.11
  24.3 0.7 %collective-permute-start.8 = (f32[8,128]{1,0:T(8,128)S(1)}, f32[8,128]{1,0:T(8,128)S(1)}, u32[]{:S(2)}, u32[]{:S(2)}) collective-permute-start(f32[8,128]{1,0:T(8,128)S(1)} %get-tuple-element.68), channel_id=1, source_target_pairs={{0,4},{4,0},{8,12},{12,8},{1,5},{5,1},{9,13},{13,9},{2,6},{6,2},{1... | collective-permute-start | bytes 12296 | tf_op jit(solution)/shard_map/ppermute | solution.py:492
  25.0 0.6 %collective-permute-start.9 = (f32[8,128]{1,0:T(8,128)S(1)}, f32[8,128]{1,0:T(8,128)S(1)}, u32[]{:S(2)}, u32[]{:S(2)}) collective-permute-start(f32[8,128]{1,0:T(8,128)S(1)} %get-tuple-element.69), channel_id=1, source_target_pairs={{4,8},{8,4},{5,9},{9,5},{6,10},{10,6},{7,11},{11,7},{20,24},{24,20... | collective-permute-start | bytes 12296 | tf_op jit(solution)/shard_map/ppermute | solution.py:492
  25.6 1.8 %collective-permute-start.10 = (f32[4,128]{1,0:T(4,128)S(1)}, f32[4,128]{1,0:T(4,128)S(1)}, u32[]{:S(2)}, u32[]{:S(2)}) collective-permute-start(f32[4,128]{1,0:T(4,128)S(1)} %get-tuple-element.70), channel_id=1, source_target_pairs={{0,2},{2,0},{1,3},{3,1},{4,6},{6,4},{5,7},{7,5},{8,10},{10,8},{9,1... | collective-permute-start | bytes 6152 | tf_op jit(solution)/shard_map/ppermute | solution.py:492
  27.4 0.6 %sums.1 = (f32[4,256,128]{2,1,0:T(8,128)S(1)}, f32[3,8,128]{2,1,0:T(8,128)S(1)}) custom-call(f32[4,272,128]{2,1,0:T(8,128)S(1)} %get-tuple-element.63.m_ref.refs_1_, f32[4,272,128]{2,1,0:T(8,128)S(1)} %get-tuple-element.53.u_ref, f32[4,256,128]{2,1,0:T(8,128)S(1)} %get-tuple-element.64.r_ref, f32[4,256,128]{2,1,0:T(8,128)S(1)} %get-tuple-element.65.w_ref, ...), custom_call_target="tpu_custom_call" | custom-call | tf_op jit(solution)/shard_map/sums/pallas_call | solution.py:471
  28.1 1.2 %collective-permute-done.10.refs_8_ = f32[4,128]{1,0:T(4,128)S(1)} collective-permute-done((f32[4,128]{1,0:T(4,128)S(1)}, f32[4,128]{1,0:T(4,128)S(1)}, u32[]{:S(2)}, u32[]{:S(2)}) %collective-permute-start.10) | collective-permute-done | bytes 2080 | tf_op jit(solution)/shard_map/ppermute | solution.py:492
  29.3 0.0 collective-permute-done.8.refs_6_
  29.3 0.0 collective-permute-done.9.refs_7_
  29.3 0.0 collective-permute-done.11.refs_9_
  29.3 0.4 finish.1
  29.7 12.1 %all_to_all.5.all_ref = f32[16,4,128]{2,1,0:T(4,128)S(1)} all-to-all(f32[16,4,128]{2,1,0:T(4,128)S(1)} %get-tuple-element.72), channel_id=1, replica_groups=mesh['groups'=2,'gx'=4,'gy'=2,'gz'=2] {'gx','gy','gz'}, dimensions={0} | all-to-all | bytes 65536 | tf_op jit(solution)/shard_map/all_to_all | solution.py:554
  41.8 1.3 %update.1 = (f32[4,256,128]{2,1,0:T(8,128)}, f32[4,256,128]{2,1,0:T(8,128)}) custom-call(f32[16,4,128]{2,1,0:T(4,128)S(1)} %all_to_all.5.all_ref, f32[4,272,128]{2,1,0:T(8,128)S(1)} %get-tuple-element.38.x_ref.refs_0_, f32[4,256,128]{2,1,0:T(8,128)S(1)} %get-tuple-element.64.r_ref, f32[4,272,128]{2,1,0:T(8,128)S(1)} %get-tuple-element.53.u_ref, ...), custom_call_target="tpu_custom_call" | custom-call | tf_op jit(solution)/shard_map/update/pallas_call | solution.py:471
Async XLA Ops:
  2.3 8.0 %collective-permute-start.3 = (f32[2,256,128]{2,1,0:T(8,128)S(1)}, f32[2,256,128]{2,1,0:T(8,128)S(1)}, u32[]{:S(2)}, u32[]{:S(2)}) collective-permute-start(f32[2,256,128]{2,1,0:T(8,128)S(1)} %get-tuple-element.52), channel_id=1, source_target_pairs={{0,1},{1,0},{2,3},{3,2},{4,5},{5,4},{6,7},{7,6},{8,9},{9,8},{10,11... | collective-permute-start | bytes 786440 | tf_op jit(solution)/shard_map/ppermute | solution.py:492
  2.9 7.4 %collective-permute-start = (f32[2,8,128]{2,1,0:T(8,128)S(1)}, f32[2,8,128]{2,1,0:T(8,128)S(1)}, u32[]{:S(2)}, u32[]{:S(2)}) collective-permute-start(f32[2,8,128]{2,1,0:T(8,128)S(1)} %get-tuple-element.49), channel_id=1, source_target_pairs={{0,4},{4,0},{8,12},{12,8},{1,5},{5,1},{9,13},{13,9},{2,6},{6,2},{1... | collective-permute-start | bytes 24584 | tf_op jit(solution)/shard_map/ppermute | solution.py:492
  5.5 4.8 %collective-permute-start.1 = (f32[2,8,128]{2,1,0:T(8,128)S(1)}, f32[2,8,128]{2,1,0:T(8,128)S(1)}, u32[]{:S(2)}, u32[]{:S(2)}) collective-permute-start(f32[2,8,128]{2,1,0:T(8,128)S(1)} %get-tuple-element.50), channel_id=1, source_target_pairs={{4,8},{8,4},{5,9},{9,5},{6,10},{10,6},{7,11},{11,7},{20,24},{24,20... | collective-permute-start | bytes 24584 | tf_op jit(solution)/shard_map/ppermute | solution.py:492
  6.2 4.1 %collective-permute-start.2 = (f32[2,4,128]{2,1,0:T(4,128)S(1)}, f32[2,4,128]{2,1,0:T(4,128)S(1)}, u32[]{:S(2)}, u32[]{:S(2)}) collective-permute-start(f32[2,4,128]{2,1,0:T(4,128)S(1)} %get-tuple-element.51), channel_id=1, source_target_pairs={{0,2},{2,0},{1,3},{3,1},{4,6},{6,4},{5,7},{7,5},{8,10},{10,8},{9,1... | collective-permute-start | bytes 12296 | tf_op jit(solution)/shard_map/ppermute | solution.py:492
  13.4 8.1 %collective-permute-start.7 = (f32[256,128]{1,0:T(8,128)S(1)}, f32[256,128]{1,0:T(8,128)S(1)}, u32[]{:S(2)}, u32[]{:S(2)}) collective-permute-start(f32[256,128]{1,0:T(8,128)S(1)} %get-tuple-element.62), channel_id=1, source_target_pairs={{0,1},{1,0},{2,3},{3,2},{4,5},{5,4},{6,7},{7,6},{8,9},{9,8},{10,11... | collective-permute-start | bytes 393224 | tf_op jit(solution)/shard_map/ppermute | solution.py:492
  13.4 8.1 %collective-permute-start.4 = (f32[8,128]{1,0:T(8,128)S(1)}, f32[8,128]{1,0:T(8,128)S(1)}, u32[]{:S(2)}, u32[]{:S(2)}) collective-permute-start(f32[8,128]{1,0:T(8,128)S(1)} %get-tuple-element.59), channel_id=1, source_target_pairs={{0,4},{4,0},{8,12},{12,8},{1,5},{5,1},{9,13},{13,9},{2,6},{6,2},{1... | collective-permute-start | bytes 12296 | tf_op jit(solution)/shard_map/ppermute | solution.py:492
  17.2 4.3 %collective-permute-start.5 = (f32[8,128]{1,0:T(8,128)S(1)}, f32[8,128]{1,0:T(8,128)S(1)}, u32[]{:S(2)}, u32[]{:S(2)}) collective-permute-start(f32[8,128]{1,0:T(8,128)S(1)} %get-tuple-element.60), channel_id=1, source_target_pairs={{4,8},{8,4},{5,9},{9,5},{6,10},{10,6},{7,11},{11,7},{20,24},{24,20... | collective-permute-start | bytes 12296 | tf_op jit(solution)/shard_map/ppermute | solution.py:492
  17.8 3.7 %collective-permute-start.6 = (f32[4,128]{1,0:T(4,128)S(1)}, f32[4,128]{1,0:T(4,128)S(1)}, u32[]{:S(2)}, u32[]{:S(2)}) collective-permute-start(f32[4,128]{1,0:T(4,128)S(1)} %get-tuple-element.61), channel_id=1, source_target_pairs={{0,2},{2,0},{1,3},{3,1},{4,6},{6,4},{5,7},{7,5},{8,10},{10,8},{9,1... | collective-permute-start | bytes 6152 | tf_op jit(solution)/shard_map/ppermute | solution.py:492
  24.2 5.1 %collective-permute-start.11 = (f32[256,128]{1,0:T(8,128)S(1)}, f32[256,128]{1,0:T(8,128)S(1)}, u32[]{:S(2)}, u32[]{:S(2)}) collective-permute-start(f32[256,128]{1,0:T(8,128)S(1)} %get-tuple-element.71), channel_id=1, source_target_pairs={{0,1},{1,0},{2,3},{3,2},{4,5},{5,4},{6,7},{7,6},{8,9},{9,8},{10,11... | collective-permute-start | bytes 393224 | tf_op jit(solution)/shard_map/ppermute | solution.py:492
  24.3 5.0 %collective-permute-start.8 = (f32[8,128]{1,0:T(8,128)S(1)}, f32[8,128]{1,0:T(8,128)S(1)}, u32[]{:S(2)}, u32[]{:S(2)}) collective-permute-start(f32[8,128]{1,0:T(8,128)S(1)} %get-tuple-element.68), channel_id=1, source_target_pairs={{0,4},{4,0},{8,12},{12,8},{1,5},{5,1},{9,13},{13,9},{2,6},{6,2},{1... | collective-permute-start | bytes 12296 | tf_op jit(solution)/shard_map/ppermute | solution.py:492
  25.0 4.3 %collective-permute-start.9 = (f32[8,128]{1,0:T(8,128)S(1)}, f32[8,128]{1,0:T(8,128)S(1)}, u32[]{:S(2)}, u32[]{:S(2)}) collective-permute-start(f32[8,128]{1,0:T(8,128)S(1)} %get-tuple-element.69), channel_id=1, source_target_pairs={{4,8},{8,4},{5,9},{9,5},{6,10},{10,6},{7,11},{11,7},{20,24},{24,20... | collective-permute-start | bytes 12296 | tf_op jit(solution)/shard_map/ppermute | solution.py:492
  25.6 3.7 %collective-permute-start.10 = (f32[4,128]{1,0:T(4,128)S(1)}, f32[4,128]{1,0:T(4,128)S(1)}, u32[]{:S(2)}, u32[]{:S(2)}) collective-permute-start(f32[4,128]{1,0:T(4,128)S(1)} %get-tuple-element.70), channel_id=1, source_target_pairs={{0,2},{2,0},{1,3},{3,1},{4,6},{6,4},{5,7},{7,5},{8,10},{10,8},{9,1... | collective-permute-start | bytes 6152 | tf_op jit(solution)/shard_map/ppermute | solution.py:492

commit v4 on v3

--- a/solution.py
+++ b/solution.py
@@ -15,7 +15,6 @@
 damping = 0.8
 GRID_AXES = ("gx", "gy", "gz")
 VMEM = pl.BlockSpec(memory_space=pltpu.VMEM)
-SMEM = pl.BlockSpec(memory_space=pltpu.SMEM)
 F32 = jnp.float32
 
 
@@ -136,32 +135,34 @@
     return copies
 
 
-def faces_kernel(rounds, x_in, k_in, sel_in, lev_in, band_in, flow_in, *refs):
-    (x_ref, k_ref, sel_ref, lev_ref, band_ref, flow_ref), refs = refs[:6], refs[6:]
+def faces_kernel(rounds, x_in, k_in, x_ref, k_ref, *refs):
     sends, (own_ref, sems) = regroup(refs, rounds)
     z, y, _ = x_in.shape
-    inner = pl.ds(8, y)
-    copies = start_all(
-        (x_in, k_in, sel_in, lev_in, band_in, flow_in),
-        (x_ref.at[:, inner, :], k_ref.at[:, inner, :], sel_ref, lev_ref, band_ref, flow_ref),
-        sems,
-    )
-    for slot, ref in enumerate((x_ref, k_ref)):
+    per = y // 8
+    fields = (x_ref, k_ref)
+    copies = [
+        start_all([source.at[i] for i in range(z)], [ref.at[i, pl.ds(8, y), :] for i in range(z)], sems.at[n])
+        for n, (source, ref) in enumerate(zip((x_in, k_in), fields))
+    ]
+    for slot, ref in enumerate(fields):
         clear_margins(ref)
-        copies[slot].wait()
         tier, row, vreg = padded_access(ref)
-        columns = pack_columns(vreg, z * y // 8)
+
+        def load(i):
+            if i % per == 0:
+                copies[slot][i // per].wait()
+            return vreg(i)
+
+        columns = pack_columns(load, z * per)
         own_ref[slot, 0] = columns[0]
         own_ref[slot, 1] = columns[1]
         fill_sends(tier, row, sends, slot, columns, z, y)
-    for copy in copies[2:]:
-        copy.wait()
-
-
-def inner_kernel(tall, x_ref, k_ref, c_in, cat_in, sel_ref, band_ref, flow_ref, *refs):
-    r_ref, diag_ref, cz_ref, cs_ref, ce_ref, c_ref, cat_ref, sems = refs
+
+
+def inner_kernel(tall, x_ref, k_ref, c_ref, cat_ref, sel_in, band_in, flow_in, *refs):
+    r_ref, diag_ref, cz_ref, cs_ref, ce_ref, sel_ref, band_ref, flow_ref, sems = refs
     z, y, _ = c_ref.shape
-    copies = start_all((c_in, cat_in), (c_ref, cat_ref), sems)
+    copies = start_all((sel_in, band_in, flow_in), (sel_ref, band_ref, flow_ref), sems)
     lane = lanes((tall, 128))
     row = rows((tall, 128))
     for i in range(z):
@@ -253,11 +254,12 @@
 
 
 def border_kernel(rounds, tall, *refs):
-    (x_ref, k_ref, own_ref, r_in, diag_in, cs_ref, ce_ref, lev_ref), refs = refs[:8], refs[8:]
+    (x_ref, k_ref, own_ref, r_in, diag_in, cs_ref, ce_ref, lev_in), refs = refs[:8], refs[8:]
     (hx, hy, hz), refs = regroup(refs, rounds)
     (r_ref, diag_ref, u_ref, cx_ref, cy_ref, czh_ref), refs = refs[:6], refs[6:]
-    sends, _ = regroup(refs, rounds)
+    sends, (lev_ref, sems) = regroup(refs, rounds)
     z, y, _ = r_ref.shape
+    table = start_all((lev_in,), (lev_ref,), sems)
     for n, ref in enumerate(hz):
         p = jnp.where(low_side("gz", n), 0, z - 1)
         face = vertical_ratio * harmonic(k_ref[p, pl.ds(8, y), :], ref[1])
@@ -295,6 +297,7 @@
         diag_ref[at] = diag
         r_ref[at] = r
         u_ref[i // per, 8 + 8 * (i % per) : 16 + 8 * (i % per)] = r * (damping / diag)
+    table[0].wait()
     sweeps(u_ref, diag_ref, cs_ref, ce_ref, lev_ref, tall)
     tier, row, vreg = padded_access(u_ref)
     fill_sends(tier, row, sends, None, pack_columns(vreg, z * per), z, y)
@@ -341,11 +344,12 @@
 
 
 def smooth_kernel(rounds, tall, *refs):
-    (w_in, diag_ref, cs_ref, ce_ref, cx_ref, cy_ref, czh_ref, lev_ref), refs = refs[:8], refs[8:]
+    (w_in, diag_ref, cs_ref, ce_ref, cx_ref, cy_ref, czh_ref, lev_in), refs = refs[:8], refs[8:]
     halos, refs = regroup(refs, rounds)
     (w_ref, m_ref), refs = refs[:2], refs[2:]
-    sends, _ = regroup(refs, rounds)
+    sends, (lev_ref, sems) = regroup(refs, rounds)
     z, y, _ = w_ref.shape
+    table = start_all((lev_in,), (lev_ref,), sems)
     subtract_halos(w_in, halos, cy_ref, czh_ref)
     xlo, xhi = column_halos(halos[0])
     flux = stage_columns(cx_ref[0] * xlo, cx_ref[1] * xhi)
@@ -357,6 +361,7 @@
         w = w_in[at] - spread_columns(flux, edge, i)
         w_ref[at] = w
         m_ref[i // per, 8 + 8 * (i % per) : 16 + 8 * (i % per)] = w * (damping / diag_ref[at])
+    table[0].wait()
     sweeps(m_ref, diag_ref, cs_ref, ce_ref, lev_ref, tall)
     tier, row, vreg = padded_access(m_ref)
     fill_sends(tier, row, sends, None, pack_columns(vreg, z * per), z, y)
@@ -463,11 +468,11 @@
     full = shape(z, y, x)
     tall_field = shape(z, y + 16, x)
 
-    def outside(v):
-        return pltpu.with_memory_space_constraint(v, pltpu.HBM)
-
-    def call(kernel, outs, ins, name, scratch=(), specs=None, out_specs=None, alias=None):
-        specs = specs or [SMEM if v.dtype == jnp.int32 else VMEM for v in ins]
+    hbm = pl.BlockSpec(memory_space=pltpu.HBM)
+
+    def call(kernel, outs, ins, name, scratch=(), out_specs=None, alias=None, outer=()):
+        specs = [hbm if n in outer else VMEM for n in range(len(ins))]
+        ins = [pltpu.with_memory_space_constraint(v, pltpu.HBM) if n in outer else v for n, v in enumerate(ins)]
         return pl.pallas_call(
             kernel,
             out_shape=outs,
@@ -492,33 +497,30 @@
                 got.append(lax.ppermute(faces.pop(0), axis, swap_pairs(axis, start)))
         return got
 
-    tables = [
-        jnp.swapaxes(dissipation_selector, 1, 2),
-        jnp.swapaxes(refine_depth, 1, 2),
-        jnp.swapaxes(border_band_width, 0, 1),
-        microflow_flag,
-    ]
-    hbm = pl.BlockSpec(memory_space=pltpu.HBM)
+    selector = jnp.swapaxes(dissipation_selector, 1, 2)
+    levels = jnp.swapaxes(refine_depth, 1, 2)
+    width = jnp.swapaxes(border_band_width, 0, 1)
+
+    def table(v):
+        return pltpu.SMEM(v.shape, v.dtype)
+
     outs = call(
         functools.partial(faces_kernel, rounds),
-        [tall_field, tall_field]
-        + [pltpu.VMEM(t.shape, t.dtype) for t in tables]
-        + face_shapes((2,))
-        + [shape(2, 2, 8 * groups, x)],
-        [outside(v) for v in (earlier_warmth_field, thermal_diffusivity_coefficient, *tables)],
+        [tall_field, tall_field] + face_shapes((2,)) + [shape(2, 2, 8 * groups, x)],
+        [earlier_warmth_field, thermal_diffusivity_coefficient],
         "faces",
-        [pltpu.SemaphoreType.DMA((6,))],
-        [hbm] * 6,
-    )
-    (field, kappa, selector, levels, width, flow), outs = outs[:6], outs[6:]
+        [pltpu.SemaphoreType.DMA((2, z))],
+        outer=(0, 1),
+    )
+    (field, kappa), outs = outs[:2], outs[2:]
     own, halos = outs[sends], swap(outs[:sends])
     r, diag, cz, cs, ce = call(
         functools.partial(inner_kernel, tall),
         [full, full, shape(max(z - 1, 1), y, x), shape(z, y + 8, x), full],
-        [field, kappa, outside(caloric_storage), outside(dissipation_catalog), selector, width, flow],
+        [field, kappa, caloric_storage, dissipation_catalog, selector, width, microflow_flag],
         "inner",
-        [full, shape(*dissipation_catalog.shape), pltpu.SemaphoreType.DMA((2,))],
-        [VMEM, VMEM, hbm, hbm, SMEM, SMEM, SMEM],
+        [table(selector), table(width), table(microflow_flag), pltpu.SemaphoreType.DMA((3,))],
+        outer=(4, 5, 6),
     )
     outs = call(
         functools.partial(border_kernel, rounds, tall),
@@ -526,7 +528,9 @@
         + face_shapes(()),
         [field, kappa, own, r, diag, cs, ce, levels] + halos,
         "border",
+        [table(levels), pltpu.SemaphoreType.DMA((1,))],
         alias={3: 0, 4: 1},
+        outer=(7,),
     )
     r, diag, u, cx, cy, czh = outs[:6]
     halos = swap(outs[6:])
@@ -536,7 +540,9 @@
         [full, tall_field] + face_shapes(()),
         [w, diag, cs, ce, cx, cy, czh, levels] + halos,
         "smooth",
+        [table(levels), pltpu.SemaphoreType.DMA((1,))],
         alias={0: 0},
+        outer=(7,),
     )
     w, m = outs[:2]
     halos = swap(outs[2:])

time: 43.9 us -> 44.2 us (level)
  Pallas kernels: 13 us -> 11.4 us
  starting transfers between devices: 14.4 us -> 15.9 us
  blocking collectives: 12.1 us -> 12.7 us
    pallas_call x8, Pallas kernels: 13 us -> 11.4 us  [call(): pl.pallas_call(kernel, out_shape=outs, in_specs=specs, out_specs=out_spec...]
    ppermute x12, starting transfers between devices: 14.4 us -> 15.9 us  [swap(): got.append(lax.ppermute(faces.pop(0), axis, swap_pairs(axis, start)))]
    all_to_all x1, blocking collectives: 12.1 us -> 12.7 us  [body(): every = lax.all_to_all(parts, GRID_AXES, 0, 0, tiled=True)]
  transfers between devices with their start and end apart: 12 -> 12, of which waited for: 2 -> 3; matrix products, arithmetic and copies ran while one was open for 0% -> 0% of each run, Pallas kernels for 9% -> 6%
where the time goes in v4:
time: 44.2 us; the launch traced here: 43.9 us
  starting transfers between devices  15.9 us (36%)
  blocking collectives  12.7 us (29%)
  Pallas kernels  11.4 us (26%)
  waiting for transfers between devices  3 us (7%)
  between operations  0.76 us (2%)
    ppermute x12, starting transfers between devices, swap(): got.append(lax.ppermute(faces.pop(0), axis, swap_pairs(axis, start)))  15.9 us
    all_to_all x1, blocking collectives, body(): every = lax.all_to_all(parts, GRID_AXES, 0, 0, tiled=True)  12.7 us
    pallas_call x8, Pallas kernels, call(): pl.pallas_call(kernel, out_shape=outs, in_specs=specs, out_specs=out_spec...  11.4 us
    ppermute x12, waiting for transfers between devices, swap(): got.append(lax.ppermute(faces.pop(0), axis, swap_pairs(axis, start)))  3 us
  transfers between devices with their start and end apart: 12, of which 3 were waited for; matrix products, arithmetic and copies ran while one was open for 0% of the time, Pallas kernels for 6%

profile of v4, /device:TPU:0, one launch (start us, length us, event | category | flops | bytes accessed | tf_op | source)
XLA Modules:
  0.0 43.9 jit_solution(4166050900902867764)
XLA Ops:
  0.6 0.0 copy-start.1
  0.6 0.0 copy-start
  0.7 2.0 %faces.1 = (f32[4,272,128]{2,1,0:T(8,128)S(1)}, f32[4,272,128]{2,1,0:T(8,128)S(1)}, f32[2,8,128]{2,1,0:T(8,128)S(1)}, f32[2,8,128]{2,1,0:T(8,128)S(1)}, f32[2,4,...) custom-call(f32[4,256,128]{2,1,0:T(8,128)} %x_in.1, f32[4,256,128]{2,1,0:T(8,128)} %k_in.1), custom_call_target="tpu_custom_call" | custom-call | tf_op jit(solution)/shard_map/faces/pallas_call | solution.py:476
  2.7 0.6 %collective-permute-start.3 = (f32[2,256,128]{2,1,0:T(8,128)S(1)}, f32[2,256,128]{2,1,0:T(8,128)S(1)}, u32[]{:S(2)}, u32[]{:S(2)}) collective-permute-start(f32[2,256,128]{2,1,0:T(8,128)S(1)} %get-tuple-element.44), channel_id=1, source_target_pairs={{0,1},{1,0},{2,3},{3,2},{4,5},{5,4},{6,7},{7,6},{8,9},{9,8},{10,11... | collective-permute-start | bytes 786440 | tf_op jit(solution)/shard_map/ppermute | solution.py:497
  3.2 2.6 %collective-permute-start = (f32[2,8,128]{2,1,0:T(8,128)S(1)}, f32[2,8,128]{2,1,0:T(8,128)S(1)}, u32[]{:S(2)}, u32[]{:S(2)}) collective-permute-start(f32[2,8,128]{2,1,0:T(8,128)S(1)} %get-tuple-element.41), channel_id=1, source_target_pairs={{0,4},{4,0},{8,12},{12,8},{1,5},{5,1},{9,13},{13,9},{2,6},{6,2},{1... | collective-permute-start | bytes 24584 | tf_op jit(solution)/shard_map/ppermute | solution.py:497
  5.9 0.6 %collective-permute-start.1 = (f32[2,8,128]{2,1,0:T(8,128)S(1)}, f32[2,8,128]{2,1,0:T(8,128)S(1)}, u32[]{:S(2)}, u32[]{:S(2)}) collective-permute-start(f32[2,8,128]{2,1,0:T(8,128)S(1)} %get-tuple-element.42), channel_id=1, source_target_pairs={{4,8},{8,4},{5,9},{9,5},{6,10},{10,6},{7,11},{11,7},{20,24},{24,20... | collective-permute-start | bytes 24584 | tf_op jit(solution)/shard_map/ppermute | solution.py:497
  6.5 1.6 %collective-permute-start.2 = (f32[2,4,128]{2,1,0:T(4,128)S(1)}, f32[2,4,128]{2,1,0:T(4,128)S(1)}, u32[]{:S(2)}, u32[]{:S(2)}) collective-permute-start(f32[2,4,128]{2,1,0:T(4,128)S(1)} %get-tuple-element.43), channel_id=1, source_target_pairs={{0,2},{2,0},{1,3},{3,1},{4,6},{6,4},{5,7},{7,5},{8,10},{10,8},{9,1... | collective-permute-start | bytes 12296 | tf_op jit(solution)/shard_map/ppermute | solution.py:497
  8.1 0.0 copy-done.1
  8.1 0.0 copy-done
  8.1 1.5 %inner.1 = (f32[4,256,128]{2,1,0:T(8,128)S(1)}, f32[4,256,128]{2,1,0:T(8,128)S(1)}, f32[3,256,128]{2,1,0:T(8,128)S(1)}, f32[4,264,128]{2,1,0:T(8,128)S(1)}, f32[4,256,128]{2,1,0:T(8,128)S(1)}) custom-call(f32[4,272,128]{2,1,0:T(8,128)S(1)} %get-tuple-element.34.x_ref.refs_0_, f32[4,272,128]{2,1,0:T(8,128)S(1)} %get-tuple-element.35.k_ref.refs_1_, ...), custom_call_target="tpu_custom_call" | custom-call | tf_op jit(solution)/shard_map/inner/pallas_call | solution.py:476
  9.6 0.6 %collective-permute-done.2.refs_10_ = f32[2,4,128]{2,1,0:T(4,128)S(1)} collective-permute-done((f32[2,4,128]{2,1,0:T(4,128)S(1)}, f32[2,4,128]{2,1,0:T(4,128)S(1)}, u32[]{:S(2)}, u32[]{:S(2)}) %collective-permute-start.2) | collective-permute-done | bytes 4128 | tf_op jit(solution)/shard_map/ppermute | solution.py:497
  10.2 0.0 collective-permute-done.refs_8_
  10.2 0.0 collective-permute-done.1.refs_9_
  10.2 0.0 collective-permute-done.3.refs_11_
  10.2 2.6 %border.1 = (f32[4,256,128]{2,1,0:T(8,128)S(1)}, f32[4,256,128]{2,1,0:T(8,128)S(1)}, f32[4,272,128]{2,1,0:T(8,128)S(1)}, f32[2,8,128]{2,1,0:T(8,128)S(1)}, f32[1...) custom-call(f32[4,272,128]{2,1,0:T(8,128)S(1)} %get-tuple-element.34, ...), custom_call_target="tpu_custom_call", output_to_operand_aliasing={{0}: (3, {}), {1}: (4, {})} | custom-call | tf_op jit(solution)/shard_map/border/pallas_call | solution.py:476
  12.8 0.1 collective-permute-start.7
  12.9 4.1 %collective-permute-start.4 = (f32[8,128]{1,0:T(8,128)S(1)}, f32[8,128]{1,0:T(8,128)S(1)}, u32[]{:S(2)}, u32[]{:S(2)}) collective-permute-start(f32[8,128]{1,0:T(8,128)S(1)} %get-tuple-element.51), channel_id=1, source_target_pairs={{0,4},{4,0},{8,12},{12,8},{1,5},{5,1},{9,13},{13,9},{2,6},{6,2},{1... | collective-permute-start | bytes 12296 | tf_op jit(solution)/shard_map/ppermute | solution.py:497
  17.0 0.6 %collective-permute-start.5 = (f32[8,128]{1,0:T(8,128)S(1)}, f32[8,128]{1,0:T(8,128)S(1)}, u32[]{:S(2)}, u32[]{:S(2)}) collective-permute-start(f32[8,128]{1,0:T(8,128)S(1)} %get-tuple-element.52), channel_id=1, source_target_pairs={{4,8},{8,4},{5,9},{9,5},{6,10},{10,6},{7,11},{11,7},{20,24},{24,20... | collective-permute-start | bytes 12296 | tf_op jit(solution)/shard_map/ppermute | solution.py:497
  17.6 1.7 %collective-permute-start.6 = (f32[4,128]{1,0:T(4,128)S(1)}, f32[4,128]{1,0:T(4,128)S(1)}, u32[]{:S(2)}, u32[]{:S(2)}) collective-permute-start(f32[4,128]{1,0:T(4,128)S(1)} %get-tuple-element.53), channel_id=1, source_target_pairs={{0,2},{2,0},{1,3},{3,1},{4,6},{6,4},{5,7},{7,5},{8,10},{10,8},{9,1... | collective-permute-start | bytes 6152 | tf_op jit(solution)/shard_map/ppermute | solution.py:497
  19.4 0.6 %apply.1.refs_0_ = f32[4,256,128]{2,1,0:T(8,128)S(1)} custom-call(f32[4,272,128]{2,1,0:T(8,128)S(1)} %get-tuple-element.45.u_ref, f32[4,256,128]{2,1,0:T(8,128)S(1)} %get-tuple-element.46.diag_ref.refs_1_, f32[3,256,128]{2,1,0:T(8,128)S(1)} %get-tuple-element.47.cz_ref, f32[4,264,128]{2,1,0:T(8,128)S(1)} %get-tuple-element.39.refs_5_.cs_ref.refs_2_, ...), custom_call_target="tpu_custom_call" | custom-call | tf_op jit(solution)/shard_map/apply/pallas_call | solution.py:476
  20.0 1.3 %collective-permute-done.6.refs_10_ = f32[4,128]{1,0:T(4,128)S(1)} collective-permute-done((f32[4,128]{1,0:T(4,128)S(1)}, f32[4,128]{1,0:T(4,128)S(1)}, u32[]{:S(2)}, u32[]{:S(2)}) %collective-permute-start.6) | collective-permute-done | bytes 2080 | tf_op jit(solution)/shard_map/ppermute | solution.py:497
  21.3 0.0 collective-permute-done.4.refs_8_
  21.3 0.0 collective-permute-done.5.refs_9_
  21.3 0.0 collective-permute-done.7.refs_11_
  21.3 2.3 %smooth.1 = (f32[4,256,128]{2,1,0:T(8,128)S(1)}, f32[4,272,128]{2,1,0:T(8,128)S(1)}, f32[8,128]{1,0:T(8,128)S(1)}, f32[8,128]{1,0:T(8,128)S(1)}, f32[4,128]{1,0:T(4,128)S(1)}, /*index=5*/f32[256,128]{1,0:T(8,128)S(1)}) custom-call(f32[4,256,128]{2,1,0:T(8,128)S(1)} %apply.1.refs_0_, ...), custom_call_target="tpu_custom_call", output_to_operand_aliasing={{0}: (0, {})} | custom-call | tf_op jit(solution)/shard_map/smooth/pallas_call | solution.py:476
  23.6 0.1 collective-permute-start.11
  23.7 1.4 %collective-permute-start.8 = (f32[8,128]{1,0:T(8,128)S(1)}, f32[8,128]{1,0:T(8,128)S(1)}, u32[]{:S(2)}, u32[]{:S(2)}) collective-permute-start(f32[8,128]{1,0:T(8,128)S(1)} %get-tuple-element.60), channel_id=1, source_target_pairs={{0,4},{4,0},{8,12},{12,8},{1,5},{5,1},{9,13},{13,9},{2,6},{6,2},{1... | collective-permute-start | bytes 12296 | tf_op jit(solution)/shard_map/ppermute | solution.py:497
  25.0 0.6 %collective-permute-start.9 = (f32[8,128]{1,0:T(8,128)S(1)}, f32[8,128]{1,0:T(8,128)S(1)}, u32[]{:S(2)}, u32[]{:S(2)}) collective-permute-start(f32[8,128]{1,0:T(8,128)S(1)} %get-tuple-element.61), channel_id=1, source_target_pairs={{4,8},{8,4},{5,9},{9,5},{6,10},{10,6},{7,11},{11,7},{20,24},{24,20... | collective-permute-start | bytes 12296 | tf_op jit(solution)/shard_map/ppermute | solution.py:497
  25.7 1.9 %collective-permute-start.10 = (f32[4,128]{1,0:T(4,128)S(1)}, f32[4,128]{1,0:T(4,128)S(1)}, u32[]{:S(2)}, u32[]{:S(2)}) collective-permute-start(f32[4,128]{1,0:T(4,128)S(1)} %get-tuple-element.62), channel_id=1, source_target_pairs={{0,2},{2,0},{1,3},{3,1},{4,6},{6,4},{5,7},{7,5},{8,10},{10,8},{9,1... | collective-permute-start | bytes 6152 | tf_op jit(solution)/shard_map/ppermute | solution.py:497
  27.6 0.6 %sums.1 = (f32[4,256,128]{2,1,0:T(8,128)S(1)}, f32[3,8,128]{2,1,0:T(8,128)S(1)}) custom-call(f32[4,272,128]{2,1,0:T(8,128)S(1)} %get-tuple-element.55.m_ref.refs_1_, f32[4,272,128]{2,1,0:T(8,128)S(1)} %get-tuple-element.45.u_ref, f32[4,256,128]{2,1,0:T(8,128)S(1)} %get-tuple-element.56.r_ref, f32[4,256,128]{2,1,0:T(8,128)S(1)} %get-tuple-element.57.w_ref, ...), custom_call_target="tpu_custom_call" | custom-call | tf_op jit(solution)/shard_map/sums/pallas_call | solution.py:476
  28.3 1.1 %collective-permute-done.10.refs_8_ = f32[4,128]{1,0:T(4,128)S(1)} collective-permute-done((f32[4,128]{1,0:T(4,128)S(1)}, f32[4,128]{1,0:T(4,128)S(1)}, u32[]{:S(2)}, u32[]{:S(2)}) %collective-permute-start.10) | collective-permute-done | bytes 2080 | tf_op jit(solution)/shard_map/ppermute | solution.py:497
  29.3 0.0 collective-permute-done.8.refs_6_
  29.4 0.0 collective-permute-done.9.refs_7_
  29.4 0.0 collective-permute-done.11.refs_9_
  29.4 0.4 finish.1
  29.8 12.7 %all_to_all.5.all_ref = f32[16,4,128]{2,1,0:T(4,128)S(1)} all-to-all(f32[16,4,128]{2,1,0:T(4,128)S(1)} %get-tuple-element.64), channel_id=1, replica_groups=mesh['groups'=2,'gx'=4,'gy'=2,'gz'=2] {'gx','gy','gz'}, dimensions={0} | all-to-all | bytes 65536 | tf_op jit(solution)/shard_map/all_to_all | solution.py:560
  42.5 1.3 %update.1 = (f32[4,256,128]{2,1,0:T(8,128)}, f32[4,256,128]{2,1,0:T(8,128)}) custom-call(f32[16,4,128]{2,1,0:T(4,128)S(1)} %all_to_all.5.all_ref, f32[4,272,128]{2,1,0:T(8,128)S(1)} %get-tuple-element.34.x_ref.refs_0_, f32[4,256,128]{2,1,0:T(8,128)S(1)} %get-tuple-element.56.r_ref, f32[4,272,128]{2,1,0:T(8,128)S(1)} %get-tuple-element.45.u_ref, ...), custom_call_target="tpu_custom_call" | custom-call | tf_op jit(solution)/shard_map/update/pallas_call | solution.py:476
Async XLA Ops:
  0.6 7.4 %copy-start.1 = (f32[8,64,128]{2,1,0:T(8,128)S(1)}, f32[8,64,128]{2,1,0:T(8,128)}, u32[]{:S(2)}) copy-start(f32[8,64,128]{2,1,0:T(8,128)} %cat_ref.1) | copy-start | bytes 786436
  0.6 7.4 %copy-start = (f32[4,256,128]{2,1,0:T(8,128)S(1)}, f32[4,256,128]{2,1,0:T(8,128)}, u32[]{:S(2)}) copy-start(f32[4,256,128]{2,1,0:T(8,128)} %c_ref.1) | copy-start | bytes 1572868
  2.7 7.5 %collective-permute-start.3 = (f32[2,256,128]{2,1,0:T(8,128)S(1)}, f32[2,256,128]{2,1,0:T(8,128)S(1)}, u32[]{:S(2)}, u32[]{:S(2)}) collective-permute-start(f32[2,256,128]{2,1,0:T(8,128)S(1)} %get-tuple-element.44), channel_id=1, source_target_pairs={{0,1},{1,0},{2,3},{3,2},{4,5},{5,4},{6,7},{7,6},{8,9},{9,8},{10,11... | collective-permute-start | bytes 786440 | tf_op jit(solution)/shard_map/ppermute | solution.py:497
  3.2 7.0 %collective-permute-start = (f32[2,8,128]{2,1,0:T(8,128)S(1)}, f32[2,8,128]{2,1,0:T(8,128)S(1)}, u32[]{:S(2)}, u32[]{:S(2)}) collective-permute-start(f32[2,8,128]{2,1,0:T(8,128)S(1)} %get-tuple-element.41), channel_id=1, source_target_pairs={{0,4},{4,0},{8,12},{12,8},{1,5},{5,1},{9,13},{13,9},{2,6},{6,2},{1... | collective-permute-start | bytes 24584 | tf_op jit(solution)/shard_map/ppermute | solution.py:497
  5.9 4.3 %collective-permute-start.1 = (f32[2,8,128]{2,1,0:T(8,128)S(1)}, f32[2,8,128]{2,1,0:T(8,128)S(1)}, u32[]{:S(2)}, u32[]{:S(2)}) collective-permute-start(f32[2,8,128]{2,1,0:T(8,128)S(1)} %get-tuple-element.42), channel_id=1, source_target_pairs={{4,8},{8,4},{5,9},{9,5},{6,10},{10,6},{7,11},{11,7},{20,24},{24,20... | collective-permute-start | bytes 24584 | tf_op jit(solution)/shard_map/ppermute | solution.py:497
  6.5 3.7 %collective-permute-start.2 = (f32[2,4,128]{2,1,0:T(4,128)S(1)}, f32[2,4,128]{2,1,0:T(4,128)S(1)}, u32[]{:S(2)}, u32[]{:S(2)}) collective-permute-start(f32[2,4,128]{2,1,0:T(4,128)S(1)} %get-tuple-element.43), channel_id=1, source_target_pairs={{0,2},{2,0},{1,3},{3,1},{4,6},{6,4},{5,7},{7,5},{8,10},{10,8},{9,1... | collective-permute-start | bytes 12296 | tf_op jit(solution)/shard_map/ppermute | solution.py:497
  12.8 8.5 %collective-permute-start.7 = (f32[256,128]{1,0:T(8,128)S(1)}, f32[256,128]{1,0:T(8,128)S(1)}, u32[]{:S(2)}, u32[]{:S(2)}) collective-permute-start(f32[256,128]{1,0:T(8,128)S(1)} %get-tuple-element.54), channel_id=1, source_target_pairs={{0,1},{1,0},{2,3},{3,2},{4,5},{5,4},{6,7},{7,6},{8,9},{9,8},{10,11... | collective-permute-start | bytes 393224 | tf_op jit(solution)/shard_map/ppermute | solution.py:497
  12.9 8.4 %collective-permute-start.4 = (f32[8,128]{1,0:T(8,128)S(1)}, f32[8,128]{1,0:T(8,128)S(1)}, u32[]{:S(2)}, u32[]{:S(2)}) collective-permute-start(f32[8,128]{1,0:T(8,128)S(1)} %get-tuple-element.51), channel_id=1, source_target_pairs={{0,4},{4,0},{8,12},{12,8},{1,5},{5,1},{9,13},{13,9},{2,6},{6,2},{1... | collective-permute-start | bytes 12296 | tf_op jit(solution)/shard_map/ppermute | solution.py:497
  17.0 4.3 %collective-permute-start.5 = (f32[8,128]{1,0:T(8,128)S(1)}, f32[8,128]{1,0:T(8,128)S(1)}, u32[]{:S(2)}, u32[]{:S(2)}) collective-permute-start(f32[8,128]{1,0:T(8,128)S(1)} %get-tuple-element.52), channel_id=1, source_target_pairs={{4,8},{8,4},{5,9},{9,5},{6,10},{10,6},{7,11},{11,7},{20,24},{24,20... | collective-permute-start | bytes 12296 | tf_op jit(solution)/shard_map/ppermute | solution.py:497
  17.6 3.7 %collective-permute-start.6 = (f32[4,128]{1,0:T(4,128)S(1)}, f32[4,128]{1,0:T(4,128)S(1)}, u32[]{:S(2)}, u32[]{:S(2)}) collective-permute-start(f32[4,128]{1,0:T(4,128)S(1)} %get-tuple-element.53), channel_id=1, source_target_pairs={{0,2},{2,0},{1,3},{3,1},{4,6},{6,4},{5,7},{7,5},{8,10},{10,8},{9,1... | collective-permute-start | bytes 6152 | tf_op jit(solution)/shard_map/ppermute | solution.py:497
  23.6 5.7 %collective-permute-start.11 = (f32[256,128]{1,0:T(8,128)S(1)}, f32[256,128]{1,0:T(8,128)S(1)}, u32[]{:S(2)}, u32[]{:S(2)}) collective-permute-start(f32[256,128]{1,0:T(8,128)S(1)} %get-tuple-element.63), channel_id=1, source_target_pairs={{0,1},{1,0},{2,3},{3,2},{4,5},{5,4},{6,7},{7,6},{8,9},{9,8},{10,11... | collective-permute-start | bytes 393224 | tf_op jit(solution)/shard_map/ppermute | solution.py:497
  23.7 5.7 %collective-permute-start.8 = (f32[8,128]{1,0:T(8,128)S(1)}, f32[8,128]{1,0:T(8,128)S(1)}, u32[]{:S(2)}, u32[]{:S(2)}) collective-permute-start(f32[8,128]{1,0:T(8,128)S(1)} %get-tuple-element.60), channel_id=1, source_target_pairs={{0,4},{4,0},{8,12},{12,8},{1,5},{5,1},{9,13},{13,9},{2,6},{6,2},{1... | collective-permute-start | bytes 12296 | tf_op jit(solution)/shard_map/ppermute | solution.py:497
  25.0 4.3 %collective-permute-start.9 = (f32[8,128]{1,0:T(8,128)S(1)}, f32[8,128]{1,0:T(8,128)S(1)}, u32[]{:S(2)}, u32[]{:S(2)}) collective-permute-start(f32[8,128]{1,0:T(8,128)S(1)} %get-tuple-element.61), channel_id=1, source_target_pairs={{4,8},{8,4},{5,9},{9,5},{6,10},{10,6},{7,11},{11,7},{20,24},{24,20... | collective-permute-start | bytes 12296 | tf_op jit(solution)/shard_map/ppermute | solution.py:497
  25.7 3.7 %collective-permute-start.10 = (f32[4,128]{1,0:T(4,128)S(1)}, f32[4,128]{1,0:T(4,128)S(1)}, u32[]{:S(2)}, u32[]{:S(2)}) collective-permute-start(f32[4,128]{1,0:T(4,128)S(1)} %get-tuple-element.62), channel_id=1, source_target_pairs={{0,2},{2,0},{1,3},{3,1},{4,6},{6,4},{5,7},{7,5},{8,10},{10,8},{9,1... | collective-permute-start | bytes 6152 | tf_op jit(solution)/shard_map/ppermute | solution.py:497

commit v5 on v4

--- a/solution.py
+++ b/solution.py
@@ -276,7 +276,7 @@
             inside = pl.ds(at + 8, 8)
             face = harmonic(k_ref[i, inside, :], ref[1, i : i + 1, :])
             face = jnp.where(mask, face, 0.0)
-            cy_ref[n, i] = face
+            cy_ref[n, i : i + 1, :] = jnp.sum(face, axis=0, keepdims=True)
             diag_in[i, there, :] = diag_in[i, there, :] + face
             r_in[i, there, :] = r_in[i, there, :] + face * (ref[0, i : i + 1, :] - x_ref[i, inside, :])
     xlo, xhi = column_halos(hx, (0,))
@@ -331,26 +331,29 @@
     lax.fori_loop(0, y // tall, step, 0)
 
 
-def subtract_halos(w_ref, halos, cy_ref, czh_ref):
-    hx, hy, hz = halos
-    z, y, _ = w_ref.shape
-    for n, ref in enumerate(hz):
-        p = jnp.where(low_side("gz", n), 0, z - 1)
+def subtract_tiers(w_ref, halos, czh_ref):
+    for n, ref in enumerate(halos):
+        p = jnp.where(low_side("gz", n), 0, w_ref.shape[0] - 1)
         w_ref[p] = w_ref[p] - czh_ref[n] * ref[...]
-    for n, ref in enumerate(hy):
-        at = pl.ds(pl.multiple_of(jnp.where(low_side("gy", n), 0, y - 8), 8), 8)
-        for i in range(z):
-            w_ref[i, at, :] = w_ref[i, at, :] - cy_ref[n, i] * ref[i : i + 1, :]
+
+
+def border_rows(n, y):
+    low = low_side("gy", n)
+    at = pl.ds(pl.multiple_of(jnp.where(low, 0, y - 8), 8), 8)
+    return at, rows((8, 128)) == jnp.where(low, 0, 7)
 
 
 def smooth_kernel(rounds, tall, *refs):
     (w_in, diag_ref, cs_ref, ce_ref, cx_ref, cy_ref, czh_ref, lev_in), refs = refs[:8], refs[8:]
     halos, refs = regroup(refs, rounds)
-    (w_ref, m_ref), refs = refs[:2], refs[2:]
-    sends, (lev_ref, sems) = regroup(refs, rounds)
+    w_ref, m_ref, face_ref, *send_refs, lev_ref, sems = refs
     z, y, _ = w_ref.shape
     table = start_all((lev_in,), (lev_ref,), sems)
-    subtract_halos(w_in, halos, cy_ref, czh_ref)
+    subtract_tiers(w_in, halos[2], czh_ref)
+    for n, ref in enumerate(halos[1]):
+        at, mask = border_rows(n, y)
+        for i in range(z):
+            w_in[i, at, :] = w_in[i, at, :] - jnp.where(mask, cy_ref[n, i : i + 1, :] * ref[i : i + 1, :], 0.0)
     xlo, xhi = column_halos(halos[0])
     flux = stage_columns(cx_ref[0] * xlo, cx_ref[1] * xhi)
     edge = edge_lanes()
@@ -364,7 +367,28 @@
     table[0].wait()
     sweeps(m_ref, diag_ref, cs_ref, ce_ref, lev_ref, tall)
     tier, row, vreg = padded_access(m_ref)
-    fill_sends(tier, row, sends, None, pack_columns(vreg, z * per), z, y)
+    for n, ref in enumerate(send_refs):
+        ref[...] = tier(jnp.where(low_side("gz", n), 0, z - 1))
+    first, last = pack_columns(vreg, z * per)
+    plan, _ = face_plan(z, first.shape[0], rounds)
+    low = low_side("gy", 0)
+    if rounds[1] == 1:
+        face_ref[plan["y_low"]] = jnp.where(low, cy_ref[0] * row(0), row(y - 1))
+    else:
+        face_ref[plan["y_low"]] = jnp.where(low, cy_ref[0], cy_ref[1]) * row(0)
+        face_ref[plan["y_high"]] = row(y - 1)
+    face_ref[plan["x_low"]] = cx_ref[0] * first
+    face_ref[plan["x_high"]] = last
+    face_ref[plan["sums"]] = jnp.zeros((4, 128), F32)
+
+
+def face_plan(z, packed, rounds):
+    plan, at = {}, 0
+    parts = (("sums", 4), ("y_low", z), ("x_low", packed), ("x_high", packed), ("y_high", z))
+    for name, count in parts[: 4 if rounds[1] == 1 else 5]:
+        plan[name] = slice(at, at + count)
+        at += count
+    return plan, at
 
 
 def fold(product):
@@ -375,49 +399,70 @@
     z, y, _ = diag_ref.shape
 
     def step(t, carry):
-        gamma, delta, cross = carry
+        gamma, delta, cross, last = carry
         at = pl.multiple_of(t * tall, 8)
         near = pl.ds(at, tall)
         for i in range(z):
-            m, n_ref[i, near, :] = apply_inner(m_ref, diag_ref, cz_ref, cs_ref, ce_ref, i, at, tall)
+            m, n = apply_inner(m_ref, diag_ref, cz_ref, cs_ref, ce_ref, i, at, tall)
+            n_ref[i, near, :] = n
             u = u_ref[i, pl.ds(at + 8, tall), :]
             w = w_ref[i, near, :]
             gamma = gamma + fold(r_ref[i, near, :] * u)
             delta = delta + fold(w * u)
             cross = cross + fold(w * m)
-        return gamma, delta, cross
+            last = last + fold(n * m)
+        return gamma, delta, cross, last
 
     zero = jnp.zeros((8, 128), F32)
-    for n, value in enumerate(lax.fori_loop(0, y // tall, step, (zero, zero, zero))):
+    for n, value in enumerate(lax.fori_loop(0, y // tall, step, (zero,) * 4)):
         sum_ref[n] = value
 
 
 def finish_kernel(rounds, *refs):
-    (n_in, m_ref, sum_ref, cx_ref, cy_ref, czh_ref), refs = refs[:6], refs[6:]
-    halos, (n_ref, out_ref) = regroup(refs, rounds)
+    (n_in, m_ref, sum_ref, czh_ref, face_ref), refs = refs[:5], refs[5:]
+    (halos,), (n_ref, out_ref) = regroup(refs, rounds[2:])
     z, y, _ = n_ref.shape
-    subtract_halos(n_in, halos, cy_ref, czh_ref)
-    xlo, xhi = column_halos(halos[0])
-    flux = stage_columns(cx_ref[0] * xlo, cx_ref[1] * xhi)
-    edge = edge_lanes()
-    per = y // 8
-    parts = [jnp.zeros((8, 128), F32) for _ in range(8)]
-    for i in range(z * per):
-        at = (i // per, slice(8 * (i % per), 8 * (i % per) + 8))
-        n = n_in[at] - spread_columns(flux, edge, i)
-        n_ref[at] = n
-        parts[i % 8] = parts[i % 8] + n * m_ref[i // per, 8 + 8 * (i % per) : 16 + 8 * (i % per)]
-    while len(parts) > 1:
-        parts = [a + b for a, b in zip(parts[::2], parts[1::2])]
-    parts = [sum_ref[0], sum_ref[1], sum_ref[2], parts[0]]
-    parts = jnp.concatenate([jnp.sum(p, axis=0, keepdims=True) for p in parts], 0)
+    last = sum_ref[3]
+    for n, ref in enumerate(halos):
+        p = jnp.where(low_side("gz", n), 0, z - 1)
+        flux = czh_ref[n] * ref[...]
+        n_ref[p] = n_in[p] - flux
+        last = last - fold(flux * m_ref[p, pl.ds(8, y), :])
+    parts = [sum_ref[0], sum_ref[1], sum_ref[2], last]
+    parts = [jnp.sum(p, axis=0, keepdims=True) for p in parts]
+    height = face_ref.shape[0]
+    everything = jnp.concatenate(parts + [face_ref[4:height]], 0)
     for d in range(out_ref.shape[0]):
-        out_ref[d] = parts
-
-
-def update_kernel(all_ref, x_ref, r_ref, u_ref, w_ref, m_ref, n_ref, x_out, r_out, xo_ref, ro_ref, sems):
-    sums = jnp.sum(all_ref[...], axis=0)
+        out_ref[d] = everything
+
+
+def update_kernel(rounds, sizes, *refs):
+    all_ref, x_ref, r_ref, u_ref, w_ref, m_ref, n_ref, cx_ref, cy_ref, x_out, r_out, xo_ref, ro_ref, sems = refs
+    z, y, _ = r_ref.shape
+    packed = cx_ref.shape[1]
+    plan, _ = face_plan(z, packed, rounds)
+    nx, ny, nz = sizes
+    members = nx * ny * nz
+    y_high = plan["y_low" if rounds[1] == 1 else "y_high"]
+
+    def tree(values):
+        while len(values) > 1:
+            values = [a + b for a, b in zip(values[::2], values[1::2])] + values[len(values) // 2 * 2 :]
+        return values[0]
+
+    sums = tree([all_ref[d, plan["sums"], :] for d in range(members)])
     gamma, delta, cross, last = (sums[i : i + 1] for i in range(4))
+    links = []
+    for d in range(members - ny * nz):
+        links.append(all_ref[d, plan["x_high"], :] * all_ref[d + ny * nz, plan["x_low"], :])
+    if links:
+        last = last - 2.0 * jnp.sum(tree(links), axis=0, keepdims=True)
+    links = []
+    for d in range(members - nz):
+        if d // nz % ny + 1 < ny:
+            links.append(all_ref[d, y_high, :] * all_ref[d + nz, plan["y_low"], :])
+    if links:
+        last = last - 2.0 * jnp.sum(tree(links), axis=0, keepdims=True)
 
     def total(v):
         return jnp.sum(v, axis=1, keepdims=True)
@@ -430,13 +475,37 @@
     alpha1 = gamma1 / (delta1 - beta * gamma1 / alpha0)
     near = alpha0 + alpha1 * (1.0 + beta)
     far = alpha1 * alpha0
-    z, y, _ = r_ref.shape
+
+    gx, gy, gz = (lax.axis_index(axis) for axis in GRID_AXES)
+    me = (gx * ny + gy) * nz + gz
+    left = jnp.maximum(me - ny * nz, 0)
+    right = jnp.minimum(me + ny * nz, members - 1)
+    has_right = gx < nx - 1
+    west = far * (cx_ref[0] * all_ref[left, plan["x_high"], :])
+    east = far * jnp.where(has_right, all_ref[right, plan["x_low"], :], 0.0)
+    flux = stage_columns(west, east)
+    below = jnp.maximum(me - nz, 0)
+    above = jnp.minimum(me + nz, members - 1)
+    row_flux = []
+    for n in range(rounds[1]):
+        low = low_side("gy", n)
+        from_below = cy_ref[n] * all_ref[below, y_high, :]
+        from_above = jnp.where(gy < ny - 1, all_ref[above, plan["y_low"], :], 0.0)
+        row_flux.append(far * jnp.where(low, from_below, from_above))
+    edge = edge_lanes()
+    per = y // 8
     copies = []
     for i in range(z):
         inner = (i, slice(8, 8 + y))
+        for j in range(per):
+            at = (i, slice(8 * j, 8 * j + 8))
+            ro_ref[at] = r_ref[at] - near * w_ref[at] + (far * n_ref[at] - spread_columns(flux, edge, i * per + j))
+        for n in range(rounds[1]):
+            at, mask = border_rows(n, y)
+            ro_ref[i, at, :] = ro_ref[i, at, :] - jnp.where(mask, row_flux[n][i : i + 1], 0.0)
+        copies += start_all((ro_ref.at[i],), (r_out.at[i],), sems.at[0, i : i + 1])
         xo_ref[i] = x_ref[inner] + near * u_ref[inner] - far * m_ref[inner]
-        ro_ref[i] = r_ref[i] - near * w_ref[i] + far * n_ref[i]
-        copies += start_all((xo_ref.at[i], ro_ref.at[i]), (x_out.at[i], r_out.at[i]), sems.at[i])
+        copies += start_all((xo_ref.at[i],), (x_out.at[i],), sems.at[1, i : i + 1])
     for copy in copies:
         copy.wait()
 
@@ -467,6 +536,7 @@
     shape = lambda *s: pltpu.VMEM(s, F32)
     full = shape(z, y, x)
     tall_field = shape(z, y + 16, x)
+    _, height = face_plan(z, 8 * groups, rounds)
 
     hbm = pl.BlockSpec(memory_space=pltpu.HBM)
 
@@ -490,10 +560,10 @@
             out += [shape(*front, *axis)] * n
         return out
 
-    def swap(faces):
+    def swap(faces, axes=GRID_AXES):
         faces, got = list(faces), []
-        for axis, n in zip(GRID_AXES, rounds):
-            for start in range(n):
+        for axis in axes:
+            for start in range(rounds[GRID_AXES.index(axis)]):
                 got.append(lax.ppermute(faces.pop(0), axis, swap_pairs(axis, start)))
         return got
 
@@ -524,7 +594,7 @@
     )
     outs = call(
         functools.partial(border_kernel, rounds, tall),
-        [full, full, tall_field, shape(2, 8 * groups, x), shape(rounds[1], z, 8, x), shape(rounds[2], y, x)]
+        [full, full, tall_field, shape(2, 8 * groups, x), shape(rounds[1], z, x), shape(rounds[2], y, x)]
         + face_shapes(()),
         [field, kappa, own, r, diag, cs, ce, levels] + halos,
         "border",
@@ -537,34 +607,34 @@
     (w,) = call(functools.partial(apply_kernel, tall), [full], [u, diag, cz, cs, ce], "apply")
     outs = call(
         functools.partial(smooth_kernel, rounds, tall),
-        [full, tall_field] + face_shapes(()),
+        [full, tall_field, shape(height, x)] + [shape(y, x)] * rounds[2],
         [w, diag, cs, ce, cx, cy, czh, levels] + halos,
         "smooth",
         [table(levels), pltpu.SemaphoreType.DMA((1,))],
         alias={0: 0},
         outer=(7,),
     )
-    w, m = outs[:2]
-    halos = swap(outs[2:])
+    w, m, faces = outs[:3]
+    halos = swap(outs[3:], GRID_AXES[2:])
     n, sums = call(
-        functools.partial(sums_kernel, tall), [full, shape(3, 8, 128)], [m, u, r, w, diag, cz, cs, ce], "sums"
-    )
-    members = math.prod(lax.axis_size(axis) for axis in GRID_AXES)
+        functools.partial(sums_kernel, tall), [full, shape(4, 8, 128)], [m, u, r, w, diag, cz, cs, ce], "sums"
+    )
+    sizes = tuple(lax.axis_size(axis) for axis in GRID_AXES)
     n, parts = call(
         functools.partial(finish_kernel, rounds),
-        [full, shape(members, 4, 128)],
-        [n, m, sums, cx, cy, czh] + halos,
+        [full, shape(math.prod(sizes), height, x)],
+        [n, m, sums, czh, faces] + halos,
         "finish",
         alias={0: 0},
     )
     every = lax.all_to_all(parts, GRID_AXES, 0, 0, tiled=True)
     return tuple(
         call(
-            update_kernel,
+            functools.partial(update_kernel, rounds, sizes),
             [jax.ShapeDtypeStruct((z, y, x), F32)] * 2,
-            [every, field, r, u, w, m, n],
+            [every, field, r, u, w, m, n, cx, cy],
             "update",
-            [full, full, pltpu.SemaphoreType.DMA((z, 2))],
+            [full, full, pltpu.SemaphoreType.DMA((2, z))],
             out_specs=[hbm, hbm],
         )
     )

time: 44.2 us -> 41.5 us (0.939)
  starting transfers between devices: 15.9 us -> 12.8 us
  blocking collectives: 12.7 us -> 13.5 us
    ppermute x12 -> x9, starting transfers between devices: 15.9 us -> 12.8 us  [swap(): got.append(lax.ppermute(faces.pop(0), axis, swap_pairs(axis, start)))]
    all_to_all x1, blocking collectives: 12.7 us -> 13.5 us  [body(): every = lax.all_to_all(parts, GRID_AXES, 0, 0, tiled=True)]
    ppermute x12 -> x9, waiting for transfers between devices: 3 us -> 2.57 us  [swap(): got.append(lax.ppermute(faces.pop(0), axis, swap_pairs(axis, start)))]
  transfers between devices with their start and end apart: 12 -> 9, of which waited for: 3 -> 3; matrix products, arithmetic and copies ran while one was open for 0% -> 0% of each run, Pallas kernels for 6% -> 7%
where the time goes in v5:
time: 41.5 us; the launch traced here: 41.3 us
  blocking collectives  13.5 us (33%)
  starting transfers between devices  12.8 us (31%)
  Pallas kernels  11.7 us (28%)
  waiting for transfers between devices  2.57 us (6%)
  between operations  0.74 us (2%)
    all_to_all x1, blocking collectives, body(): every = lax.all_to_all(parts, GRID_AXES, 0, 0, tiled=True)  13.5 us
    ppermute x9, starting transfers between devices, swap(): got.append(lax.ppermute(faces.pop(0), axis, swap_pairs(axis, start)))  12.8 us
    pallas_call x8, Pallas kernels, call(): pl.pallas_call(kernel, out_shape=outs, in_specs=specs, out_specs=out_spec...  11.7 us
    ppermute x9, waiting for transfers between devices, swap(): got.append(lax.ppermute(faces.pop(0), axis, swap_pairs(axis, start)))  2.57 us
  transfers between devices with their start and end apart: 9, of which 3 were waited for; matrix products, arithmetic and copies ran while one was open for 0% of the time, Pallas kernels for 7%

profile of v5, /device:TPU:0, one launch (start us, length us, event | category | flops | bytes accessed | tf_op | source)
XLA Modules:
  0.0 41.3 jit_solution(18092433344239076582)
XLA Ops:
  0.6 0.0 copy-start.1
  0.6 0.0 copy-start
  0.7 2.0 %faces.1 = (f32[4,272,128]{2,1,0:T(8,128)S(1)}, f32[4,272,128]{2,1,0:T(8,128)S(1)}, f32[2,8,128]{2,1,0:T(8,128)S(1)}, f32[2,8,128]{2,1,0:T(8,128)S(1)}, f32[2,4,...) custom-call(f32[4,256,128]{2,1,0:T(8,128)} %x_in.1, f32[4,256,128]{2,1,0:T(8,128)} %k_in.1), custom_call_target="tpu_custom_call" | custom-call | tf_op jit(solution)/shard_map/faces/pallas_call | solution.py:546
  2.7 0.6 %collective-permute-start.3 = (f32[2,256,128]{2,1,0:T(8,128)S(1)}, f32[2,256,128]{2,1,0:T(8,128)S(1)}, u32[]{:S(2)}, u32[]{:S(2)}) collective-permute-start(f32[2,256,128]{2,1,0:T(8,128)S(1)} %get-tuple-element.42), channel_id=1, source_target_pairs={{0,1},{1,0},{2,3},{3,2},{4,5},{5,4},{6,7},{7,6},{8,9},{9,8},{10,11... | collective-permute-start | bytes 786440 | tf_op jit(solution)/shard_map/ppermute | solution.py:567
  3.2 2.6 %collective-permute-start = (f32[2,8,128]{2,1,0:T(8,128)S(1)}, f32[2,8,128]{2,1,0:T(8,128)S(1)}, u32[]{:S(2)}, u32[]{:S(2)}) collective-permute-start(f32[2,8,128]{2,1,0:T(8,128)S(1)} %get-tuple-element.39), channel_id=1, source_target_pairs={{0,4},{4,0},{8,12},{12,8},{1,5},{5,1},{9,13},{13,9},{2,6},{6,2},{1... | collective-permute-start | bytes 24584 | tf_op jit(solution)/shard_map/ppermute | solution.py:567
  5.9 0.6 %collective-permute-start.1 = (f32[2,8,128]{2,1,0:T(8,128)S(1)}, f32[2,8,128]{2,1,0:T(8,128)S(1)}, u32[]{:S(2)}, u32[]{:S(2)}) collective-permute-start(f32[2,8,128]{2,1,0:T(8,128)S(1)} %get-tuple-element.40), channel_id=1, source_target_pairs={{4,8},{8,4},{5,9},{9,5},{6,10},{10,6},{7,11},{11,7},{20,24},{24,20... | collective-permute-start | bytes 24584 | tf_op jit(solution)/shard_map/ppermute | solution.py:567
  6.5 1.6 %collective-permute-start.2 = (f32[2,4,128]{2,1,0:T(4,128)S(1)}, f32[2,4,128]{2,1,0:T(4,128)S(1)}, u32[]{:S(2)}, u32[]{:S(2)}) collective-permute-start(f32[2,4,128]{2,1,0:T(4,128)S(1)} %get-tuple-element.41), channel_id=1, source_target_pairs={{0,2},{2,0},{1,3},{3,1},{4,6},{6,4},{5,7},{7,5},{8,10},{10,8},{9,1... | collective-permute-start | bytes 12296 | tf_op jit(solution)/shard_map/ppermute | solution.py:567
  8.1 0.0 copy-done.1
  8.1 0.0 copy-done
  8.1 1.5 %inner.1 = (f32[4,256,128]{2,1,0:T(8,128)S(1)}, f32[4,256,128]{2,1,0:T(8,128)S(1)}, f32[3,256,128]{2,1,0:T(8,128)S(1)}, f32[4,264,128]{2,1,0:T(8,128)S(1)}, f32[4,256,128]{2,1,0:T(8,128)S(1)}) custom-call(f32[4,272,128]{2,1,0:T(8,128)S(1)} %get-tuple-element.32.x_ref.refs_0_.refs_1_, f32[4,272,128]{2,1,0:T(8,128)S(1)} %get-tuple-element.33.k_ref.refs_1_, ...), custom_call_target="tpu_custom_call" | custom-call | tf_op jit(solution)/shard_map/inner/pallas_call | solution.py:546
  9.6 0.6 %collective-permute-done.2.refs_10_ = f32[2,4,128]{2,1,0:T(4,128)S(1)} collective-permute-done((f32[2,4,128]{2,1,0:T(4,128)S(1)}, f32[2,4,128]{2,1,0:T(4,128)S(1)}, u32[]{:S(2)}, u32[]{:S(2)}) %collective-permute-start.2) | collective-permute-done | bytes 4128 | tf_op jit(solution)/shard_map/ppermute | solution.py:567
  10.2 0.0 collective-permute-done.refs_8_
  10.2 0.0 collective-permute-done.1.refs_9_
  10.2 0.0 collective-permute-done.3.refs_11_
  10.2 2.9 %border.1 = (f32[4,256,128]{2,1,0:T(8,128)S(1)}, f32[4,256,128]{2,1,0:T(8,128)S(1)}, f32[4,272,128]{2,1,0:T(8,128)S(1)}, f32[2,8,128]{2,1,0:T(8,128)S(1)}, f32[1...) custom-call(f32[4,272,128]{2,1,0:T(8,128)S(1)} %get-tuple-element.32, ...), custom_call_target="tpu_custom_call", output_to_operand_aliasing={{0}: (3, {}), {1}: (4, {})} | custom-call | tf_op jit(solution)/shard_map/border/pallas_call | solution.py:546
  13.1 0.1 collective-permute-start.7
  13.2 4.7 %collective-permute-start.4 = (f32[8,128]{1,0:T(8,128)S(1)}, f32[8,128]{1,0:T(8,128)S(1)}, u32[]{:S(2)}, u32[]{:S(2)}) collective-permute-start(f32[8,128]{1,0:T(8,128)S(1)} %get-tuple-element.49), channel_id=1, source_target_pairs={{0,4},{4,0},{8,12},{12,8},{1,5},{5,1},{9,13},{13,9},{2,6},{6,2},{1... | collective-permute-start | bytes 12296 | tf_op jit(solution)/shard_map/ppermute | solution.py:567
  17.9 0.6 %collective-permute-start.5 = (f32[8,128]{1,0:T(8,128)S(1)}, f32[8,128]{1,0:T(8,128)S(1)}, u32[]{:S(2)}, u32[]{:S(2)}) collective-permute-start(f32[8,128]{1,0:T(8,128)S(1)} %get-tuple-element.50), channel_id=1, source_target_pairs={{4,8},{8,4},{5,9},{9,5},{6,10},{10,6},{7,11},{11,7},{20,24},{24,20... | collective-permute-start | bytes 12296 | tf_op jit(solution)/shard_map/ppermute | solution.py:567
  18.6 1.8 %collective-permute-start.6 = (f32[4,128]{1,0:T(4,128)S(1)}, f32[4,128]{1,0:T(4,128)S(1)}, u32[]{:S(2)}, u32[]{:S(2)}) collective-permute-start(f32[4,128]{1,0:T(4,128)S(1)} %get-tuple-element.51), channel_id=1, source_target_pairs={{0,2},{2,0},{1,3},{3,1},{4,6},{6,4},{5,7},{7,5},{8,10},{10,8},{9,1... | collective-permute-start | bytes 6152 | tf_op jit(solution)/shard_map/ppermute | solution.py:567
  20.4 0.5 %apply.1.refs_0_ = f32[4,256,128]{2,1,0:T(8,128)S(1)} custom-call(f32[4,272,128]{2,1,0:T(8,128)S(1)} %get-tuple-element.43.u_ref.refs_3_, f32[4,256,128]{2,1,0:T(8,128)S(1)} %get-tuple-element.44.diag_ref.refs_1_, f32[3,256,128]{2,1,0:T(8,128)S(1)} %get-tuple-element.45.cz_ref, f32[4,264,128]{2,1,0:T(8,128)S(1)} %get-tuple-element.37.refs_5_.cs_ref.refs_2_, ...), custom_call_target="tpu_custom_call" | custom-call | tf_op jit(solution)/shard_map/apply/pallas_call | solution.py:546
  20.9 1.3 %collective-permute-done.6.refs_10_ = f32[4,128]{1,0:T(4,128)S(1)} collective-permute-done((f32[4,128]{1,0:T(4,128)S(1)}, f32[4,128]{1,0:T(4,128)S(1)}, u32[]{:S(2)}, u32[]{:S(2)}) %collective-permute-start.6) | collective-permute-done | bytes 2080 | tf_op jit(solution)/shard_map/ppermute | solution.py:567
  22.2 0.0 collective-permute-done.4.refs_8_
  22.2 0.0 collective-permute-done.5.refs_9_
  22.2 0.0 collective-permute-done.7.refs_11_
  22.2 2.6 %smooth.1 = (f32[4,256,128]{2,1,0:T(8,128)S(1)}, f32[4,272,128]{2,1,0:T(8,128)S(1)}, f32[24,128]{1,0:T(8,128)S(1)}, f32[256,128]{1,0:T(8,128)S(1)}) custom-call(f32[4,256,128]{2,1,0:T(8,128)S(1)} %apply.1.refs_0_, f32[4,256,128]{2,1,0:T(8,128)S(1)} %get-tuple-element.44.diag_ref.refs_1_, ...), custom_call_target="tpu_custom_call", output_to_operand_aliasing={{0}: (0, {})} | custom-call | tf_op jit(solution)/shard_map/smooth/pallas_call | solution.py:546
  24.8 0.1 collective-permute-start.8
  24.9 0.7 %sums.1 = (f32[4,256,128]{2,1,0:T(8,128)S(1)}, f32[4,8,128]{2,1,0:T(8,128)S(1)}) custom-call(f32[4,272,128]{2,1,0:T(8,128)S(1)} %get-tuple-element.53.m_ref.refs_1_.refs_5_, f32[4,272,128]{2,1,0:T(8,128)S(1)} %get-tuple-element.43.u_ref.refs_3_, f32[4,256,128]{2,1,0:T(8,128)S(1)} %get-tuple-element.54.r_ref.refs_2_, ...), custom_call_target="tpu_custom_call" | custom-call | tf_op jit(solution)/shard_map/sums/pallas_call | solution.py:546
  25.6 0.6 %collective-permute-done.8.refs_5_ = f32[256,128]{1,0:T(8,128)S(1)} collective-permute-done((f32[256,128]{1,0:T(8,128)S(1)}, f32[256,128]{1,0:T(8,128)S(1)}, u32[]{:S(2)}, u32[]{:S(2)}) %collective-permute-start.8) | collective-permute-done | bytes 131104 | tf_op jit(solution)/shard_map/ppermute | solution.py:567
  26.2 0.1 finish.1
  26.3 13.5 %all_to_all.5.refs_0_ = f32[16,24,128]{2,1,0:T(8,128)S(1)} all-to-all(f32[16,24,128]{2,1,0:T(8,128)S(1)} %get-tuple-element.60), channel_id=1, replica_groups=mesh['groups'=2,'gx'=4,'gy'=2,'gz'=2] {'gx','gy','gz'}, dimensions={0} | all-to-all | bytes 393216 | tf_op jit(solution)/shard_map/all_to_all | solution.py:630
  39.8 1.5 %update.1 = (f32[4,256,128]{2,1,0:T(8,128)}, f32[4,256,128]{2,1,0:T(8,128)}) custom-call(f32[16,24,128]{2,1,0:T(8,128)S(1)} %all_to_all.5.refs_0_, f32[4,272,128]{2,1,0:T(8,128)S(1)} %get-tuple-element.32.x_ref.refs_0_.refs_1_, f32[4,256,128]{2,1,0:T(8,128)S(1)} %get-tuple-element.54.r_ref.refs_2_, f32[4,272,128]{2,1,0:T(8,128)S(1)} %get-tuple-element.43.u_ref.refs_3_, ...), custom_call_target="tpu_custom_call" | custom-call | tf_op jit(solution)/shard_map/update/pallas_call | solution.py:546
Async XLA Ops:
  0.6 7.4 %copy-start.1 = (f32[8,64,128]{2,1,0:T(8,128)S(1)}, f32[8,64,128]{2,1,0:T(8,128)}, u32[]{:S(2)}) copy-start(f32[8,64,128]{2,1,0:T(8,128)} %cat_ref.1) | copy-start | bytes 786436
  0.6 7.4 %copy-start = (f32[4,256,128]{2,1,0:T(8,128)S(1)}, f32[4,256,128]{2,1,0:T(8,128)}, u32[]{:S(2)}) copy-start(f32[4,256,128]{2,1,0:T(8,128)} %c_ref.1) | copy-start | bytes 1572868
  2.7 7.5 %collective-permute-start.3 = (f32[2,256,128]{2,1,0:T(8,128)S(1)}, f32[2,256,128]{2,1,0:T(8,128)S(1)}, u32[]{:S(2)}, u32[]{:S(2)}) collective-permute-start(f32[2,256,128]{2,1,0:T(8,128)S(1)} %get-tuple-element.42), channel_id=1, source_target_pairs={{0,1},{1,0},{2,3},{3,2},{4,5},{5,4},{6,7},{7,6},{8,9},{9,8},{10,11... | collective-permute-start | bytes 786440 | tf_op jit(solution)/shard_map/ppermute | solution.py:567
  3.2 7.0 %collective-permute-start = (f32[2,8,128]{2,1,0:T(8,128)S(1)}, f32[2,8,128]{2,1,0:T(8,128)S(1)}, u32[]{:S(2)}, u32[]{:S(2)}) collective-permute-start(f32[2,8,128]{2,1,0:T(8,128)S(1)} %get-tuple-element.39), channel_id=1, source_target_pairs={{0,4},{4,0},{8,12},{12,8},{1,5},{5,1},{9,13},{13,9},{2,6},{6,2},{1... | collective-permute-start | bytes 24584 | tf_op jit(solution)/shard_map/ppermute | solution.py:567
  5.9 4.3 %collective-permute-start.1 = (f32[2,8,128]{2,1,0:T(8,128)S(1)}, f32[2,8,128]{2,1,0:T(8,128)S(1)}, u32[]{:S(2)}, u32[]{:S(2)}) collective-permute-start(f32[2,8,128]{2,1,0:T(8,128)S(1)} %get-tuple-element.40), channel_id=1, source_target_pairs={{4,8},{8,4},{5,9},{9,5},{6,10},{10,6},{7,11},{11,7},{20,24},{24,20... | collective-permute-start | bytes 24584 | tf_op jit(solution)/shard_map/ppermute | solution.py:567
  6.5 3.7 %collective-permute-start.2 = (f32[2,4,128]{2,1,0:T(4,128)S(1)}, f32[2,4,128]{2,1,0:T(4,128)S(1)}, u32[]{:S(2)}, u32[]{:S(2)}) collective-permute-start(f32[2,4,128]{2,1,0:T(4,128)S(1)} %get-tuple-element.41), channel_id=1, source_target_pairs={{0,2},{2,0},{1,3},{3,1},{4,6},{6,4},{5,7},{7,5},{8,10},{10,8},{9,1... | collective-permute-start | bytes 12296 | tf_op jit(solution)/shard_map/ppermute | solution.py:567
  13.1 9.1 %collective-permute-start.7 = (f32[256,128]{1,0:T(8,128)S(1)}, f32[256,128]{1,0:T(8,128)S(1)}, u32[]{:S(2)}, u32[]{:S(2)}) collective-permute-start(f32[256,128]{1,0:T(8,128)S(1)} %get-tuple-element.52), channel_id=1, source_target_pairs={{0,1},{1,0},{2,3},{3,2},{4,5},{5,4},{6,7},{7,6},{8,9},{9,8},{10,11... | collective-permute-start | bytes 393224 | tf_op jit(solution)/shard_map/ppermute | solution.py:567
  13.2 9.0 %collective-permute-start.4 = (f32[8,128]{1,0:T(8,128)S(1)}, f32[8,128]{1,0:T(8,128)S(1)}, u32[]{:S(2)}, u32[]{:S(2)}) collective-permute-start(f32[8,128]{1,0:T(8,128)S(1)} %get-tuple-element.49), channel_id=1, source_target_pairs={{0,4},{4,0},{8,12},{12,8},{1,5},{5,1},{9,13},{13,9},{2,6},{6,2},{1... | collective-permute-start | bytes 12296 | tf_op jit(solution)/shard_map/ppermute | solution.py:567
  17.9 4.3 %collective-permute-start.5 = (f32[8,128]{1,0:T(8,128)S(1)}, f32[8,128]{1,0:T(8,128)S(1)}, u32[]{:S(2)}, u32[]{:S(2)}) collective-permute-start(f32[8,128]{1,0:T(8,128)S(1)} %get-tuple-element.50), channel_id=1, source_target_pairs={{4,8},{8,4},{5,9},{9,5},{6,10},{10,6},{7,11},{11,7},{20,24},{24,20... | collective-permute-start | bytes 12296 | tf_op jit(solution)/shard_map/ppermute | solution.py:567
  18.6 3.7 %collective-permute-start.6 = (f32[4,128]{1,0:T(4,128)S(1)}, f32[4,128]{1,0:T(4,128)S(1)}, u32[]{:S(2)}, u32[]{:S(2)}) collective-permute-start(f32[4,128]{1,0:T(4,128)S(1)} %get-tuple-element.51), channel_id=1, source_target_pairs={{0,2},{2,0},{1,3},{3,1},{4,6},{6,4},{5,7},{7,5},{8,10},{10,8},{9,1... | collective-permute-start | bytes 6152 | tf_op jit(solution)/shard_map/ppermute | solution.py:567
  24.8 1.4 %collective-permute-start.8 = (f32[256,128]{1,0:T(8,128)S(1)}, f32[256,128]{1,0:T(8,128)S(1)}, u32[]{:S(2)}, u32[]{:S(2)}) collective-permute-start(f32[256,128]{1,0:T(8,128)S(1)} %get-tuple-element.59), channel_id=1, source_target_pairs={{0,1},{1,0},{2,3},{3,2},{4,5},{5,4},{6,7},{7,6},{8,9},{9,8},{10,11... | collective-permute-start | bytes 393224 | tf_op jit(solution)/shard_map/ppermute | solution.py:567

commit v6 on v5

--- a/solution.py
+++ b/solution.py
@@ -47,17 +47,39 @@
     lane = lanes()
     firsts, lasts = [], []
     for start in range(0, count, 128):
-        parts = [jnp.zeros((8, 128), F32), jnp.zeros((8, 128), F32)]
-        for i in range(min(128, count - start)):
-            turned = load(start + i)
-            if i:
-                turned = pltpu.roll(turned, i, 1)
-            here = (lane == i) | (lane == (i + 127) % 128)
-            parts[i % 2] = jnp.where(here, turned, parts[i % 2])
-        even = lane % 2 == 0
-        firsts.append(jnp.where(even, parts[0], parts[1]))
-        lasts.append(pltpu.roll(jnp.where(even, parts[1], parts[0]), 1, 1))
+        parts = [[], []]
+        for chunk in range(start, min(start + 128, count), 16):
+            sums = [None, None]
+            for i in range(chunk, min(chunk + 16, count)):
+                j = i - start
+                turned = load(i)
+                if j:
+                    turned = pltpu.roll(turned, j, 1)
+                turned = jnp.where((lane == j) | (lane == (j + 127) % 128), turned, 0.0)
+                sums[j % 2] = turned if sums[j % 2] is None else sums[j % 2] + turned
+            for kept, new in zip(parts, sums):
+                if new is not None:
+                    kept.append(new)
+        odd = tree(parts[1]) if parts[1] else jnp.zeros((8, 128), F32)
+        even = tree(parts[0])
+        here = lane % 2 == 0
+        firsts.append(jnp.where(here, even, odd))
+        lasts.append(pltpu.roll(jnp.where(here, odd, even), 1, 1))
     return jnp.concatenate(firsts, 0), jnp.concatenate(lasts, 0)
+
+
+def tree(values):
+    while len(values) > 1:
+        values = [a + b for a, b in zip(values[::2], values[1::2])] + values[len(values) // 2 * 2 :]
+    return values[0]
+
+
+def vreg_groups(z, per, size=8):
+    places = []
+    for i in range(z * per):
+        tier, at = i // per, 8 * (i % per)
+        places.append((i, (tier, slice(at, at + 8)), (tier, slice(at + 8, at + 16))))
+    return [places[k : k + size] for k in range(0, len(places), size)]
 
 
 def stage_columns(first, last):
@@ -159,10 +181,12 @@
         fill_sends(tier, row, sends, slot, columns, z, y)
 
 
-def inner_kernel(tall, x_ref, k_ref, c_ref, cat_ref, sel_in, band_in, flow_in, *refs):
-    r_ref, diag_ref, cz_ref, cs_ref, ce_ref, sel_ref, band_ref, flow_ref, sems = refs
+def inner_kernel(tall, x_ref, k_ref, c_in, cat_in, sel_in, band_in, flow_in, *refs):
+    r_ref, diag_ref, cz_ref, cs_ref, ce_ref, c_ref, cat_ref, sel_ref, band_ref, flow_ref, sems = refs
     z, y, _ = c_ref.shape
-    copies = start_all((sel_in, band_in, flow_in), (sel_ref, band_ref, flow_ref), sems)
+    copies = start_all(
+        (c_in, cat_in, sel_in, band_in, flow_in), (c_ref, cat_ref, sel_ref, band_ref, flow_ref), sems
+    )
     lane = lanes((tall, 128))
     row = rows((tall, 128))
     for i in range(z):
@@ -220,35 +244,34 @@
 
 def sweeps(field_ref, diag_ref, cs_ref, ce_ref, lev_ref, tall):
     z, y, _ = diag_ref.shape
-    tiles = y // tall
     row = rows((tall, 128))
 
     def tile(i, t):
         level = lev_ref[i, 0, t]
-
-        @pl.when(level > 1)
-        def _():
-            at = pl.multiple_of(t * tall, 8)
-            mid = pl.ds(at + 8, tall)
+        at = t * tall
+        mid = pl.ds(at + 8, tall)
+
+        def run(count):
             start = field_ref[i, mid, :]
             weight = damping / diag_ref[i, pl.ds(at, tall), :]
             north = jnp.where(row == 0, 0.0, cs_ref[i, pl.ds(at + 7, tall), :])
             south = jnp.where(row == tall - 1, 0.0, cs_ref[i, mid, :])
             east = ce_ref[i, pl.ds(at, tall), :]
-
-            def once(_, state):
+            state = start
+            for sweep in range(1, count + 1):
                 inner = north * pltpu.roll(state, 1, 0) + south * pltpu.roll(state, tall - 1, 0)
-                inner = inner + east * pltpu.roll(state, 127, 1) + pltpu.roll(east * state, 1, 1)
-                return (1.0 - damping) * state + (start + weight * inner)
-
-            field_ref[i, mid, :] = lax.fori_loop(1, jnp.minimum(level, 4), once, start)
+                inner = inner + (east * pltpu.roll(state, 127, 1) + pltpu.roll(east * state, 1, 1))
+                fresh = ((1.0 - damping) * state + start) + weight * inner
+                state = fresh if sweep < 3 else jnp.where(level > sweep, fresh, state)
+            field_ref[i, mid, :] = state
+
+        pl.when(level == 2)(functools.partial(run, 1))
+        pl.when(level > 2)(functools.partial(run, 3))
 
     def tier(i, carry):
-        def step(t, carry):
+        for t in range(y // tall):
             tile(i, t)
-            return carry
-
-        return lax.fori_loop(0, tiles, step, carry)
+        return carry
 
     lax.fori_loop(0, z, tier, 0)
 
@@ -262,10 +285,14 @@
     table = start_all((lev_in,), (lev_ref,), sems)
     for n, ref in enumerate(hz):
         p = jnp.where(low_side("gz", n), 0, z - 1)
-        face = vertical_ratio * harmonic(k_ref[p, pl.ds(8, y), :], ref[1])
-        czh_ref[n] = face
-        diag_in[p] = diag_in[p] + face
-        r_in[p] = r_in[p] + face * (ref[0] - x_ref[p, pl.ds(8, y), :])
+        for at in range(0, y, tall):
+            near, inside = slice(at, at + tall), slice(at + 8, at + 8 + tall)
+            face = vertical_ratio * harmonic(k_ref[p, inside, :], ref[1, near, :])
+            diag = diag_in[p, near, :] + face
+            r = r_in[p, near, :] + face * (ref[0, near, :] - x_ref[p, inside, :])
+            czh_ref[n, near, :] = face
+            diag_in[p, near, :] = diag
+            r_in[p, near, :] = r
     row8 = rows((8, 128))
     for n, ref in enumerate(hy):
         low = low_side("gy", n)
@@ -290,13 +317,13 @@
     edge = edge_lanes()
     clear_margins(u_ref)
     per = y // 8
-    for i in range(z * per):
-        at = (i // per, slice(8 * (i % per), 8 * (i % per) + 8))
-        diag = diag_in[at] + spread_columns(faces, edge, i)
-        r = r_in[at] + spread_columns(flux, edge, i)
-        diag_ref[at] = diag
-        r_ref[at] = r
-        u_ref[i // per, 8 + 8 * (i % per) : 16 + 8 * (i % per)] = r * (damping / diag)
+    for group in vreg_groups(z, per):
+        diags = [diag_in[at] + spread_columns(faces, edge, i) for i, at, _ in group]
+        values = [r_in[at] + spread_columns(flux, edge, i) for i, at, _ in group]
+        for (_, at, inside), diag, r in zip(group, diags, values):
+            diag_ref[at] = diag
+            r_ref[at] = r
+            u_ref[inside] = r * (damping / diag)
     table[0].wait()
     sweeps(u_ref, diag_ref, cs_ref, ce_ref, lev_ref, tall)
     tier, row, vreg = padded_access(u_ref)
@@ -359,11 +386,12 @@
     edge = edge_lanes()
     clear_margins(m_ref)
     per = y // 8
-    for i in range(z * per):
-        at = (i // per, slice(8 * (i % per), 8 * (i % per) + 8))
-        w = w_in[at] - spread_columns(flux, edge, i)
-        w_ref[at] = w
-        m_ref[i // per, 8 + 8 * (i % per) : 16 + 8 * (i % per)] = w * (damping / diag_ref[at])
+    for group in vreg_groups(z, per):
+        values = [w_in[at] - spread_columns(flux, edge, i) for i, at, _ in group]
+        weights = [damping / diag_ref[at] for _, at, _ in group]
+        for (_, at, inside), w, weight in zip(group, values, weights):
+            w_ref[at] = w
+            m_ref[inside] = w * weight
     table[0].wait()
     sweeps(m_ref, diag_ref, cs_ref, ce_ref, lev_ref, tall)
     tier, row, vreg = padded_access(m_ref)
@@ -444,11 +472,6 @@
     nx, ny, nz = sizes
     members = nx * ny * nz
     y_high = plan["y_low" if rounds[1] == 1 else "y_high"]
-
-    def tree(values):
-        while len(values) > 1:
-            values = [a + b for a, b in zip(values[::2], values[1::2])] + values[len(values) // 2 * 2 :]
-        return values[0]
 
     sums = tree([all_ref[d, plan["sums"], :] for d in range(members)])
     gamma, delta, cross, last = (sums[i : i + 1] for i in range(4))
@@ -493,19 +516,23 @@
         from_above = jnp.where(gy < ny - 1, all_ref[above, plan["y_low"], :], 0.0)
         row_flux.append(far * jnp.where(low, from_below, from_above))
     edge = edge_lanes()
+    near, far = (jnp.broadcast_to(v, (8, 128)) for v in (near, far))
     per = y // 8
     copies = []
+    batches = vreg_groups(z, per)
     for i in range(z):
-        inner = (i, slice(8, 8 + y))
-        for j in range(per):
-            at = (i, slice(8 * j, 8 * j + 8))
-            ro_ref[at] = r_ref[at] - near * w_ref[at] + (far * n_ref[at] - spread_columns(flux, edge, i * per + j))
+        for group in batches[i * len(batches) // z : (i + 1) * len(batches) // z]:
+            values = [
+                r_ref[at] - near * w_ref[at] + (far * n_ref[at] - spread_columns(flux, edge, j)) for j, at, _ in group
+            ]
+            fields = [x_ref[inside] + near * u_ref[inside] - far * m_ref[inside] for _, _, inside in group]
+            for (_, at, _), value, field in zip(group, values, fields):
+                ro_ref[at] = value
+                xo_ref[at] = field
         for n in range(rounds[1]):
             at, mask = border_rows(n, y)
             ro_ref[i, at, :] = ro_ref[i, at, :] - jnp.where(mask, row_flux[n][i : i + 1], 0.0)
-        copies += start_all((ro_ref.at[i],), (r_out.at[i],), sems.at[0, i : i + 1])
-        xo_ref[i] = x_ref[inner] + near * u_ref[inner] - far * m_ref[inner]
-        copies += start_all((xo_ref.at[i],), (x_out.at[i],), sems.at[1, i : i + 1])
+        copies += start_all((ro_ref.at[i], xo_ref.at[i]), (r_out.at[i], x_out.at[i]), sems.at[i])
     for copy in copies:
         copy.wait()
 
@@ -589,8 +616,15 @@
         [full, full, shape(max(z - 1, 1), y, x), shape(z, y + 8, x), full],
         [field, kappa, caloric_storage, dissipation_catalog, selector, width, microflow_flag],
         "inner",
-        [table(selector), table(width), table(microflow_flag), pltpu.SemaphoreType.DMA((3,))],
-        outer=(4, 5, 6),
+        [
+            full,
+            shape(*dissipation_catalog.shape),
+            table(selector),
+            table(width),
+            table(microflow_flag),
+            pltpu.SemaphoreType.DMA((5,)),
+        ],
+        outer=(2, 3, 4, 5, 6),
     )
     outs = call(
         functools.partial(border_kernel, rounds, tall),
@@ -634,7 +668,7 @@
             [jax.ShapeDtypeStruct((z, y, x), F32)] * 2,
             [every, field, r, u, w, m, n, cx, cy],
             "update",
-            [full, full, pltpu.SemaphoreType.DMA((2, z))],
+            [full, full, pltpu.SemaphoreType.DMA((z, 2))],
             out_specs=[hbm, hbm],
         )
     )

time: 41.5 us -> 40.6 us (0.978); the launches traced: 41.3 us -> 40.9 us
  waiting for transfers between devices: 2.57 us -> 1.87 us
  blocking collectives: 13.5 us -> 14.1 us
    ppermute x9, waiting for transfers between devices: 2.57 us -> 1.87 us  [swap(): got.append(lax.ppermute(faces.pop(0), axis, swap_pairs(axis, start)))]
    all_to_all x1, blocking collectives: 13.5 us -> 14.1 us  [body(): every = lax.all_to_all(parts, GRID_AXES, 0, 0, tiled=True)]
  transfers between devices with their start and end apart: 9 -> 9, of which waited for: 3 -> 3; matrix products, arithmetic and copies ran while one was open for 0% -> 0% of each run, Pallas kernels for 7% -> 8%
where the time goes in v6:
time: 40.6 us; the launch traced here: 40.9 us
  blocking collectives  14.1 us (35%)
  starting transfers between devices  12.6 us (31%)
  Pallas kernels  11.6 us (29%)
  waiting for transfers between devices  1.87 us (5%)
  between operations  0.72 us (2%)
    all_to_all x1, blocking collectives, body(): every = lax.all_to_all(parts, GRID_AXES, 0, 0, tiled=True)  14.1 us
    ppermute x9, starting transfers between devices, swap(): got.append(lax.ppermute(faces.pop(0), axis, swap_pairs(axis, start)))  12.6 us
    pallas_call x8, Pallas kernels, call(): pl.pallas_call(kernel, out_shape=outs, in_specs=specs, out_specs=out_spec...  11.6 us
    ppermute x9, waiting for transfers between devices, swap(): got.append(lax.ppermute(faces.pop(0), axis, swap_pairs(axis, start)))  1.87 us
  transfers between devices with their start and end apart: 9, of which 3 were waited for; matrix products, arithmetic and copies ran while one was open for 0% of the time, Pallas kernels for 8%

profile of v6, /device:TPU:0, one launch (start us, length us, event | category | flops | bytes accessed | tf_op | source)
XLA Modules:
  0.0 40.9 jit_solution(17379980386826109801)
XLA Ops:
  0.6 1.9 %faces.1 = (f32[4,272,128]{2,1,0:T(8,128)S(1)}, f32[4,272,128]{2,1,0:T(8,128)S(1)}, f32[2,8,128]{2,1,0:T(8,128)S(1)}, f32[2,8,128]{2,1,0:T(8,128)S(1)}, f32[2,4,...) custom-call(f32[4,256,128]{2,1,0:T(8,128)} %x_in.1, f32[4,256,128]{2,1,0:T(8,128)} %k_in.1), custom_call_target="tpu_custom_call" | custom-call | tf_op jit(solution)/shard_map/faces/pallas_call | solution.py:573
  2.6 0.6 %collective-permute-start.3 = (f32[2,256,128]{2,1,0:T(8,128)S(1)}, f32[2,256,128]{2,1,0:T(8,128)S(1)}, u32[]{:S(2)}, u32[]{:S(2)}) collective-permute-start(f32[2,256,128]{2,1,0:T(8,128)S(1)} %get-tuple-element.42), channel_id=1, source_target_pairs={{0,1},{1,0},{2,3},{3,2},{4,5},{5,4},{6,7},{7,6},{8,9},{9,8},{10,11... | collective-permute-start | bytes 786440 | tf_op jit(solution)/shard_map/ppermute | solution.py:594
  3.1 2.6 %collective-permute-start = (f32[2,8,128]{2,1,0:T(8,128)S(1)}, f32[2,8,128]{2,1,0:T(8,128)S(1)}, u32[]{:S(2)}, u32[]{:S(2)}) collective-permute-start(f32[2,8,128]{2,1,0:T(8,128)S(1)} %get-tuple-element.39), channel_id=1, source_target_pairs={{0,4},{4,0},{8,12},{12,8},{1,5},{5,1},{9,13},{13,9},{2,6},{6,2},{1... | collective-permute-start | bytes 24584 | tf_op jit(solution)/shard_map/ppermute | solution.py:594
  5.8 0.6 %collective-permute-start.1 = (f32[2,8,128]{2,1,0:T(8,128)S(1)}, f32[2,8,128]{2,1,0:T(8,128)S(1)}, u32[]{:S(2)}, u32[]{:S(2)}) collective-permute-start(f32[2,8,128]{2,1,0:T(8,128)S(1)} %get-tuple-element.40), channel_id=1, source_target_pairs={{4,8},{8,4},{5,9},{9,5},{6,10},{10,6},{7,11},{11,7},{20,24},{24,20... | collective-permute-start | bytes 24584 | tf_op jit(solution)/shard_map/ppermute | solution.py:594
  6.4 1.6 %collective-permute-start.2 = (f32[2,4,128]{2,1,0:T(4,128)S(1)}, f32[2,4,128]{2,1,0:T(4,128)S(1)}, u32[]{:S(2)}, u32[]{:S(2)}) collective-permute-start(f32[2,4,128]{2,1,0:T(4,128)S(1)} %get-tuple-element.41), channel_id=1, source_target_pairs={{0,2},{2,0},{1,3},{3,1},{4,6},{6,4},{5,7},{7,5},{8,10},{10,8},{9,1... | collective-permute-start | bytes 12296 | tf_op jit(solution)/shard_map/ppermute | solution.py:594
  8.0 1.9 %inner.1 = (f32[4,256,128]{2,1,0:T(8,128)S(1)}, f32[4,256,128]{2,1,0:T(8,128)S(1)}, f32[3,256,128]{2,1,0:T(8,128)S(1)}, f32[4,264,128]{2,1,0:T(8,128)S(1)}, f32[4,256,128]{2,1,0:T(8,128)S(1)}) custom-call(f32[4,272,128]{2,1,0:T(8,128)S(1)} %get-tuple-element.32.x_ref.refs_0_.refs_1_, f32[4,272,128]{2,1,0:T(8,128)S(1)} %get-tuple-element.33.k_ref.refs_1_, ...), custom_call_target="tpu_custom_call" | custom-call | tf_op jit(solution)/shard_map/inner/pallas_call | solution.py:573
  9.9 0.2 collective-permute-done.2.refs_10_
  10.1 0.0 collective-permute-done.refs_8_
  10.1 0.0 collective-permute-done.1.refs_9_
  10.1 0.0 collective-permute-done.3.refs_11_
  10.1 2.6 %border.1 = (f32[4,256,128]{2,1,0:T(8,128)S(1)}, f32[4,256,128]{2,1,0:T(8,128)S(1)}, f32[4,272,128]{2,1,0:T(8,128)S(1)}, f32[2,8,128]{2,1,0:T(8,128)S(1)}, f32[1...) custom-call(f32[4,272,128]{2,1,0:T(8,128)S(1)} %get-tuple-element.32, ...), custom_call_target="tpu_custom_call", output_to_operand_aliasing={{0}: (3, {}), {1}: (4, {})} | custom-call | tf_op jit(solution)/shard_map/border/pallas_call | solution.py:573
  12.7 0.1 collective-permute-start.7
  12.8 4.1 %collective-permute-start.4 = (f32[8,128]{1,0:T(8,128)S(1)}, f32[8,128]{1,0:T(8,128)S(1)}, u32[]{:S(2)}, u32[]{:S(2)}) collective-permute-start(f32[8,128]{1,0:T(8,128)S(1)} %get-tuple-element.49), channel_id=1, source_target_pairs={{0,4},{4,0},{8,12},{12,8},{1,5},{5,1},{9,13},{13,9},{2,6},{6,2},{1... | collective-permute-start | bytes 12296 | tf_op jit(solution)/shard_map/ppermute | solution.py:594
  16.9 0.6 %collective-permute-start.5 = (f32[8,128]{1,0:T(8,128)S(1)}, f32[8,128]{1,0:T(8,128)S(1)}, u32[]{:S(2)}, u32[]{:S(2)}) collective-permute-start(f32[8,128]{1,0:T(8,128)S(1)} %get-tuple-element.50), channel_id=1, source_target_pairs={{4,8},{8,4},{5,9},{9,5},{6,10},{10,6},{7,11},{11,7},{20,24},{24,20... | collective-permute-start | bytes 12296 | tf_op jit(solution)/shard_map/ppermute | solution.py:594
  17.6 2.3 %collective-permute-start.6 = (f32[4,128]{1,0:T(4,128)S(1)}, f32[4,128]{1,0:T(4,128)S(1)}, u32[]{:S(2)}, u32[]{:S(2)}) collective-permute-start(f32[4,128]{1,0:T(4,128)S(1)} %get-tuple-element.51), channel_id=1, source_target_pairs={{0,2},{2,0},{1,3},{3,1},{4,6},{6,4},{5,7},{7,5},{8,10},{10,8},{9,1... | collective-permute-start | bytes 6152 | tf_op jit(solution)/shard_map/ppermute | solution.py:594
  19.9 0.5 %apply.1.refs_0_ = f32[4,256,128]{2,1,0:T(8,128)S(1)} custom-call(f32[4,272,128]{2,1,0:T(8,128)S(1)} %get-tuple-element.43.u_ref.refs_3_, f32[4,256,128]{2,1,0:T(8,128)S(1)} %get-tuple-element.44.diag_ref.refs_1_, f32[3,256,128]{2,1,0:T(8,128)S(1)} %get-tuple-element.45.cz_ref, f32[4,264,128]{2,1,0:T(8,128)S(1)} %get-tuple-element.37.refs_5_.cs_ref.refs_2_, ...), custom_call_target="tpu_custom_call" | custom-call | tf_op jit(solution)/shard_map/apply/pallas_call | solution.py:573
  20.4 1.0 %collective-permute-done.6.refs_10_ = f32[4,128]{1,0:T(4,128)S(1)} collective-permute-done((f32[4,128]{1,0:T(4,128)S(1)}, f32[4,128]{1,0:T(4,128)S(1)}, u32[]{:S(2)}, u32[]{:S(2)}) %collective-permute-start.6) | collective-permute-done | bytes 2080 | tf_op jit(solution)/shard_map/ppermute | solution.py:594
  21.4 0.0 collective-permute-done.4.refs_8_
  21.4 0.0 collective-permute-done.5.refs_9_
  21.4 0.0 collective-permute-done.7.refs_11_
  21.4 2.3 %smooth.1 = (f32[4,256,128]{2,1,0:T(8,128)S(1)}, f32[4,272,128]{2,1,0:T(8,128)S(1)}, f32[24,128]{1,0:T(8,128)S(1)}, f32[256,128]{1,0:T(8,128)S(1)}) custom-call(f32[4,256,128]{2,1,0:T(8,128)S(1)} %apply.1.refs_0_, f32[4,256,128]{2,1,0:T(8,128)S(1)} %get-tuple-element.44.diag_ref.refs_1_, ...), custom_call_target="tpu_custom_call", output_to_operand_aliasing={{0}: (0, {})} | custom-call | tf_op jit(solution)/shard_map/smooth/pallas_call | solution.py:573
  23.8 0.1 collective-permute-start.8
  23.9 0.7 %sums.1 = (f32[4,256,128]{2,1,0:T(8,128)S(1)}, f32[4,8,128]{2,1,0:T(8,128)S(1)}) custom-call(f32[4,272,128]{2,1,0:T(8,128)S(1)} %get-tuple-element.53.m_ref.refs_1_.refs_5_, f32[4,272,128]{2,1,0:T(8,128)S(1)} %get-tuple-element.43.u_ref.refs_3_, f32[4,256,128]{2,1,0:T(8,128)S(1)} %get-tuple-element.54.r_ref.refs_2_, ...), custom_call_target="tpu_custom_call" | custom-call | tf_op jit(solution)/shard_map/sums/pallas_call | solution.py:573
  24.5 0.6 %collective-permute-done.8.refs_5_ = f32[256,128]{1,0:T(8,128)S(1)} collective-permute-done((f32[256,128]{1,0:T(8,128)S(1)}, f32[256,128]{1,0:T(8,128)S(1)}, u32[]{:S(2)}, u32[]{:S(2)}) %collective-permute-start.8) | collective-permute-done | bytes 131104 | tf_op jit(solution)/shard_map/ppermute | solution.py:594
  25.2 0.1 finish.1
  25.3 14.1 %all_to_all.5.refs_0_ = f32[16,24,128]{2,1,0:T(8,128)S(1)} all-to-all(f32[16,24,128]{2,1,0:T(8,128)S(1)} %get-tuple-element.60), channel_id=1, replica_groups=mesh['groups'=2,'gx'=4,'gy'=2,'gz'=2] {'gx','gy','gz'}, dimensions={0} | all-to-all | bytes 393216 | tf_op jit(solution)/shard_map/all_to_all | solution.py:664
  39.4 1.5 %update.1 = (f32[4,256,128]{2,1,0:T(8,128)}, f32[4,256,128]{2,1,0:T(8,128)}) custom-call(f32[16,24,128]{2,1,0:T(8,128)S(1)} %all_to_all.5.refs_0_, f32[4,272,128]{2,1,0:T(8,128)S(1)} %get-tuple-element.32.x_ref.refs_0_.refs_1_, f32[4,256,128]{2,1,0:T(8,128)S(1)} %get-tuple-element.54.r_ref.refs_2_, f32[4,272,128]{2,1,0:T(8,128)S(1)} %get-tuple-element.43.u_ref.refs_3_, ...), custom_call_target="tpu_custom_call" | custom-call | tf_op jit(solution)/shard_map/update/pallas_call | solution.py:573
Async XLA Ops:
  2.6 7.5 %collective-permute-start.3 = (f32[2,256,128]{2,1,0:T(8,128)S(1)}, f32[2,256,128]{2,1,0:T(8,128)S(1)}, u32[]{:S(2)}, u32[]{:S(2)}) collective-permute-start(f32[2,256,128]{2,1,0:T(8,128)S(1)} %get-tuple-element.42), channel_id=1, source_target_pairs={{0,1},{1,0},{2,3},{3,2},{4,5},{5,4},{6,7},{7,6},{8,9},{9,8},{10,11... | collective-permute-start | bytes 786440 | tf_op jit(solution)/shard_map/ppermute | solution.py:594
  3.1 7.0 %collective-permute-start = (f32[2,8,128]{2,1,0:T(8,128)S(1)}, f32[2,8,128]{2,1,0:T(8,128)S(1)}, u32[]{:S(2)}, u32[]{:S(2)}) collective-permute-start(f32[2,8,128]{2,1,0:T(8,128)S(1)} %get-tuple-element.39), channel_id=1, source_target_pairs={{0,4},{4,0},{8,12},{12,8},{1,5},{5,1},{9,13},{13,9},{2,6},{6,2},{1... | collective-permute-start | bytes 24584 | tf_op jit(solution)/shard_map/ppermute | solution.py:594
  5.8 4.3 %collective-permute-start.1 = (f32[2,8,128]{2,1,0:T(8,128)S(1)}, f32[2,8,128]{2,1,0:T(8,128)S(1)}, u32[]{:S(2)}, u32[]{:S(2)}) collective-permute-start(f32[2,8,128]{2,1,0:T(8,128)S(1)} %get-tuple-element.40), channel_id=1, source_target_pairs={{4,8},{8,4},{5,9},{9,5},{6,10},{10,6},{7,11},{11,7},{20,24},{24,20... | collective-permute-start | bytes 24584 | tf_op jit(solution)/shard_map/ppermute | solution.py:594
  6.4 3.7 %collective-permute-start.2 = (f32[2,4,128]{2,1,0:T(4,128)S(1)}, f32[2,4,128]{2,1,0:T(4,128)S(1)}, u32[]{:S(2)}, u32[]{:S(2)}) collective-permute-start(f32[2,4,128]{2,1,0:T(4,128)S(1)} %get-tuple-element.41), channel_id=1, source_target_pairs={{0,2},{2,0},{1,3},{3,1},{4,6},{6,4},{5,7},{7,5},{8,10},{10,8},{9,1... | collective-permute-start | bytes 12296 | tf_op jit(solution)/shard_map/ppermute | solution.py:594
  12.7 8.7 %collective-permute-start.7 = (f32[256,128]{1,0:T(8,128)S(1)}, f32[256,128]{1,0:T(8,128)S(1)}, u32[]{:S(2)}, u32[]{:S(2)}) collective-permute-start(f32[256,128]{1,0:T(8,128)S(1)} %get-tuple-element.52), channel_id=1, source_target_pairs={{0,1},{1,0},{2,3},{3,2},{4,5},{5,4},{6,7},{7,6},{8,9},{9,8},{10,11... | collective-permute-start | bytes 393224 | tf_op jit(solution)/shard_map/ppermute | solution.py:594
  12.8 8.7 %collective-permute-start.4 = (f32[8,128]{1,0:T(8,128)S(1)}, f32[8,128]{1,0:T(8,128)S(1)}, u32[]{:S(2)}, u32[]{:S(2)}) collective-permute-start(f32[8,128]{1,0:T(8,128)S(1)} %get-tuple-element.49), channel_id=1, source_target_pairs={{0,4},{4,0},{8,12},{12,8},{1,5},{5,1},{9,13},{13,9},{2,6},{6,2},{1... | collective-permute-start | bytes 12296 | tf_op jit(solution)/shard_map/ppermute | solution.py:594
  16.9 4.5 %collective-permute-start.5 = (f32[8,128]{1,0:T(8,128)S(1)}, f32[8,128]{1,0:T(8,128)S(1)}, u32[]{:S(2)}, u32[]{:S(2)}) collective-permute-start(f32[8,128]{1,0:T(8,128)S(1)} %get-tuple-element.50), channel_id=1, source_target_pairs={{4,8},{8,4},{5,9},{9,5},{6,10},{10,6},{7,11},{11,7},{20,24},{24,20... | collective-permute-start | bytes 12296 | tf_op jit(solution)/shard_map/ppermute | solution.py:594
  17.6 3.9 %collective-permute-start.6 = (f32[4,128]{1,0:T(4,128)S(1)}, f32[4,128]{1,0:T(4,128)S(1)}, u32[]{:S(2)}, u32[]{:S(2)}) collective-permute-start(f32[4,128]{1,0:T(4,128)S(1)} %get-tuple-element.51), channel_id=1, source_target_pairs={{0,2},{2,0},{1,3},{3,1},{4,6},{6,4},{5,7},{7,5},{8,10},{10,8},{9,1... | collective-permute-start | bytes 6152 | tf_op jit(solution)/shard_map/ppermute | solution.py:594
  23.8 1.4 %collective-permute-start.8 = (f32[256,128]{1,0:T(8,128)S(1)}, f32[256,128]{1,0:T(8,128)S(1)}, u32[]{:S(2)}, u32[]{:S(2)}) collective-permute-start(f32[256,128]{1,0:T(8,128)S(1)} %get-tuple-element.59), channel_id=1, source_target_pairs={{0,1},{1,0},{2,3},{3,2},{4,5},{5,4},{6,7},{7,6},{8,9},{9,8},{10,11... | collective-permute-start | bytes 393224 | tf_op jit(solution)/shard_map/ppermute | solution.py:594

commit v7 on v6

--- a/solution.py
+++ b/solution.py
@@ -181,11 +181,14 @@
         fill_sends(tier, row, sends, slot, columns, z, y)
 
 
-def inner_kernel(tall, x_ref, k_ref, c_in, cat_in, sel_in, band_in, flow_in, *refs):
-    r_ref, diag_ref, cz_ref, cs_ref, ce_ref, c_ref, cat_ref, sel_ref, band_ref, flow_ref, sems = refs
+def inner_kernel(tall, x_ref, k_ref, c_in, cat_in, sel_in, band_in, flow_in, lev_in, *refs):
+    r_ref, diag_ref, cz_ref, cs_ref, ce_ref, mask_ref, c_ref, cat_ref, *tables, sems = refs
+    sel_ref, band_ref, flow_ref, lev_ref = tables
     z, y, _ = c_ref.shape
     copies = start_all(
-        (c_in, cat_in, sel_in, band_in, flow_in), (c_ref, cat_ref, sel_ref, band_ref, flow_ref), sems
+        (c_in, cat_in, sel_in, band_in, flow_in, lev_in),
+        (c_ref, cat_ref, *tables),
+        sems,
     )
     lane = lanes((tall, 128))
     row = rows((tall, 128))
@@ -208,6 +211,16 @@
     lax.fori_loop(0, y // tall, faces, 0)
     for copy in copies:
         copy.wait()
+
+    tiles = y // tall
+    for word in range(mask_ref.shape[1]):
+        few, many = jnp.int32(0), jnp.int32(0)
+        for number in range(16 * word, min(16 * word + 16, z * tiles)):
+            level = lev_ref[number // tiles, 0, number % tiles]
+            few = few + jnp.where(level == 2, 1 << (number - 16 * word), 0)
+            many = many + jnp.where(level > 2, 1 << (number - 16 * word), 0)
+        mask_ref[0, word] = jnp.full((8, 128), few.astype(F32))
+        mask_ref[1, word] = jnp.full((8, 128), many.astype(F32))
 
     def rest(t, carry):
         at = pl.multiple_of(t * tall, 8)
@@ -242,47 +255,64 @@
     lax.fori_loop(0, y // tall, rest, 0)
 
 
-def sweeps(field_ref, diag_ref, cs_ref, ce_ref, lev_ref, tall):
+def list_tiles(mask_ref, todo_ref, tiles):
+    counts = []
+    for kind in range(2):
+        count = jnp.int32(0)
+        for word in range(mask_ref.shape[1]):
+            mask = jnp.max(mask_ref[kind, word]).astype(jnp.int32)
+            for bit in range(min(16, tiles - 16 * word)):
+                todo_ref[kind, count] = 16 * word + bit
+                count = count + ((mask >> bit) & 1)
+        counts.append(count)
+    return counts
+
+
+def sweeps(field_ref, diag_ref, cs_ref, ce_ref, todo_ref, counts, tall):
     z, y, _ = diag_ref.shape
-    row = rows((tall, 128))
-
-    def tile(i, t):
-        level = lev_ref[i, 0, t]
-        at = t * tall
-        mid = pl.ds(at + 8, tall)
-
-        def run(count):
+    tiles = y // tall
+
+    def run(count):
+        def tile(n, carry):
+            number = todo_ref[min(count, 2) - 1, n]
+            i, t = lax.div(number, tiles), lax.rem(number, tiles)
+            at = pl.multiple_of(t * tall, 8)
+            mid = pl.ds(at + 8, tall)
             start = field_ref[i, mid, :]
             weight = damping / diag_ref[i, pl.ds(at, tall), :]
-            north = jnp.where(row == 0, 0.0, cs_ref[i, pl.ds(at + 7, tall), :])
-            south = jnp.where(row == tall - 1, 0.0, cs_ref[i, mid, :])
+            first = rows((8, 128)) == 0
+            final = rows((8, 128)) == 7
+            north = cs_ref[i, pl.ds(at + 7, tall), :]
+            north = jnp.concatenate([jnp.where(first, 0.0, north[:8]), north[8:]], 0)
+            south = cs_ref[i, mid, :]
+            south = jnp.concatenate([south[:-8], jnp.where(final, 0.0, south[-8:])], 0)
             east = ce_ref[i, pl.ds(at, tall), :]
             state = start
             for sweep in range(1, count + 1):
-                inner = north * pltpu.roll(state, 1, 0) + south * pltpu.roll(state, tall - 1, 0)
-                inner = inner + (east * pltpu.roll(state, 127, 1) + pltpu.roll(east * state, 1, 1))
-                fresh = ((1.0 - damping) * state + start) + weight * inner
-                state = fresh if sweep < 3 else jnp.where(level > sweep, fresh, state)
+                if sweep == 1:
+                    above, below = field_ref[i, pl.ds(at + 7, tall), :], field_ref[i, pl.ds(at + 9, tall), :]
+                else:
+                    above, below = pltpu.roll(state, 1, 0), pltpu.roll(state, tall - 1, 0)
+                inner = (north * above + south * below) + (
+                    east * pltpu.roll(state, 127, 1) + pltpu.roll(east * state, 1, 1)
+                )
+                state = ((1.0 - damping) * state + start) + weight * inner
             field_ref[i, mid, :] = state
-
-        pl.when(level == 2)(functools.partial(run, 1))
-        pl.when(level > 2)(functools.partial(run, 3))
-
-    def tier(i, carry):
-        for t in range(y // tall):
-            tile(i, t)
-        return carry
-
-    lax.fori_loop(0, z, tier, 0)
+            return carry
+
+        lax.fori_loop(0, counts[min(count, 2) - 1], tile, 0)
+
+    run(1)
+    run(3)
 
 
 def border_kernel(rounds, tall, *refs):
-    (x_ref, k_ref, own_ref, r_in, diag_in, cs_ref, ce_ref, lev_in), refs = refs[:8], refs[8:]
+    (x_ref, k_ref, own_ref, r_in, diag_in, cs_ref, ce_ref, mask_ref), refs = refs[:8], refs[8:]
     (hx, hy, hz), refs = regroup(refs, rounds)
     (r_ref, diag_ref, u_ref, cx_ref, cy_ref, czh_ref), refs = refs[:6], refs[6:]
-    sends, (lev_ref, sems) = regroup(refs, rounds)
+    sends, (todo_ref,) = regroup(refs, rounds)
     z, y, _ = r_ref.shape
-    table = start_all((lev_in,), (lev_ref,), sems)
+    counts = list_tiles(mask_ref, todo_ref, z * (y // tall))
     for n, ref in enumerate(hz):
         p = jnp.where(low_side("gz", n), 0, z - 1)
         for at in range(0, y, tall):
@@ -324,8 +354,7 @@
             diag_ref[at] = diag
             r_ref[at] = r
             u_ref[inside] = r * (damping / diag)
-    table[0].wait()
-    sweeps(u_ref, diag_ref, cs_ref, ce_ref, lev_ref, tall)
+    sweeps(u_ref, diag_ref, cs_ref, ce_ref, todo_ref, counts, tall)
     tier, row, vreg = padded_access(u_ref)
     fill_sends(tier, row, sends, None, pack_columns(vreg, z * per), z, y)
 
@@ -371,11 +400,11 @@
 
 
 def smooth_kernel(rounds, tall, *refs):
-    (w_in, diag_ref, cs_ref, ce_ref, cx_ref, cy_ref, czh_ref, lev_in), refs = refs[:8], refs[8:]
+    (w_in, diag_ref, cs_ref, ce_ref, cx_ref, cy_ref, czh_ref, mask_ref), refs = refs[:8], refs[8:]
     halos, refs = regroup(refs, rounds)
-    w_ref, m_ref, face_ref, *send_refs, lev_ref, sems = refs
+    w_ref, m_ref, face_ref, *send_refs, todo_ref = refs
     z, y, _ = w_ref.shape
-    table = start_all((lev_in,), (lev_ref,), sems)
+    counts = list_tiles(mask_ref, todo_ref, z * (y // tall))
     subtract_tiers(w_in, halos[2], czh_ref)
     for n, ref in enumerate(halos[1]):
         at, mask = border_rows(n, y)
@@ -392,8 +421,7 @@
         for (_, at, inside), w, weight in zip(group, values, weights):
             w_ref[at] = w
             m_ref[inside] = w * weight
-    table[0].wait()
-    sweeps(m_ref, diag_ref, cs_ref, ce_ref, lev_ref, tall)
+    sweeps(m_ref, diag_ref, cs_ref, ce_ref, todo_ref, counts, tall)
     tier, row, vreg = padded_access(m_ref)
     for n, ref in enumerate(send_refs):
         ref[...] = tier(jnp.where(low_side("gz", n), 0, z - 1))
@@ -598,6 +626,8 @@
     levels = jnp.swapaxes(refine_depth, 1, 2)
     width = jnp.swapaxes(border_band_width, 0, 1)
 
+    todo = pltpu.SMEM((2, z * (y // tall) + 1), jnp.int32)
+
     def table(v):
         return pltpu.SMEM(v.shape, v.dtype)
 
@@ -611,10 +641,10 @@
     )
     (field, kappa), outs = outs[:2], outs[2:]
     own, halos = outs[sends], swap(outs[:sends])
-    r, diag, cz, cs, ce = call(
+    r, diag, cz, cs, ce, masks = call(
         functools.partial(inner_kernel, tall),
-        [full, full, shape(max(z - 1, 1), y, x), shape(z, y + 8, x), full],
-        [field, kappa, caloric_storage, dissipation_catalog, selector, width, microflow_flag],
+        [full, full, shape(max(z - 1, 1), y, x), shape(z, y + 8, x), full, shape(2, -(-z * (y // tall) // 16), 8, 128)],
+        [field, kappa, caloric_storage, dissipation_catalog, selector, width, microflow_flag, levels],
         "inner",
         [
             full,
@@ -622,19 +652,19 @@
             table(selector),
             table(width),
             table(microflow_flag),
-            pltpu.SemaphoreType.DMA((5,)),
+            table(levels),
+            pltpu.SemaphoreType.DMA((6,)),
         ],
-        outer=(2, 3, 4, 5, 6),
+        outer=(2, 3, 4, 5, 6, 7),
     )
     outs = call(
         functools.partial(border_kernel, rounds, tall),
         [full, full, tall_field, shape(2, 8 * groups, x), shape(rounds[1], z, x), shape(rounds[2], y, x)]
         + face_shapes(()),
-        [field, kappa, own, r, diag, cs, ce, levels] + halos,
+        [field, kappa, own, r, diag, cs, ce, masks] + halos,
         "border",
-        [table(levels), pltpu.SemaphoreType.DMA((1,))],
+        [todo],
         alias={3: 0, 4: 1},
-        outer=(7,),
     )
     r, diag, u, cx, cy, czh = outs[:6]
     halos = swap(outs[6:])
@@ -642,11 +672,10 @@
     outs = call(
         functools.partial(smooth_kernel, rounds, tall),
         [full, tall_field, shape(height, x)] + [shape(y, x)] * rounds[2],
-        [w, diag, cs, ce, cx, cy, czh, levels] + halos,
+        [w, diag, cs, ce, cx, cy, czh, masks] + halos,
         "smooth",
-        [table(levels), pltpu.SemaphoreType.DMA((1,))],
+        [todo],
         alias={0: 0},
-        outer=(7,),
     )
     w, m, faces = outs[:3]
     halos = swap(outs[3:], GRID_AXES[2:])

time: 40.6 us -> 39.3 us (0.968); the launches traced: 40.9 us -> 39 us
  blocking collectives: 14.1 us -> 13 us
  starting transfers between devices: 12.6 us -> 11.6 us
  waiting for transfers between devices: 1.87 us -> 2.76 us
  Pallas kernels: 11.6 us -> 11 us
    all_to_all x1, blocking collectives: 14.1 us -> 13 us  [body(): every = lax.all_to_all(parts, GRID_AXES, 0, 0, tiled=True)]
    ppermute x9, starting transfers between devices: 12.6 us -> 11.6 us  [swap(): got.append(lax.ppermute(faces.pop(0), axis, swap_pairs(axis, start)))]
    ppermute x9, waiting for transfers between devices: 1.87 us -> 2.76 us  [swap(): got.append(lax.ppermute(faces.pop(0), axis, swap_pairs(axis, start)))]
    pallas_call x8, Pallas kernels: 11.6 us -> 11 us  [call(): pl.pallas_call(kernel, out_shape=outs, in_specs=specs, out_specs=out_spec...]
where the time goes in v7:
time: 39.3 us; the launch traced here: 39 us
  blocking collectives  13 us (33%)
  starting transfers between devices  11.6 us (30%)
  Pallas kernels  11 us (28%)
  waiting for transfers between devices  2.76 us (7%)
  between operations  0.71 us (2%)
    all_to_all x1, blocking collectives, body(): every = lax.all_to_all(parts, GRID_AXES, 0, 0, tiled=True)  13 us
    ppermute x9, starting transfers between devices, swap(): got.append(lax.ppermute(faces.pop(0), axis, swap_pairs(axis, start)))  11.6 us
    pallas_call x8, Pallas kernels, call(): pl.pallas_call(kernel, out_shape=outs, in_specs=specs, out_specs=out_spec...  11 us
    ppermute x9, waiting for transfers between devices, swap(): got.append(lax.ppermute(faces.pop(0), axis, swap_pairs(axis, start)))  2.76 us
  transfers between devices with their start and end apart: 9, of which 3 were waited for; matrix products, arithmetic and copies ran while one was open for 0% of the time, Pallas kernels for 8%

profile of v7, /device:TPU:0, one launch (start us, length us, event | category | flops | bytes accessed | tf_op | source)
XLA Modules:
  0.0 39.0 jit_solution(4201847733139822117)
XLA Ops:
  0.6 1.9 %faces.1 = (f32[4,272,128]{2,1,0:T(8,128)S(1)}, f32[4,272,128]{2,1,0:T(8,128)S(1)}, f32[2,8,128]{2,1,0:T(8,128)S(1)}, f32[2,8,128]{2,1,0:T(8,128)S(1)}, f32[2,4,...) custom-call(f32[4,256,128]{2,1,0:T(8,128)} %x_in.1, f32[4,256,128]{2,1,0:T(8,128)} %k_in.1), custom_call_target="tpu_custom_call" | custom-call | tf_op jit(solution)/shard_map/faces/pallas_call | solution.py:601
  2.6 0.6 %collective-permute-start.3 = (f32[2,256,128]{2,1,0:T(8,128)S(1)}, f32[2,256,128]{2,1,0:T(8,128)S(1)}, u32[]{:S(2)}, u32[]{:S(2)}) collective-permute-start(f32[2,256,128]{2,1,0:T(8,128)S(1)} %get-tuple-element.44), channel_id=1, source_target_pairs={{0,1},{1,0},{2,3},{3,2},{4,5},{5,4},{6,7},{7,6},{8,9},{9,8},{10,11... | collective-permute-start | bytes 786440 | tf_op jit(solution)/shard_map/ppermute | solution.py:622
  3.1 2.6 %collective-permute-start = (f32[2,8,128]{2,1,0:T(8,128)S(1)}, f32[2,8,128]{2,1,0:T(8,128)S(1)}, u32[]{:S(2)}, u32[]{:S(2)}) collective-permute-start(f32[2,8,128]{2,1,0:T(8,128)S(1)} %get-tuple-element.41), channel_id=1, source_target_pairs={{0,4},{4,0},{8,12},{12,8},{1,5},{5,1},{9,13},{13,9},{2,6},{6,2},{1... | collective-permute-start | bytes 24584 | tf_op jit(solution)/shard_map/ppermute | solution.py:622
  5.8 0.6 %collective-permute-start.1 = (f32[2,8,128]{2,1,0:T(8,128)S(1)}, f32[2,8,128]{2,1,0:T(8,128)S(1)}, u32[]{:S(2)}, u32[]{:S(2)}) collective-permute-start(f32[2,8,128]{2,1,0:T(8,128)S(1)} %get-tuple-element.42), channel_id=1, source_target_pairs={{4,8},{8,4},{5,9},{9,5},{6,10},{10,6},{7,11},{11,7},{20,24},{24,20... | collective-permute-start | bytes 24584 | tf_op jit(solution)/shard_map/ppermute | solution.py:622
  6.4 1.6 %collective-permute-start.2 = (f32[2,4,128]{2,1,0:T(4,128)S(1)}, f32[2,4,128]{2,1,0:T(4,128)S(1)}, u32[]{:S(2)}, u32[]{:S(2)}) collective-permute-start(f32[2,4,128]{2,1,0:T(4,128)S(1)} %get-tuple-element.43), channel_id=1, source_target_pairs={{0,2},{2,0},{1,3},{3,1},{4,6},{6,4},{5,7},{7,5},{8,10},{10,8},{9,1... | collective-permute-start | bytes 12296 | tf_op jit(solution)/shard_map/ppermute | solution.py:622
  8.0 2.0 %inner.1 = (f32[4,256,128]{2,1,0:T(8,128)S(1)}, f32[4,256,128]{2,1,0:T(8,128)S(1)}, f32[3,256,128]{2,1,0:T(8,128)S(1)}, f32[4,264,128]{2,1,0:T(8,128)S(1)}, f32[...) custom-call(f32[4,272,128]{2,1,0:T(8,128)S(1)} %get-tuple-element.33.x_ref.refs_0_.refs_1_, ...), custom_call_target="tpu_custom_call" | custom-call | tf_op jit(solution)/shard_map/inner/pallas_call | solution.py:601
  10.0 0.1 collective-permute-done.2.refs_10_
  10.1 0.0 collective-permute-done.refs_8_
  10.1 0.0 collective-permute-done.1.refs_9_
  10.1 0.0 collective-permute-done.3.refs_11_
  10.1 2.3 %border.1 = (f32[4,256,128]{2,1,0:T(8,128)S(1)}, f32[4,256,128]{2,1,0:T(8,128)S(1)}, f32[4,272,128]{2,1,0:T(8,128)S(1)}, f32[2,8,128]{2,1,0:T(8,128)S(1)}, f32[1...) custom-call(f32[4,272,128]{2,1,0:T(8,128)S(1)} %get-tuple-element.33, ...), custom_call_target="tpu_custom_call", output_to_operand_aliasing={{0}: (3, {}), {1}: (4, {})} | custom-call | tf_op jit(solution)/shard_map/border/pallas_call | solution.py:601
  12.4 0.0 collective-permute-start.7
  12.4 4.4 %collective-permute-start.4 = (f32[8,128]{1,0:T(8,128)S(1)}, f32[8,128]{1,0:T(8,128)S(1)}, u32[]{:S(2)}, u32[]{:S(2)}) collective-permute-start(f32[8,128]{1,0:T(8,128)S(1)} %get-tuple-element.51), channel_id=1, source_target_pairs={{0,4},{4,0},{8,12},{12,8},{1,5},{5,1},{9,13},{13,9},{2,6},{6,2},{1... | collective-permute-start | bytes 12296 | tf_op jit(solution)/shard_map/ppermute | solution.py:622
  16.8 0.6 %collective-permute-start.5 = (f32[8,128]{1,0:T(8,128)S(1)}, f32[8,128]{1,0:T(8,128)S(1)}, u32[]{:S(2)}, u32[]{:S(2)}) collective-permute-start(f32[8,128]{1,0:T(8,128)S(1)} %get-tuple-element.52), channel_id=1, source_target_pairs={{4,8},{8,4},{5,9},{9,5},{6,10},{10,6},{7,11},{11,7},{20,24},{24,20... | collective-permute-start | bytes 12296 | tf_op jit(solution)/shard_map/ppermute | solution.py:622
  17.4 1.1 %collective-permute-start.6 = (f32[4,128]{1,0:T(4,128)S(1)}, f32[4,128]{1,0:T(4,128)S(1)}, u32[]{:S(2)}, u32[]{:S(2)}) collective-permute-start(f32[4,128]{1,0:T(4,128)S(1)} %get-tuple-element.53), channel_id=1, source_target_pairs={{0,2},{2,0},{1,3},{3,1},{4,6},{6,4},{5,7},{7,5},{8,10},{10,8},{9,1... | collective-permute-start | bytes 6152 | tf_op jit(solution)/shard_map/ppermute | solution.py:622
  18.6 0.5 %apply.1.refs_0_ = f32[4,256,128]{2,1,0:T(8,128)S(1)} custom-call(f32[4,272,128]{2,1,0:T(8,128)S(1)} %get-tuple-element.45.u_ref.refs_3_, f32[4,256,128]{2,1,0:T(8,128)S(1)} %get-tuple-element.46.diag_ref.refs_1_, f32[3,256,128]{2,1,0:T(8,128)S(1)} %get-tuple-element.47.cz_ref, f32[4,264,128]{2,1,0:T(8,128)S(1)} %get-tuple-element.38.refs_5_.cs_ref.refs_2_, ...), custom_call_target="tpu_custom_call" | custom-call | tf_op jit(solution)/shard_map/apply/pallas_call | solution.py:601
  19.1 2.0 %collective-permute-done.6.refs_10_ = f32[4,128]{1,0:T(4,128)S(1)} collective-permute-done((f32[4,128]{1,0:T(4,128)S(1)}, f32[4,128]{1,0:T(4,128)S(1)}, u32[]{:S(2)}, u32[]{:S(2)}) %collective-permute-start.6) | collective-permute-done | bytes 2080 | tf_op jit(solution)/shard_map/ppermute | solution.py:622
  21.1 0.0 collective-permute-done.4.refs_8_
  21.1 0.0 collective-permute-done.5.refs_9_
  21.1 0.0 collective-permute-done.7.refs_11_
  21.1 2.0 %smooth.1 = (f32[4,256,128]{2,1,0:T(8,128)S(1)}, f32[4,272,128]{2,1,0:T(8,128)S(1)}, f32[24,128]{1,0:T(8,128)S(1)}, f32[256,128]{1,0:T(8,128)S(1)}) custom-call(f32[4,256,128]{2,1,0:T(8,128)S(1)} %apply.1.refs_0_, f32[4,256,128]{2,1,0:T(8,128)S(1)} %get-tuple-element.46.diag_ref.refs_1_, ...), custom_call_target="tpu_custom_call", output_to_operand_aliasing={{0}: (0, {})} | custom-call | tf_op jit(solution)/shard_map/smooth/pallas_call | solution.py:601
  23.1 0.0 collective-permute-start.8
  23.1 0.7 %sums.1 = (f32[4,256,128]{2,1,0:T(8,128)S(1)}, f32[4,8,128]{2,1,0:T(8,128)S(1)}) custom-call(f32[4,272,128]{2,1,0:T(8,128)S(1)} %get-tuple-element.55.m_ref.refs_1_.refs_5_, f32[4,272,128]{2,1,0:T(8,128)S(1)} %get-tuple-element.45.u_ref.refs_3_, f32[4,256,128]{2,1,0:T(8,128)S(1)} %get-tuple-element.56.r_ref.refs_2_, ...), custom_call_target="tpu_custom_call" | custom-call | tf_op jit(solution)/shard_map/sums/pallas_call | solution.py:601
  23.8 0.6 %collective-permute-done.8.refs_5_ = f32[256,128]{1,0:T(8,128)S(1)} collective-permute-done((f32[256,128]{1,0:T(8,128)S(1)}, f32[256,128]{1,0:T(8,128)S(1)}, u32[]{:S(2)}, u32[]{:S(2)}) %collective-permute-start.8) | collective-permute-done | bytes 131104 | tf_op jit(solution)/shard_map/ppermute | solution.py:622
  24.5 0.1 finish.1
  24.6 13.0 %all_to_all.5.refs_0_ = f32[16,24,128]{2,1,0:T(8,128)S(1)} all-to-all(f32[16,24,128]{2,1,0:T(8,128)S(1)} %get-tuple-element.62), channel_id=1, replica_groups=mesh['groups'=2,'gx'=4,'gy'=2,'gz'=2] {'gx','gy','gz'}, dimensions={0} | all-to-all | bytes 393216 | tf_op jit(solution)/shard_map/all_to_all | solution.py:693
  37.5 1.5 %update.1 = (f32[4,256,128]{2,1,0:T(8,128)}, f32[4,256,128]{2,1,0:T(8,128)}) custom-call(f32[16,24,128]{2,1,0:T(8,128)S(1)} %all_to_all.5.refs_0_, f32[4,272,128]{2,1,0:T(8,128)S(1)} %get-tuple-element.33.x_ref.refs_0_.refs_1_, f32[4,256,128]{2,1,0:T(8,128)S(1)} %get-tuple-element.56.r_ref.refs_2_, f32[4,272,128]{2,1,0:T(8,128)S(1)} %get-tuple-element.45.u_ref.refs_3_, ...), custom_call_target="tpu_custom_call" | custom-call | tf_op jit(solution)/shard_map/update/pallas_call | solution.py:601
Async XLA Ops:
  2.6 7.5 %collective-permute-start.3 = (f32[2,256,128]{2,1,0:T(8,128)S(1)}, f32[2,256,128]{2,1,0:T(8,128)S(1)}, u32[]{:S(2)}, u32[]{:S(2)}) collective-permute-start(f32[2,256,128]{2,1,0:T(8,128)S(1)} %get-tuple-element.44), channel_id=1, source_target_pairs={{0,1},{1,0},{2,3},{3,2},{4,5},{5,4},{6,7},{7,6},{8,9},{9,8},{10,11... | collective-permute-start | bytes 786440 | tf_op jit(solution)/shard_map/ppermute | solution.py:622
  3.1 7.0 %collective-permute-start = (f32[2,8,128]{2,1,0:T(8,128)S(1)}, f32[2,8,128]{2,1,0:T(8,128)S(1)}, u32[]{:S(2)}, u32[]{:S(2)}) collective-permute-start(f32[2,8,128]{2,1,0:T(8,128)S(1)} %get-tuple-element.41), channel_id=1, source_target_pairs={{0,4},{4,0},{8,12},{12,8},{1,5},{5,1},{9,13},{13,9},{2,6},{6,2},{1... | collective-permute-start | bytes 24584 | tf_op jit(solution)/shard_map/ppermute | solution.py:622
  5.8 4.3 %collective-permute-start.1 = (f32[2,8,128]{2,1,0:T(8,128)S(1)}, f32[2,8,128]{2,1,0:T(8,128)S(1)}, u32[]{:S(2)}, u32[]{:S(2)}) collective-permute-start(f32[2,8,128]{2,1,0:T(8,128)S(1)} %get-tuple-element.42), channel_id=1, source_target_pairs={{4,8},{8,4},{5,9},{9,5},{6,10},{10,6},{7,11},{11,7},{20,24},{24,20... | collective-permute-start | bytes 24584 | tf_op jit(solution)/shard_map/ppermute | solution.py:622
  6.4 3.7 %collective-permute-start.2 = (f32[2,4,128]{2,1,0:T(4,128)S(1)}, f32[2,4,128]{2,1,0:T(4,128)S(1)}, u32[]{:S(2)}, u32[]{:S(2)}) collective-permute-start(f32[2,4,128]{2,1,0:T(4,128)S(1)} %get-tuple-element.43), channel_id=1, source_target_pairs={{0,2},{2,0},{1,3},{3,1},{4,6},{6,4},{5,7},{7,5},{8,10},{10,8},{9,1... | collective-permute-start | bytes 12296 | tf_op jit(solution)/shard_map/ppermute | solution.py:622
  12.4 8.7 %collective-permute-start.7 = (f32[256,128]{1,0:T(8,128)S(1)}, f32[256,128]{1,0:T(8,128)S(1)}, u32[]{:S(2)}, u32[]{:S(2)}) collective-permute-start(f32[256,128]{1,0:T(8,128)S(1)} %get-tuple-element.54), channel_id=1, source_target_pairs={{0,1},{1,0},{2,3},{3,2},{4,5},{5,4},{6,7},{7,6},{8,9},{9,8},{10,11... | collective-permute-start | bytes 393224 | tf_op jit(solution)/shard_map/ppermute | solution.py:622
  12.4 8.7 %collective-permute-start.4 = (f32[8,128]{1,0:T(8,128)S(1)}, f32[8,128]{1,0:T(8,128)S(1)}, u32[]{:S(2)}, u32[]{:S(2)}) collective-permute-start(f32[8,128]{1,0:T(8,128)S(1)} %get-tuple-element.51), channel_id=1, source_target_pairs={{0,4},{4,0},{8,12},{12,8},{1,5},{5,1},{9,13},{13,9},{2,6},{6,2},{1... | collective-permute-start | bytes 12296 | tf_op jit(solution)/shard_map/ppermute | solution.py:622
  16.8 4.3 %collective-permute-start.5 = (f32[8,128]{1,0:T(8,128)S(1)}, f32[8,128]{1,0:T(8,128)S(1)}, u32[]{:S(2)}, u32[]{:S(2)}) collective-permute-start(f32[8,128]{1,0:T(8,128)S(1)} %get-tuple-element.52), channel_id=1, source_target_pairs={{4,8},{8,4},{5,9},{9,5},{6,10},{10,6},{7,11},{11,7},{20,24},{24,20... | collective-permute-start | bytes 12296 | tf_op jit(solution)/shard_map/ppermute | solution.py:622
  17.4 3.7 %collective-permute-start.6 = (f32[4,128]{1,0:T(4,128)S(1)}, f32[4,128]{1,0:T(4,128)S(1)}, u32[]{:S(2)}, u32[]{:S(2)}) collective-permute-start(f32[4,128]{1,0:T(4,128)S(1)} %get-tuple-element.53), channel_id=1, source_target_pairs={{0,2},{2,0},{1,3},{3,1},{4,6},{6,4},{5,7},{7,5},{8,10},{10,8},{9,1... | collective-permute-start | bytes 6152 | tf_op jit(solution)/shard_map/ppermute | solution.py:622
  23.1 1.4 %collective-permute-start.8 = (f32[256,128]{1,0:T(8,128)S(1)}, f32[256,128]{1,0:T(8,128)S(1)}, u32[]{:S(2)}, u32[]{:S(2)}) collective-permute-start(f32[256,128]{1,0:T(8,128)S(1)} %get-tuple-element.61), channel_id=1, source_target_pairs={{0,1},{1,0},{2,3},{3,2},{4,5},{5,4},{6,7},{7,6},{8,9},{9,8},{10,11... | collective-permute-start | bytes 393224 | tf_op jit(solution)/shard_map/ppermute | solution.py:622

commit v8 on v7

--- a/solution.py
+++ b/solution.py
@@ -163,7 +163,7 @@
     per = y // 8
     fields = (x_ref, k_ref)
     copies = [
-        start_all([source.at[i] for i in range(z)], [ref.at[i, pl.ds(8, y), :] for i in range(z)], sems.at[n])
+        start_all([source], [ref.at[:, pl.ds(8, y), :]], sems.at[n])
         for n, (source, ref) in enumerate(zip((x_in, k_in), fields))
     ]
     for slot, ref in enumerate(fields):
@@ -171,8 +171,8 @@
         tier, row, vreg = padded_access(ref)
 
         def load(i):
-            if i % per == 0:
-                copies[slot][i // per].wait()
+            if i == 0:
+                copies[slot][0].wait()
             return vreg(i)
 
         columns = pack_columns(load, z * per)
@@ -181,13 +181,13 @@
         fill_sends(tier, row, sends, slot, columns, z, y)
 
 
-def inner_kernel(tall, x_ref, k_ref, c_in, cat_in, sel_in, band_in, flow_in, lev_in, *refs):
-    r_ref, diag_ref, cz_ref, cs_ref, ce_ref, mask_ref, c_ref, cat_ref, *tables, sems = refs
+def inner_kernel(tall, x_ref, k_ref, c_ref, cat_ref, sel_in, band_in, flow_in, lev_in, *refs):
+    r_ref, diag_ref, cz_ref, cs_ref, ce_ref, mask_ref, *tables, sems = refs
     sel_ref, band_ref, flow_ref, lev_ref = tables
     z, y, _ = c_ref.shape
     copies = start_all(
-        (c_in, cat_in, sel_in, band_in, flow_in, lev_in),
-        (c_ref, cat_ref, *tables),
+        (sel_in, band_in, flow_in, lev_in),
+        tables,
         sems,
     )
     lane = lanes((tall, 128))
@@ -647,15 +647,13 @@
         [field, kappa, caloric_storage, dissipation_catalog, selector, width, microflow_flag, levels],
         "inner",
         [
-            full,
-            shape(*dissipation_catalog.shape),
             table(selector),
             table(width),
             table(microflow_flag),
             table(levels),
-            pltpu.SemaphoreType.DMA((6,)),
+            pltpu.SemaphoreType.DMA((4,)),
         ],
-        outer=(2, 3, 4, 5, 6, 7),
+        outer=(4, 5, 6, 7),
     )
     outs = call(
         functools.partial(border_kernel, rounds, tall),

time: 39.3 us -> 39.1 us (level)
  Pallas kernels: 11 us -> 8.91 us
  blocking collectives: 13 us -> 14.3 us
  starting transfers between devices: 11.6 us -> 12.2 us
    pallas_call x8, Pallas kernels: 11 us -> 8.91 us  [call(): pl.pallas_call(kernel, out_shape=outs, in_specs=specs, out_specs=out_spec...]
    all_to_all x1, blocking collectives: 13 us -> 14.3 us  [body(): every = lax.all_to_all(parts, GRID_AXES, 0, 0, tiled=True)]
    ppermute x9, starting transfers between devices: 11.6 us -> 12.2 us  [swap(): got.append(lax.ppermute(faces.pop(0), axis, swap_pairs(axis, start)))]
  transfers between devices with their start and end apart: 9 -> 9, of which waited for: 3 -> 3; matrix products, arithmetic and copies ran while one was open for 0% -> 0% of each run, Pallas kernels for 8% -> 7%
where the time goes in v8:
time: 39.1 us; the launch traced here: 38.8 us
  blocking collectives  14.3 us (37%)
  starting transfers between devices  12.2 us (31%)
  Pallas kernels  8.91 us (23%)
  waiting for transfers between devices  2.72 us (7%)
  between operations  0.73 us (2%)
    all_to_all x1, blocking collectives, body(): every = lax.all_to_all(parts, GRID_AXES, 0, 0, tiled=True)  14.3 us
    ppermute x9, starting transfers between devices, swap(): got.append(lax.ppermute(faces.pop(0), axis, swap_pairs(axis, start)))  12.2 us
    pallas_call x8, Pallas kernels, call(): pl.pallas_call(kernel, out_shape=outs, in_specs=specs, out_specs=out_spec...  8.91 us
    ppermute x9, waiting for transfers between devices, swap(): got.append(lax.ppermute(faces.pop(0), axis, swap_pairs(axis, start)))  2.72 us
  transfers between devices with their start and end apart: 9, of which 3 were waited for; matrix products, arithmetic and copies ran while one was open for 0% of the time, Pallas kernels for 7%

profile of v8, /device:TPU:0, one launch (start us, length us, event | category | flops | bytes accessed | tf_op | source)
XLA Modules:
  0.0 38.8 jit_solution(17362745080794437241)
XLA Ops:
  0.6 0.0 copy-start.1
  0.6 0.0 copy-start
  0.7 1.8 %faces.1 = (f32[4,272,128]{2,1,0:T(8,128)S(1)}, f32[4,272,128]{2,1,0:T(8,128)S(1)}, f32[2,8,128]{2,1,0:T(8,128)S(1)}, f32[2,8,128]{2,1,0:T(8,128)S(1)}, f32[2,4,...) custom-call(f32[4,256,128]{2,1,0:T(8,128)} %x_in.1, f32[4,256,128]{2,1,0:T(8,128)} %k_in.1), custom_call_target="tpu_custom_call" | custom-call | tf_op jit(solution)/shard_map/faces/pallas_call | solution.py:601
  2.4 0.6 %collective-permute-start.3 = (f32[2,256,128]{2,1,0:T(8,128)S(1)}, f32[2,256,128]{2,1,0:T(8,128)S(1)}, u32[]{:S(2)}, u32[]{:S(2)}) collective-permute-start(f32[2,256,128]{2,1,0:T(8,128)S(1)} %get-tuple-element.44), channel_id=1, source_target_pairs={{0,1},{1,0},{2,3},{3,2},{4,5},{5,4},{6,7},{7,6},{8,9},{9,8},{10,11... | collective-permute-start | bytes 786440 | tf_op jit(solution)/shard_map/ppermute | solution.py:622
  3.0 2.6 %collective-permute-start = (f32[2,8,128]{2,1,0:T(8,128)S(1)}, f32[2,8,128]{2,1,0:T(8,128)S(1)}, u32[]{:S(2)}, u32[]{:S(2)}) collective-permute-start(f32[2,8,128]{2,1,0:T(8,128)S(1)} %get-tuple-element.41), channel_id=1, source_target_pairs={{0,4},{4,0},{8,12},{12,8},{1,5},{5,1},{9,13},{13,9},{2,6},{6,2},{1... | collective-permute-start | bytes 24584 | tf_op jit(solution)/shard_map/ppermute | solution.py:622
  5.6 0.6 %collective-permute-start.1 = (f32[2,8,128]{2,1,0:T(8,128)S(1)}, f32[2,8,128]{2,1,0:T(8,128)S(1)}, u32[]{:S(2)}, u32[]{:S(2)}) collective-permute-start(f32[2,8,128]{2,1,0:T(8,128)S(1)} %get-tuple-element.42), channel_id=1, source_target_pairs={{4,8},{8,4},{5,9},{9,5},{6,10},{10,6},{7,11},{11,7},{20,24},{24,20... | collective-permute-start | bytes 24584 | tf_op jit(solution)/shard_map/ppermute | solution.py:622
  6.3 1.6 %collective-permute-start.2 = (f32[2,4,128]{2,1,0:T(4,128)S(1)}, f32[2,4,128]{2,1,0:T(4,128)S(1)}, u32[]{:S(2)}, u32[]{:S(2)}) collective-permute-start(f32[2,4,128]{2,1,0:T(4,128)S(1)} %get-tuple-element.43), channel_id=1, source_target_pairs={{0,2},{2,0},{1,3},{3,1},{4,6},{6,4},{5,7},{7,5},{8,10},{10,8},{9,1... | collective-permute-start | bytes 12296 | tf_op jit(solution)/shard_map/ppermute | solution.py:622
  7.8 0.0 copy-done.1
  7.8 0.0 copy-done
  7.8 1.6 %inner.1 = (f32[4,256,128]{2,1,0:T(8,128)S(1)}, f32[4,256,128]{2,1,0:T(8,128)S(1)}, f32[3,256,128]{2,1,0:T(8,128)S(1)}, f32[4,264,128]{2,1,0:T(8,128)S(1)}, f32[...) custom-call(f32[4,272,128]{2,1,0:T(8,128)S(1)} %get-tuple-element.33.x_ref.refs_0_.refs_1_, ...), custom_call_target="tpu_custom_call" | custom-call | tf_op jit(solution)/shard_map/inner/pallas_call | solution.py:601
  9.4 0.5 %collective-permute-done.2.refs_10_ = f32[2,4,128]{2,1,0:T(4,128)S(1)} collective-permute-done((f32[2,4,128]{2,1,0:T(4,128)S(1)}, f32[2,4,128]{2,1,0:T(4,128)S(1)}, u32[]{:S(2)}, u32[]{:S(2)}) %collective-permute-start.2) | collective-permute-done | bytes 4128 | tf_op jit(solution)/shard_map/ppermute | solution.py:622
  9.9 0.0 collective-permute-done.refs_8_
  10.0 0.0 collective-permute-done.1.refs_9_
  10.0 0.0 collective-permute-done.3.refs_11_
  10.0 1.5 %border.1 = (f32[4,256,128]{2,1,0:T(8,128)S(1)}, f32[4,256,128]{2,1,0:T(8,128)S(1)}, f32[4,272,128]{2,1,0:T(8,128)S(1)}, f32[2,8,128]{2,1,0:T(8,128)S(1)}, f32[1...) custom-call(f32[4,272,128]{2,1,0:T(8,128)S(1)} %get-tuple-element.33, ...), custom_call_target="tpu_custom_call", output_to_operand_aliasing={{0}: (3, {}), {1}: (4, {})} | custom-call | tf_op jit(solution)/shard_map/border/pallas_call | solution.py:601
  11.5 0.0 collective-permute-start.7
  11.5 4.5 %collective-permute-start.4 = (f32[8,128]{1,0:T(8,128)S(1)}, f32[8,128]{1,0:T(8,128)S(1)}, u32[]{:S(2)}, u32[]{:S(2)}) collective-permute-start(f32[8,128]{1,0:T(8,128)S(1)} %get-tuple-element.51), channel_id=1, source_target_pairs={{0,4},{4,0},{8,12},{12,8},{1,5},{5,1},{9,13},{13,9},{2,6},{6,2},{1... | collective-permute-start | bytes 12296 | tf_op jit(solution)/shard_map/ppermute | solution.py:622
  16.0 0.6 %collective-permute-start.5 = (f32[8,128]{1,0:T(8,128)S(1)}, f32[8,128]{1,0:T(8,128)S(1)}, u32[]{:S(2)}, u32[]{:S(2)}) collective-permute-start(f32[8,128]{1,0:T(8,128)S(1)} %get-tuple-element.52), channel_id=1, source_target_pairs={{4,8},{8,4},{5,9},{9,5},{6,10},{10,6},{7,11},{11,7},{20,24},{24,20... | collective-permute-start | bytes 12296 | tf_op jit(solution)/shard_map/ppermute | solution.py:622
  16.7 1.6 %collective-permute-start.6 = (f32[4,128]{1,0:T(4,128)S(1)}, f32[4,128]{1,0:T(4,128)S(1)}, u32[]{:S(2)}, u32[]{:S(2)}) collective-permute-start(f32[4,128]{1,0:T(4,128)S(1)} %get-tuple-element.53), channel_id=1, source_target_pairs={{0,2},{2,0},{1,3},{3,1},{4,6},{6,4},{5,7},{7,5},{8,10},{10,8},{9,1... | collective-permute-start | bytes 6152 | tf_op jit(solution)/shard_map/ppermute | solution.py:622
  18.2 0.5 %apply.1.refs_0_ = f32[4,256,128]{2,1,0:T(8,128)S(1)} custom-call(f32[4,272,128]{2,1,0:T(8,128)S(1)} %get-tuple-element.45.u_ref.refs_3_, f32[4,256,128]{2,1,0:T(8,128)S(1)} %get-tuple-element.46.diag_ref.refs_1_, f32[3,256,128]{2,1,0:T(8,128)S(1)} %get-tuple-element.47.cz_ref, f32[4,264,128]{2,1,0:T(8,128)S(1)} %get-tuple-element.38.refs_5_.cs_ref.refs_2_, ...), custom_call_target="tpu_custom_call" | custom-call | tf_op jit(solution)/shard_map/apply/pallas_call | solution.py:601
  18.8 1.5 %collective-permute-done.6.refs_10_ = f32[4,128]{1,0:T(4,128)S(1)} collective-permute-done((f32[4,128]{1,0:T(4,128)S(1)}, f32[4,128]{1,0:T(4,128)S(1)}, u32[]{:S(2)}, u32[]{:S(2)}) %collective-permute-start.6) | collective-permute-done | bytes 2080 | tf_op jit(solution)/shard_map/ppermute | solution.py:622
  20.3 0.0 collective-permute-done.4.refs_8_
  20.3 0.0 collective-permute-done.5.refs_9_
  20.3 0.0 collective-permute-done.7.refs_11_
  20.3 1.2 %smooth.1 = (f32[4,256,128]{2,1,0:T(8,128)S(1)}, f32[4,272,128]{2,1,0:T(8,128)S(1)}, f32[24,128]{1,0:T(8,128)S(1)}, f32[256,128]{1,0:T(8,128)S(1)}) custom-call(f32[4,256,128]{2,1,0:T(8,128)S(1)} %apply.1.refs_0_, f32[4,256,128]{2,1,0:T(8,128)S(1)} %get-tuple-element.46.diag_ref.refs_1_, ...), custom_call_target="tpu_custom_call", output_to_operand_aliasing={{0}: (0, {})} | custom-call | tf_op jit(solution)/shard_map/smooth/pallas_call | solution.py:601
  21.6 0.0 collective-permute-start.8
  21.6 0.7 %sums.1 = (f32[4,256,128]{2,1,0:T(8,128)S(1)}, f32[4,8,128]{2,1,0:T(8,128)S(1)}) custom-call(f32[4,272,128]{2,1,0:T(8,128)S(1)} %get-tuple-element.55.m_ref.refs_1_.refs_5_, f32[4,272,128]{2,1,0:T(8,128)S(1)} %get-tuple-element.45.u_ref.refs_3_, f32[4,256,128]{2,1,0:T(8,128)S(1)} %get-tuple-element.56.r_ref.refs_2_, ...), custom_call_target="tpu_custom_call" | custom-call | tf_op jit(solution)/shard_map/sums/pallas_call | solution.py:601
  22.3 0.6 %collective-permute-done.8.refs_5_ = f32[256,128]{1,0:T(8,128)S(1)} collective-permute-done((f32[256,128]{1,0:T(8,128)S(1)}, f32[256,128]{1,0:T(8,128)S(1)}, u32[]{:S(2)}, u32[]{:S(2)}) %collective-permute-start.8) | collective-permute-done | bytes 131104 | tf_op jit(solution)/shard_map/ppermute | solution.py:622
  22.9 0.1 finish.1
  23.0 14.3 %all_to_all.5.refs_0_ = f32[16,24,128]{2,1,0:T(8,128)S(1)} all-to-all(f32[16,24,128]{2,1,0:T(8,128)S(1)} %get-tuple-element.62), channel_id=1, replica_groups=mesh['groups'=2,'gx'=4,'gy'=2,'gz'=2] {'gx','gy','gz'}, dimensions={0} | all-to-all | bytes 393216 | tf_op jit(solution)/shard_map/all_to_all | solution.py:691
  37.3 1.5 %update.1 = (f32[4,256,128]{2,1,0:T(8,128)}, f32[4,256,128]{2,1,0:T(8,128)}) custom-call(f32[16,24,128]{2,1,0:T(8,128)S(1)} %all_to_all.5.refs_0_, f32[4,272,128]{2,1,0:T(8,128)S(1)} %get-tuple-element.33.x_ref.refs_0_.refs_1_, f32[4,256,128]{2,1,0:T(8,128)S(1)} %get-tuple-element.56.r_ref.refs_2_, f32[4,272,128]{2,1,0:T(8,128)S(1)} %get-tuple-element.45.u_ref.refs_3_, ...), custom_call_target="tpu_custom_call" | custom-call | tf_op jit(solution)/shard_map/update/pallas_call | solution.py:601
Async XLA Ops:
  0.6 7.2 %copy-start.1 = (f32[8,64,128]{2,1,0:T(8,128)S(1)}, f32[8,64,128]{2,1,0:T(8,128)}, u32[]{:S(2)}) copy-start(f32[8,64,128]{2,1,0:T(8,128)} %cat_ref.1) | copy-start | bytes 786436
  0.6 7.2 %copy-start = (f32[4,256,128]{2,1,0:T(8,128)S(1)}, f32[4,256,128]{2,1,0:T(8,128)}, u32[]{:S(2)}) copy-start(f32[4,256,128]{2,1,0:T(8,128)} %c_ref.1) | copy-start | bytes 1572868
  2.4 7.5 %collective-permute-start.3 = (f32[2,256,128]{2,1,0:T(8,128)S(1)}, f32[2,256,128]{2,1,0:T(8,128)S(1)}, u32[]{:S(2)}, u32[]{:S(2)}) collective-permute-start(f32[2,256,128]{2,1,0:T(8,128)S(1)} %get-tuple-element.44), channel_id=1, source_target_pairs={{0,1},{1,0},{2,3},{3,2},{4,5},{5,4},{6,7},{7,6},{8,9},{9,8},{10,11... | collective-permute-start | bytes 786440 | tf_op jit(solution)/shard_map/ppermute | solution.py:622
  3.0 7.0 %collective-permute-start = (f32[2,8,128]{2,1,0:T(8,128)S(1)}, f32[2,8,128]{2,1,0:T(8,128)S(1)}, u32[]{:S(2)}, u32[]{:S(2)}) collective-permute-start(f32[2,8,128]{2,1,0:T(8,128)S(1)} %get-tuple-element.41), channel_id=1, source_target_pairs={{0,4},{4,0},{8,12},{12,8},{1,5},{5,1},{9,13},{13,9},{2,6},{6,2},{1... | collective-permute-start | bytes 24584 | tf_op jit(solution)/shard_map/ppermute | solution.py:622
  5.6 4.3 %collective-permute-start.1 = (f32[2,8,128]{2,1,0:T(8,128)S(1)}, f32[2,8,128]{2,1,0:T(8,128)S(1)}, u32[]{:S(2)}, u32[]{:S(2)}) collective-permute-start(f32[2,8,128]{2,1,0:T(8,128)S(1)} %get-tuple-element.42), channel_id=1, source_target_pairs={{4,8},{8,4},{5,9},{9,5},{6,10},{10,6},{7,11},{11,7},{20,24},{24,20... | collective-permute-start | bytes 24584 | tf_op jit(solution)/shard_map/ppermute | solution.py:622
  6.3 3.7 %collective-permute-start.2 = (f32[2,4,128]{2,1,0:T(4,128)S(1)}, f32[2,4,128]{2,1,0:T(4,128)S(1)}, u32[]{:S(2)}, u32[]{:S(2)}) collective-permute-start(f32[2,4,128]{2,1,0:T(4,128)S(1)} %get-tuple-element.43), channel_id=1, source_target_pairs={{0,2},{2,0},{1,3},{3,1},{4,6},{6,4},{5,7},{7,5},{8,10},{10,8},{9,1... | collective-permute-start | bytes 12296 | tf_op jit(solution)/shard_map/ppermute | solution.py:622
  11.5 8.9 %collective-permute-start.7 = (f32[256,128]{1,0:T(8,128)S(1)}, f32[256,128]{1,0:T(8,128)S(1)}, u32[]{:S(2)}, u32[]{:S(2)}) collective-permute-start(f32[256,128]{1,0:T(8,128)S(1)} %get-tuple-element.54), channel_id=1, source_target_pairs={{0,1},{1,0},{2,3},{3,2},{4,5},{5,4},{6,7},{7,6},{8,9},{9,8},{10,11... | collective-permute-start | bytes 393224 | tf_op jit(solution)/shard_map/ppermute | solution.py:622
  11.5 8.8 %collective-permute-start.4 = (f32[8,128]{1,0:T(8,128)S(1)}, f32[8,128]{1,0:T(8,128)S(1)}, u32[]{:S(2)}, u32[]{:S(2)}) collective-permute-start(f32[8,128]{1,0:T(8,128)S(1)} %get-tuple-element.51), channel_id=1, source_target_pairs={{0,4},{4,0},{8,12},{12,8},{1,5},{5,1},{9,13},{13,9},{2,6},{6,2},{1... | collective-permute-start | bytes 12296 | tf_op jit(solution)/shard_map/ppermute | solution.py:622
  16.0 4.3 %collective-permute-start.5 = (f32[8,128]{1,0:T(8,128)S(1)}, f32[8,128]{1,0:T(8,128)S(1)}, u32[]{:S(2)}, u32[]{:S(2)}) collective-permute-start(f32[8,128]{1,0:T(8,128)S(1)} %get-tuple-element.52), channel_id=1, source_target_pairs={{4,8},{8,4},{5,9},{9,5},{6,10},{10,6},{7,11},{11,7},{20,24},{24,20... | collective-permute-start | bytes 12296 | tf_op jit(solution)/shard_map/ppermute | solution.py:622
  16.7 3.7 %collective-permute-start.6 = (f32[4,128]{1,0:T(4,128)S(1)}, f32[4,128]{1,0:T(4,128)S(1)}, u32[]{:S(2)}, u32[]{:S(2)}) collective-permute-start(f32[4,128]{1,0:T(4,128)S(1)} %get-tuple-element.53), channel_id=1, source_target_pairs={{0,2},{2,0},{1,3},{3,1},{4,6},{6,4},{5,7},{7,5},{8,10},{10,8},{9,1... | collective-permute-start | bytes 6152 | tf_op jit(solution)/shard_map/ppermute | solution.py:622
  21.6 1.4 %collective-permute-start.8 = (f32[256,128]{1,0:T(8,128)S(1)}, f32[256,128]{1,0:T(8,128)S(1)}, u32[]{:S(2)}, u32[]{:S(2)}) collective-permute-start(f32[256,128]{1,0:T(8,128)S(1)} %get-tuple-element.61), channel_id=1, source_target_pairs={{0,1},{1,0},{2,3},{3,2},{4,5},{5,4},{6,7},{7,6},{8,9},{9,8},{10,11... | collective-permute-start | bytes 393224 | tf_op jit(solution)/shard_map/ppermute | solution.py:622
